TPU v7x, 32 devices: a whole 2x2x4 slice. The times are simulated.
32 devices in a mesh: fsdp: 8 (over y, x, core), ep: 4 (over z).
Axes of the slice: x: 2, y: 2, z: 4, core: 2. Of those that a mesh axis runs over, the one named last changes fastest.
Arguments:
- tokens: bfloat16 [8192, 2048], P(('fsdp', 'ep')), may hold values from -6 to 6
- out_grad: bfloat16 [8192, 2048], P(('fsdp', 'ep')), may hold values from -4 to 4
- expert_ids: int32 [8192, 8], P(('fsdp', 'ep')), may hold values from 0 to 127, as said below
- gate_probs: bfloat16 [8192, 8], P(('fsdp', 'ep')), may hold values from 0.19921875 to 1
- w_gate: bfloat16 [2048, 4, 768], P('fsdp', 'ep'), may hold values from -0.125 to 0.125
- w_up: bfloat16 [2048, 4, 768], P('fsdp', 'ep'), may hold values from -0.125 to 0.125
- w_down: bfloat16 [2048, 4, 768], P('fsdp', 'ep'), may hold values from -0.21875 to 0.21875
Outputs:
- in_grad: bfloat16 [8192, 2048], P(('fsdp', 'ep'))
- gate_grad: bfloat16 [8192, 8], P(('fsdp', 'ep'))
- grad_gate: bfloat16 [2048, 4, 768], P('fsdp', 'ep')
- grad_up: bfloat16 [2048, 4, 768], P('fsdp', 'ep')
- grad_down: bfloat16 [2048, 4, 768], P('fsdp', 'ep')
Inputs may be any that keep to these rules, and one draw needn't show every extreme that they name: `expert_ids`: each token names 8 different experts. Among the 256 tokens of one device each expert below 4 is named by at most 32 tokens; in each group of devices that share an index of fsdp, one expert below 4 is named by exactly 32 tokens of every device of the group.
All inputs are finite; a program needn't handle non-finite values.
Results may differ from a plain program's by a relative error of at most 0.014.
Values may be sent and summed in bfloat16 or wider, within the bound.
No kernel may reach another device: no remote copies, remote signals or barrier semaphores. Data moves between devices by JAX's collectives and lax.ppermute only.
A program may use at most 128 MiB of HBM per device.

v0:
```python
import jax
import jax.numpy as jnp
from jax import lax
from jax.sharding import PartitionSpec as P

MOST = 32


def expert_math(grad_rows, gate_rows, gate_pre, up_pre, back_proj):
    sigmoid_gate = jax.nn.sigmoid(gate_pre)
    silu_gate = gate_pre * sigmoid_gate
    activated = (silu_gate * up_pre).astype(jnp.bfloat16)
    pick_grad = jnp.sum(activated.astype(jnp.float32) * back_proj, axis=-1).astype(jnp.bfloat16)
    weight_col = gate_rows.astype(jnp.float32)[:, None]
    scaled_back = weight_col * back_proj
    gate_delta = (
        scaled_back * up_pre * sigmoid_gate * (1.0 + gate_pre * (1.0 - sigmoid_gate))
    ).astype(jnp.bfloat16)
    up_delta = (scaled_back * silu_gate).astype(jnp.bfloat16)
    scaled_grad = (weight_col * grad_rows.astype(jnp.float32)).astype(jnp.bfloat16)
    return (activated, pick_grad, gate_delta, up_delta, scaled_grad)


def leading_product(left, right):
    return lax.dot_general(
        left, right, (((0,), (0,)), ((), ())), preferred_element_type=jnp.float32
    )


def trailing_product(left, right):
    return lax.dot_general(
        left, right, (((1,), (1,)), ((), ())), preferred_element_type=jnp.float32
    )


def per_device(tokens, out_grad, expert_ids, gate_probs, w_gate, w_up, w_down):
    tok_count, model_width = tokens.shape
    hidden = w_gate.shape[2]
    experts_here = lax.axis_size("ep")
    capacity = MOST
    owners = lax.iota(jnp.int32, experts_here)
    matches = expert_ids[:, :, None] == owners[None, None, :]
    chosen = jnp.any(matches, axis=1)
    gate_pick = jnp.sum(jnp.where(matches, gate_probs[:, :, None].astype(jnp.float32), 0.0), axis=1)
    chosen_int = chosen.astype(jnp.int32)
    slot_rows = (jnp.cumsum(chosen_int, axis=0) - chosen_int).T
    placed = chosen.T[:, None, :] & (
        slot_rows[:, None, :] == lax.iota(jnp.int32, capacity)[None, :, None]
    )
    token_range = lax.iota(jnp.int32, tok_count)
    token_index = jnp.sum(jnp.where(placed, token_range[None, None, :], 0), axis=2)
    filled = jnp.any(placed, axis=2)
    send_tokens = jnp.where(filled[:, :, None], tokens[token_index], jnp.zeros((), jnp.bfloat16))
    send_grads = jnp.where(filled[:, :, None], out_grad[token_index], jnp.zeros((), jnp.bfloat16))
    send_gates = jnp.where(
        filled, jnp.take_along_axis(gate_pick.T, token_index, axis=1), 0.0
    ).astype(jnp.bfloat16)
    gathered = (
        lax.all_gather(w_gate, "fsdp", axis=0, tiled=True),
        lax.all_gather(w_up, "fsdp", axis=0, tiled=True),
        lax.all_gather(w_down, "fsdp", axis=0, tiled=True),
    )
    weight_in = jnp.concatenate([gathered[0][:, 0, :], gathered[1][:, 0, :]], axis=1)
    weight_out = gathered[2][:, 0, :]
    recv_tokens = lax.all_to_all(send_tokens, "ep", split_axis=0, concat_axis=0, tiled=True)
    recv_grads = lax.all_to_all(send_grads, "ep", split_axis=0, concat_axis=0, tiled=True)
    recv_gates = lax.all_to_all(send_gates, "ep", split_axis=0, concat_axis=0, tiled=True)
    slots = recv_tokens.shape[1]
    flat_tokens = recv_tokens.reshape(-1, model_width)
    flat_grads = recv_grads.reshape(-1, model_width)
    both_pre = jnp.dot(flat_tokens, weight_in, preferred_element_type=jnp.float32)
    back_proj = jnp.dot(flat_grads, weight_out, preferred_element_type=jnp.float32)
    activated, pick_grad, gate_delta, up_delta, scaled_grad = expert_math(
        flat_grads, recv_gates.reshape(-1), both_pre[:, :hidden], both_pre[:, hidden:], back_proj
    )
    deltas = jnp.concatenate([gate_delta, up_delta], axis=1)
    row_grads = trailing_product(deltas, weight_in).astype(jnp.bfloat16)
    back_rows, back_picks, recv_tokens, deltas, activated, scaled_grad = (
        lax.all_to_all(
            row_grads.reshape(experts_here, slots, model_width),
            "ep",
            split_axis=0,
            concat_axis=0,
            tiled=True,
        ),
        lax.all_to_all(
            pick_grad.reshape(experts_here, slots), "ep", split_axis=0, concat_axis=0, tiled=True
        ),
        recv_tokens,
        deltas.reshape(experts_here, slots, 2 * hidden),
        activated.reshape(experts_here, slots, hidden),
        scaled_grad.reshape(experts_here, slots, model_width),
    )
    flat_back = back_rows.reshape(-1, model_width).astype(jnp.float32)
    in_grad = jax.ops.segment_sum(
        jnp.where(filled.reshape(-1)[:, None], flat_back, 0.0),
        token_index.reshape(-1),
        num_segments=tok_count,
    ).astype(jnp.bfloat16)
    safe_slot = jnp.minimum(slot_rows, capacity - 1)
    pick_values = jnp.take_along_axis(back_picks, safe_slot, axis=1).astype(jnp.float32)
    gate_grad = jnp.sum(jnp.where(matches, pick_values.T[:, None, :], 0.0), axis=2).astype(
        jnp.bfloat16
    )
    rows_x = recv_tokens.reshape(-1, model_width)
    rows_delta = deltas.reshape(-1, 2 * hidden)
    rows_act = activated.reshape(-1, hidden)
    rows_scaled = scaled_grad.reshape(-1, model_width)
    term = jnp.concatenate(
        [leading_product(rows_x, rows_delta), leading_product(rows_scaled, rows_act)], axis=1
    )
    summed = lax.psum_scatter(
        term.astype(jnp.bfloat16), "fsdp", scatter_dimension=0, tiled=True
    ).astype(jnp.float32)
    grad_gate = summed[:, None, :hidden].astype(jnp.bfloat16)
    grad_up = summed[:, None, hidden : 2 * hidden].astype(jnp.bfloat16)
    grad_down = summed[:, None, 2 * hidden :].astype(jnp.bfloat16)
    return (in_grad, gate_grad, grad_gate, grad_up, grad_down)


def solution(mesh):
    in_specs = (
        P(("fsdp", "ep"), None),
        P(("fsdp", "ep"), None),
        P(("fsdp", "ep"), None),
        P(("fsdp", "ep"), None),
        P("fsdp", "ep", None),
        P("fsdp", "ep", None),
        P("fsdp", "ep", None),
    )
    out_specs = (
        P(("fsdp", "ep"), None),
        P(("fsdp", "ep"), None),
        P("fsdp", "ep", None),
        P("fsdp", "ep", None),
        P("fsdp", "ep", None),
    )
    return jax.shard_map(
        per_device, mesh=mesh, in_specs=in_specs, out_specs=out_specs, check_vma=False
    )
```

profile of v0, /device:TPU:0, one launch (start us, length us, event | category | flops | bytes accessed | tf_op | source)
XLA Modules:
  0.0 247.1 jit_solution(5933653130253614245)
XLA Ops:
  10.2 1.2 reduce-window.6
  15.0 20.6 %all_to_all.30 = bf16[4,32,2048]{2,1,0:T(8,128)(2,1)S(1)} all-to-all(bf16[4,32,2048]{2,1,0:T(8,128)(2,1)S(1)} %get-tuple-element.43), channel_id=1, replica_groups=mesh['fsdp'=8,'ep'=4] {'ep'}, dimensions={0} | all-to-all | bytes 1048576 | tf_op jit(solution)/shard_map/all_to_all | solution.py:65
  35.6 3.5 %all-to-all-start.1 = ((bf16[4,32,2048]{2,1,0:T(8,128)(2,1)}), bf16[4,32,2048]{2,1,0:T(8,128)(2,1)S(1)}, u32[]{:S(2)}, u32[]{:S(2)}) async-start(bf16[4,32,2048]{2,1,0:T(8,128)(2,1)} %get-tuple-element.44), calls=%async_computation.1 | async-start | bytes 1048576 | tf_op jit(solution)/shard_map/all_to_all | solution.py:66
  39.1 5.8 %all-gather.6.cloned.1.call-done = bf16[2048,1,768]{2,0,1:T(8,128)(2,1)} async-done(((bf16[256,1,768]{2,0,1:T(8,128)(2,1)}), bf16[2048,1,768]{2,0,1:T(8,128)(2,1)}) %all-gather.6.cloned.1.call-update) | async-done | bytes 3145744 | tf_op jit(solution)/shard_map/all_gather | solution.py:59
  45.0 34.2 %all-gather.8.cloned.1.call-done = bf16[2048,1,768]{2,0,1:T(8,128)(2,1)} async-done(((bf16[256,1,768]{2,0,1:T(8,128)(2,1)}), bf16[2048,1,768]{2,0,1:T(8,128)(2,1)}) %all-gather.8.cloned.1.call-update) | async-done | bytes 3145744 | tf_op jit(solution)/shard_map/all_gather | solution.py:60
  79.2 3.8 %fusion.1 = f32[128,1536]{1,0:T(8,128)S(1)} fusion(bf16[128,2048]{1,0:T(8,128)(2,1)S(1)} %bitcast.65, bf16[2048,768]{1,0:T(8,128)(2,1)} %bitcast.77, bf16[2048,768]{1,0:T(8,128)(2,1)} %bitcast.75), kind=kOutput, calls=%fused_computation.9 | convolution fusion | flops 817889280 | bytes 7602176 | tf_op jit(solution)/shard_map/dot_general | solution.py:71
  83.1 30.4 %all-gather.4.cloned.1.call-done = bf16[2048,1,768]{2,0,1:T(8,128)(2,1)} async-done(((bf16[256,1,768]{2,0,1:T(8,128)(2,1)}), bf16[2048,1,768]{2,0,1:T(8,128)(2,1)}) %all-gather.4.cloned.1.call-update) | async-done | bytes 3145744 | tf_op jit(solution)/shard_map/all_gather | solution.py:61
  113.4 3.2 %multiply_reduce_fusion = (bf16[128]{0:T(256)(128)(2,1)S(1)}, bf16[128,768]{1,0:T(8,128)(2,1)S(1)}, f32[128,768]{1,0:T(8,128)}) fusion(f32[128,1536]{1,0:T(8,128)S(1)} %fusion.1, bf16[128,2048]{1,0:T(8,128)(2,1)S(1)} %bitcast.69, bf16[2048,1,768]{2,0,1:T(8,128)(2,1)} %all-gather.4.cloned.1.call-done), kind=kOutput, calls=%fused_computation.27 | convolution fusion | flops 403537792 | bytes 5046528 | tf_op jit(solution)/shard_map/dot_general | solution.py:72
  117.3 4.6 %all-to-all-start.4 = ((bf16[4,1,32]{2,1,0:T(2,128)(2,1)}), bf16[4,1,32]{2,1,0:T(2,128)(2,1)S(1)}, u32[]{:S(2)}, u32[]{:S(2)}) async-start(bf16[4,1,32]{2,1,0:T(2,128)(2,1)} %convert_element_type.114), calls=%async_computation.4 | async-start | bytes 4096 | tf_op jit(solution)/shard_map/all_to_all | solution.py:86
  122.0 5.4 %all-to-all-done.4 = bf16[4,1,32]{2,1,0:T(2,128)(2,1)S(1)} async-done(((bf16[4,1,32]{2,1,0:T(2,128)(2,1)}), bf16[4,1,32]{2,1,0:T(2,128)(2,1)S(1)}, u32[]{:S(2)}, u32[]{:S(2)}) %all-to-all-start.4) | async-done | bytes 288 | tf_op jit(solution)/shard_map/all_to_all | solution.py:86
  127.4 9.0 %gather_fusion.3 = bf16[1024]{0:T(1024)(128)(2,1)S(1)} fusion(bf16[4,32]{1,0:T(4,128)(2,1)S(1)} %bitcast.62, s32[1024]{0:T(1024)S(1)} %bitcast.63), kind=kCustom, calls=%fused_computation.3 | custom fusion | bytes 12288 | tf_op jit(solution)/shard_map/jit(take_along_axis)/gather | solution.py:101
  137.3 1.5 gather_fusion.2
  138.9 7.9 %all_to_all.31 = bf16[4,1,32]{2,1,0:T(2,128)(2,1)S(1)} all-to-all(bf16[4,1,32]{2,1,0:T(2,128)(2,1)S(1)} %copy.51), channel_id=1, replica_groups=mesh['fsdp'=8,'ep'=4] {'ep'}, dimensions={0} | all-to-all | bytes 512 | tf_op jit(solution)/shard_map/all_to_all | solution.py:67
  146.9 1.2 multiply_convert_fusion.4
  148.1 1.0 convolution_convert_fusion.1
  149.1 1.8 convolution_convert_fusion
  151.0 11.6 %pad_maximum_fusion = bf16[2048,2304]{0,1:T(8,128)(2,1)} fusion(bf16[2048,768]{0,1:T(8,128)(2,1)S(1)} %convolution_convert_fusion.1, bf16[2048,1536]{0,1:T(8,128)(2,1)S(1)} %convolution_convert_fusion), kind=kLoop, calls=%fused_computation.5 | loop fusion | flops 18874368 | bytes 18874368 | tf_op jit(solution)/shard_map/concatenate | solution.py:109
  162.6 5.8 %fusion.4 = bf16[128,2048]{1,0:T(8,128)(2,1)} fusion(bf16[2048,768]{1,0:T(8,128)(2,1)} %bitcast.78, bf16[2048,768]{1,0:T(8,128)(2,1)} %bitcast.76, bf16[128,768]{1,0:T(8,128)(2,1)S(1)} %get-tuple-element.37, bf16[128,768]{1,0:T(8,128)(2,1)S(1)} %get-tuple-element.36), kind=kOutput, calls=%fused_computation.13 | convolution fusion | flops 818937856 | bytes 7208960 | tf_op jit(solution)/shard_map/dot_general | solution.py:31
  168.4 3.7 %all-to-all-start.3 = ((bf16[4,32,2048]{2,1,0:T(8,128)(2,1)}), bf16[4,32,2048]{2,1,0:T(8,128)(2,1)S(1)}, u32[]{:S(2)}, u32[]{:S(2)}) async-start(bf16[4,32,2048]{2,1,0:T(8,128)(2,1)} %bitcast.13), calls=%async_computation.3 | async-start | bytes 1048576 | tf_op jit(solution)/shard_map/all_to_all | solution.py:79
  172.3 12.2 %all-to-all-done.3 = bf16[4,32,2048]{2,1,0:T(8,128)(2,1)S(1)} async-done(((bf16[4,32,2048]{2,1,0:T(8,128)(2,1)}), bf16[4,32,2048]{2,1,0:T(8,128)(2,1)S(1)}, u32[]{:S(2)}, u32[]{:S(2)}) %all-to-all-start.3) | async-done | bytes 524320 | tf_op jit(solution)/shard_map/all_to_all | solution.py:79
  185.3 3.4 %scatter_custom_fusion = f32[256,2048]{1,0:T(8,128)S(1)} fusion(s32[128]{0:T(128)S(1)} %reshape.176, bf16[128,2048]{1,0:T(8,128)(2,1)} %bitcast.71, f32[]{:T(128)} %constant.15.clone.1, pred[128]{0:T(512)(128)(4,1)S(1)} %broadcast_in_dim.98), kind=kCustom, calls=%fused_computation.15 | custom fusion | flops 786432 | bytes 2622976 | tf_op jit(solution)/shard_map/scatter-add | solution.py:95
  188.7 1.1 convert_element_type.101
  189.8 46.6 %reduce-scatter.2.cloned.1.call-done = bf16[256,2304]{0,1:T(8,128)(2,1)} async-done(((bf16[2048,2304]{0,1:T(8,128)(2,1)}), bf16[256,2304]{0,1:T(8,128)(2,1)}) %reduce-scatter.2.cloned.1.call-update) | async-done | bytes 1179664 | tf_op jit(solution)/shard_map/reduce_scatter | solution.py:112
  236.5 1.3 slice_bitcast_fusion
  (56 shorter events, 12.0 us)
Async XLA Ops:
  7.2 4.9 %copy-start = (bf16[256,2048]{1,0:T(8,128)(2,1)S(1)}, bf16[256,2048]{1,0:T(8,128)(2,1)}, u32[]{:S(2)}) copy-start(bf16[256,2048]{1,0:T(8,128)(2,1)} %param.7) | copy-start | bytes 3145732
  7.2 5.8 %copy-start.1 = (bf16[256,2048]{1,0:T(8,128)(2,1)S(1)}, bf16[256,2048]{1,0:T(8,128)(2,1)}, u32[]{:S(2)}) copy-start(bf16[256,2048]{1,0:T(8,128)(2,1)} %param.8) | copy-start | bytes 3145732
  7.2 37.8 %all-gather.6.cloned.1.call-start = ((), (), s32[]{:S(2)}) async-start(), calls=%async_computation.7 | async-start | bytes 3538944 | tf_op jit(solution)/shard_map/all_gather | solution.py:59
  7.9 71.3 %all-gather.8.cloned.1.call-start = ((), (), s32[]{:S(2)}) async-start(), calls=%async_computation.8 | async-start | bytes 3538944 | tf_op jit(solution)/shard_map/all_gather | solution.py:60
  8.7 104.8 %all-gather.4.cloned.1.call-start = ((), (), s32[]{:S(2)}) async-start(), calls=%async_computation.6 | async-start | bytes 3538944 | tf_op jit(solution)/shard_map/all_gather | solution.py:61
  35.6 47.4 %all-to-all-start.1 = ((bf16[4,32,2048]{2,1,0:T(8,128)(2,1)}), bf16[4,32,2048]{2,1,0:T(8,128)(2,1)S(1)}, u32[]{:S(2)}, u32[]{:S(2)}) async-start(bf16[4,32,2048]{2,1,0:T(8,128)(2,1)} %get-tuple-element.44), calls=%async_computation.1 | async-start | bytes 1048576 | tf_op jit(solution)/shard_map/all_to_all | solution.py:66
  79.2 42.8 %copy-start.4 = (bf16[256,8]{0,1:T(8,128)(2,1)S(1)}, bf16[256,8]{0,1:T(8,128)(2,1)}, u32[]{:S(2)}) copy-start(bf16[256,8]{0,1:T(8,128)(2,1)} %param.10) | copy-start | bytes 12292
  83.0 53.5 %copy-start.3 = (s32[256,8]{0,1:T(8,128)S(1)}, s32[256,8]{0,1:T(8,128)}, u32[]{:S(2)}) copy-start(s32[256,8]{0,1:T(8,128)} %param.9) | copy-start | bytes 24580
  117.3 10.1 %all-to-all-start.4 = ((bf16[4,1,32]{2,1,0:T(2,128)(2,1)}), bf16[4,1,32]{2,1,0:T(2,128)(2,1)S(1)}, u32[]{:S(2)}, u32[]{:S(2)}) async-start(bf16[4,1,32]{2,1,0:T(2,128)(2,1)} %convert_element_type.114), calls=%async_computation.4 | async-start | bytes 4096 | tf_op jit(solution)/shard_map/all_to_all | solution.py:86
  121.9 114.5 %reduce-scatter.2.cloned.1.call-start = ((), (), s32[]{:S(2)}) async-start(), calls=%async_computation.9 | async-start | bytes 10616832 | tf_op jit(solution)/shard_map/reduce_scatter | solution.py:112
  168.4 16.0 %all-to-all-start.3 = ((bf16[4,32,2048]{2,1,0:T(8,128)(2,1)}), bf16[4,32,2048]{2,1,0:T(8,128)(2,1)S(1)}, u32[]{:S(2)}, u32[]{:S(2)}) async-start(bf16[4,32,2048]{2,1,0:T(8,128)(2,1)} %bitcast.13), calls=%async_computation.3 | async-start | bytes 1048576 | tf_op jit(solution)/shard_map/all_to_all | solution.py:79
  184.5 0.8 copy-start.2
Sparse Core Ops, SparseCore 0:
  9.9 35.0 all-gather.5
  46.8 32.3 all-gather.7
  81.1 32.3 all-gather.3
  162.7 73.7 reduce-scatter.1
where the time goes:
time: 248 us; the launch traced here: 247 us
  waiting for transfers between devices  137 us (55%)
  blocking collectives  28.5 us (11%)
  other arithmetic  21.3 us (9%)
  local copies, waits for them, and re-layouts  18.9 us (8%)
  matrix products  15.8 us (6%)
  between operations  13.9 us (6%)
  starting transfers between devices  11.9 us (5%)
    reduce_scatter x1, waiting for transfers between devices, per_device(): lax.psum_scatter(term.astype(jnp.bfloat16), 'fsdp', scatter_dimension=0,...  46.6 us
    all_gather x1, waiting for transfers between devices, per_device(): lax.all_gather(w_up, 'fsdp', axis=0, tiled=True)  34.2 us
    all_gather x1, waiting for transfers between devices, per_device(): lax.all_gather(w_down, 'fsdp', axis=0, tiled=True)  30.4 us
    all_to_all x1, blocking collectives, per_device(): lax.all_to_all(send_tokens, 'ep', split_axis=0, concat_axis=0, tiled=True)  20.6 us
    all_to_all x1, waiting for transfers between devices, per_device(): lax.all_to_all(row_grads.reshape(experts_here, slots, model_width), 'ep',...  12.2 us
    concatenate x1, other arithmetic, per_device(): jnp.concatenate([leading_product(rows_x, rows_delta), leading_product(row...  11.6 us
    gather x2, local copies, waits for them, and re-layouts, per_device(): jnp.take_along_axis(back_picks, safe_slot, axis=1).astype(jnp.float32)  9.05 us
    all_to_all x1, blocking collectives, per_device(): lax.all_to_all(send_gates, 'ep', split_axis=0, concat_axis=0, tiled=True)  7.89 us
  transfers between devices with their start and end apart: 7, of which 6 were waited for; matrix products, arithmetic and copies ran while one was open for 8% of the time, Pallas kernels for 0%

commit v1 on v0

v1 whole, which is shorter than its diff:
```python
import functools

import jax
import jax.numpy as jnp
from jax import lax
from jax.experimental import pallas as pl
from jax.experimental.pallas import tpu as pltpu
from jax.sharding import PartitionSpec as P

MOST = 32
F32 = jnp.float32
BF16 = jnp.bfloat16
MIB = 1024 * 1024


def mm(left, right):
    return lax.dot_general(left, right, (((1,), (0,)), ((), ())), preferred_element_type=F32)


def mm_lead(left, right):
    return lax.dot_general(left, right, (((0,), (0,)), ((), ())), preferred_element_type=F32)


def mm_trail(left, right):
    return lax.dot_general(left, right, (((1,), (1,)), ((), ())), preferred_element_type=F32)


def params(mib):
    return pltpu.CompilerParams(vmem_limit_bytes=mib * MIB)


def hop(x, axis, offset):
    return lax.ppermute(x, axis, [(i, i ^ offset) for i in range(lax.axis_size(axis))])


def prep_kernel(pos, ids, gates, tokens, grads, *outs, n_f, n_e):
    sends, select = outs[:n_e], outs[n_e]
    f, e = pos[0], pos[1]
    tok = ids.shape[1]
    width = tokens.shape[1] // n_f
    rows = max(16, n_e)
    row = lax.broadcasted_iota(jnp.int32, (rows, tok), 0)
    chosen = []
    weight = []
    stacked = jnp.zeros((rows, tok), F32)
    for k in range(n_e):
        match = ids[...] == (e ^ k)
        chosen.append(jnp.max(jnp.where(match, 1.0, 0.0), axis=0, keepdims=True))
        weight.append(jnp.sum(jnp.where(match, gates[...].astype(F32), 0.0), axis=0, keepdims=True))
        stacked = jnp.where(row == k, chosen[k], stacked)
    before = lax.broadcasted_iota(jnp.int32, (tok, tok), 0) < lax.broadcasted_iota(jnp.int32, (tok, tok), 1)
    slot = mm(stacked.astype(BF16), jnp.where(before, 1.0, 0.0).astype(BF16))
    want = lax.broadcasted_iota(jnp.int32, (MOST, tok), 0).astype(F32)
    picks = []
    scaled = []
    for k in range(n_e):
        hit = jnp.where(want == slot[k : k + 1], chosen[k], 0.0)
        picks.append(hit)
        scaled.append(hit * weight[k])
    picks = jnp.concatenate(picks, axis=0).astype(BF16)
    scaled = jnp.concatenate(scaled, axis=0).astype(BF16)
    select[...] = picks
    for j in range(n_f):
        at = pl.ds(pl.multiple_of((f ^ j) * width, width), width)
        here = slice(j * width, (j + 1) * width)
        x = mm(picks, tokens[:, at]).astype(BF16)
        q = mm(scaled, grads[:, at]).astype(BF16)
        for k in range(n_e):
            sends[k][:MOST, here] = x[k * MOST : (k + 1) * MOST]
            sends[k][MOST:, here] = q[k * MOST : (k + 1) * MOST]


def pack_kernel(*refs, n_f, n_e):
    recv, outs = refs[:n_e], refs[n_e:]
    width = recv[0].shape[1] // n_f
    rows = n_e * MOST
    for c, out in enumerate(outs):
        for side in range(2):
            j = 2 * c + side
            here = slice(j * width, (j + 1) * width)
            for k in range(n_e):
                out[side, k * MOST : (k + 1) * MOST] = recv[k][:MOST, here]
                out[side, rows + k * MOST : rows + (k + 1) * MOST] = recv[k][MOST:, here]


def up_kernel(*refs, n_f, n_e):
    recv = refs[:n_e]
    gates, ups = refs[n_e : n_e + n_f], refs[n_e + n_f : n_e + 2 * n_f]
    a_out, b_out = refs[n_e + 2 * n_f :]
    width = recv[0].shape[1] // n_f
    a = b = None
    for j in range(n_f):
        here = slice(j * width, (j + 1) * width)
        x = jnp.concatenate([r[:MOST, here] for r in recv], axis=0)
        pa, pb = mm(x, gates[j][...]), mm(x, ups[j][...])
        a, b = (pa, pb) if a is None else (a + pa, b + pb)
    a_out[...] = a
    b_out[...] = b


def delta_kernel(*refs, n_f, n_e):
    recv = refs[:n_e]
    low, high = refs[n_e : n_e + n_f], refs[n_e + n_f : n_e + 2 * n_f]
    a_in, b_in, first, second, pick_out = refs[n_e + 2 * n_f :]
    width = recv[0].shape[1] // n_f
    hidden = a_in.shape[1]
    r = None
    for j in range(n_f):
        here = slice(j * width, (j + 1) * width)
        q = jnp.concatenate([rows[MOST:, here] for rows in recv], axis=0)
        part = mm(q, jnp.concatenate([low[j][...], high[j][...]], axis=0))
        r = part if r is None else r + part
    a, b = a_in[...], b_in[...]
    s = jax.nn.sigmoid(a)
    silu = a * s
    h = (silu * b).astype(BF16)
    pick = jnp.sum(h.astype(F32) * r, axis=1, keepdims=True)
    da = (r * b * s * (1.0 + a * (1.0 - s))).astype(BF16)
    du = (r * silu).astype(BF16)
    half = a.shape[0] // 2
    for out, rows in ((first, slice(0, half)), (second, slice(half, 2 * half))):
        out[:, :hidden] = da[rows]
        out[:, hidden : 2 * hidden] = du[rows]
        out[:, 2 * hidden :] = h[rows]
    coarse = pick.astype(BF16)
    fine = (pick - coarse.astype(F32)).astype(BF16)
    lane = lax.broadcasted_iota(jnp.int32, pick_out.shape, 1)
    wide = pick_out.shape
    pick_out[...] = jnp.where(
        lane < wide[1] // 2, jnp.broadcast_to(coarse.astype(F32), wide), jnp.broadcast_to(fine.astype(F32), wide)
    ).astype(BF16)


def back_kernel(*refs, n_f, n_e):
    first, second, pick = refs[:3]
    gates, ups = refs[3 : 3 + n_f], refs[3 + n_f : 3 + 2 * n_f]
    outs = refs[3 + 2 * n_f :]
    width, hidden = gates[0].shape
    da = jnp.concatenate([first[:, :hidden], second[:, :hidden]], axis=0)
    du = jnp.concatenate([first[:, hidden : 2 * hidden], second[:, hidden : 2 * hidden]], axis=0)
    for j in range(n_f):
        c = (mm_trail(da, gates[j][...]) + mm_trail(du, ups[j][...])).astype(BF16)
        for k in range(n_e):
            outs[k][:, j * width : (j + 1) * width] = c[k * MOST : (k + 1) * MOST]
    for k in range(n_e):
        outs[k][:, n_f * width :] = pick[k * MOST : (k + 1) * MOST]


def weight_kernel(*refs, n_f):
    rows_of, firsts, seconds = refs[:n_f], refs[n_f : 2 * n_f], refs[2 * n_f : 3 * n_f]
    grad_gate, grad_up, grad_down = refs[3 * n_f :]
    hidden = grad_gate.shape[1]
    count = 2 * firsts[0].shape[0]
    both = down = None
    for j in range(n_f):
        side = j % 2
        x, q = rows_of[j][side, :count], rows_of[j][side, count:]
        d = jnp.concatenate([firsts[j][...], seconds[j][...]], axis=0)
        pb, pd = mm_lead(x, d[:, : 2 * hidden]), mm_lead(q, d[:, 2 * hidden :])
        both, down = (pb, pd) if both is None else (both + pb, down + pd)
    grad_gate[...] = both[:, :hidden].astype(BF16)
    grad_up[...] = both[:, hidden:].astype(BF16)
    grad_down[...] = down.astype(BF16)


def final_kernel(pos, ids, gates, select, *refs, n_f, n_e):
    back, in_grad, gate_grad = refs[:n_e], refs[n_e], refs[n_e + 1]
    f, e = pos[0], pos[1]
    width = in_grad.shape[1] // n_f
    total = n_f * width
    for j in range(n_f):
        at = pl.ds(pl.multiple_of((f ^ j) * width, width), width)
        c = jnp.concatenate([b[:, j * width : (j + 1) * width] for b in back], axis=0)
        in_grad[:, at] = mm_lead(select[...], c).astype(BF16)
    half = (back[0].shape[1] - total) // 2
    found = jnp.zeros(ids.shape, F32)
    for k in range(n_e):
        pick = back[k][:, total : total + 1].astype(F32) + back[k][:, total + half : total + half + 1].astype(F32)
        hit = select[k * MOST : (k + 1) * MOST].astype(F32)
        value = jnp.sum(hit * pick, axis=0, keepdims=True)
        found = found + jnp.where(ids[...] == (e ^ k), value, 0.0)
    gate_grad[...] = (found / gates[...].astype(F32)).astype(BF16)


def call(kernel, outs, mib, **static):
    return pl.pallas_call(functools.partial(kernel, **static), out_shape=outs, compiler_params=params(mib))


def call_at(kernel, inputs, outs, mib, **static):
    return pl.pallas_call(
        functools.partial(kernel, **static),
        out_shape=outs,
        in_specs=[pl.BlockSpec(memory_space=pltpu.SMEM)] + [pl.BlockSpec(memory_space=pltpu.VMEM)] * (inputs - 1),
        compiler_params=params(mib),
    )


def spread(x, bits):
    have = {0: x}
    for bit in bits:
        have.update({o ^ bit: hop(v, "fsdp", bit) for o, v in list(have.items())})
    return have


def swap_cores(have):
    return have | {o ^ 1: hop(v, "fsdp", 1) for o, v in have.items()}


def in_order(have):
    return [have[j] for j in range(len(have))]


def per_device(tokens, out_grad, expert_ids, gate_probs, w_gate, w_up, w_down):
    tok, model = tokens.shape
    local, _, hidden = w_gate.shape
    n_f, n_e = lax.axis_size("fsdp"), lax.axis_size("ep")
    rows = n_e * MOST
    sizes = dict(n_f=n_f, n_e=n_e)
    bits = [1 << i for i in range(1, n_f.bit_length() - 1)]
    mirrored = bits[::-1]
    shape = jax.ShapeDtypeStruct

    down = w_down[:, 0]
    gate_at = spread(w_gate[:, 0], bits)
    up_at = spread(w_up[:, 0], mirrored)
    low_at = spread(down[: local // 2], bits)
    high_at = spread(down[local // 2 :], mirrored)
    gate_at, up_at, low_at, high_at = map(in_order, map(swap_cores, (gate_at, up_at, low_at, high_at)))

    pos = jnp.stack([lax.axis_index("fsdp"), lax.axis_index("ep")]).astype(jnp.int32)
    ids, gates = expert_ids.T, gate_probs.T
    *sends, select = call_at(
        prep_kernel, 5, [shape((2 * MOST, model), BF16)] * n_e + [shape((rows, tok), BF16)], 16, **sizes
    )(pos, ids, gates, tokens, out_grad)
    recv = [sends[0]] + [hop(sends[k], "ep", k) for k in range(1, n_e)]

    packed = call(pack_kernel, [shape((2, 2 * rows, local), BF16)] * (n_f // 2), 8, **sizes)(*recv)
    rows_at = {0: packed[0]} | {2 * c: hop(packed[c], "fsdp", 2 * c) for c in range(1, n_f // 2)}
    rows_at = in_order(swap_cores(rows_at))

    a, b = call(up_kernel, [shape((rows, hidden), F32)] * 2, 16, **sizes)(*recv, *gate_at, *up_at)
    first, second, pick = call(
        delta_kernel, [shape((rows // 2, 3 * hidden), BF16)] * 2 + [shape((rows, 128), BF16)], 16, **sizes
    )(*recv, *low_at, *high_at, a, b)

    first_at = in_order(swap_cores(spread(first, bits)))
    second_at = in_order(swap_cores(spread(second, mirrored)))

    back = call(back_kernel, [shape((MOST, model + 128), BF16)] * n_e, 16, **sizes)(
        first, second, pick, *gate_at, *up_at
    )
    back = [back[0]] + [hop(back[k], "ep", k) for k in range(1, n_e)]
    in_grad, gate_grad = call_at(
        final_kernel, 4 + n_e, [shape((tok, model), BF16), shape(ids.shape, BF16)], 16, **sizes
    )(pos, ids, gates, select, *back)

    grads = call(weight_kernel, [shape((local, hidden), BF16)] * 3, 24, n_f=n_f)(*rows_at, *first_at, *second_at)
    return (in_grad, gate_grad.T, *(g[:, None] for g in grads))


def solution(mesh):
    tok = P(("fsdp", "ep"), None)
    weight = P("fsdp", "ep", None)
    return jax.shard_map(
        per_device,
        mesh=mesh,
        in_specs=(tok, tok, tok, tok, weight, weight, weight),
        out_specs=(tok, tok, weight, weight, weight),
        check_vma=False,
    )
```

time: 248 us -> 128 us (0.52)
  waiting for transfers between devices: 137 us -> 70.3 us
  starting transfers between devices: 11.9 us -> 41.6 us
  blocking collectives: 28.5 us -> 0 us
  other arithmetic: 21.3 us -> 0.07 us
  matrix products: 15.8 us -> 0 us
  local copies, waits for them, and re-layouts: 18.9 us -> 4.13 us
  between operations: 13.9 us -> 0.77 us
  Pallas kernels: 0 us -> 10.6 us
    all_gather x3 -> x0, waiting for transfers between devices: 70.4 us -> none  [the longest x1 34.2 us: per_device(): lax.all_gather(w_up, 'fsdp', axis=0, tiled=True)]
    ppermute x0 -> x55, waiting for transfers between devices: none -> 70.3 us  [hop(): lax.ppermute(x, axis, [(i, i ^ offset) for i in range(lax.axis_size(axis))])]
    reduce_scatter x1 -> x0, waiting for transfers between devices: 46.6 us -> none  [per_device(): lax.psum_scatter(term.astype(jnp.bfloat16), 'fsdp', scatter_dimension=0,...]
    ppermute x0 -> x55, starting transfers between devices: none -> 41.6 us  [hop(): lax.ppermute(x, axis, [(i, i ^ offset) for i in range(lax.axis_size(axis))])]
    all_to_all x2 -> x0, blocking collectives: 28.5 us -> none  [the longest x1 20.6 us: per_device(): lax.all_to_all(send_tokens, 'ep', split_axis=0, concat_axis=0, tiled=True)]
    all_to_all x3 -> x0, waiting for transfers between devices: 17.5 us -> none  [the longest x1 12.2 us: per_device(): lax.all_to_all(row_grads.reshape(experts_here, slots, model_width), 'ep',...]
    dot_general x5 -> x0, matrix products: 15.8 us -> none  [the longest x1 5.84 us: trailing_product(): lax.dot_general(left, right, (((1,), (1,)), ((), ())), preferred_element_...]
    gather x7 -> x0, local copies, waits for them, and re-layouts: 12.6 us -> none  [the longest x2 9.05 us: per_device(): jnp.take_along_axis(back_picks, safe_slot, axis=1).astype(jnp.float32)]
  transfers between devices with their start and end apart: 7 -> 55, of which waited for: 6 -> 20; matrix products, arithmetic and copies ran while one was open for 8% -> 0% of each run, Pallas kernels for 0% -> 6%
where the time goes in v1:
time: 128 us; the launch traced here: 127 us
  waiting for transfers between devices  70.3 us (55%)
  starting transfers between devices  41.6 us (32%)
  Pallas kernels  10.6 us (8%)
  local copies, waits for them, and re-layouts  4.13 us (3%)
    ppermute x55, waiting for transfers between devices, hop(): lax.ppermute(x, axis, [(i, i ^ offset) for i in range(lax.axis_size(axis))])  70.3 us
    ppermute x55, starting transfers between devices, hop(): lax.ppermute(x, axis, [(i, i ^ offset) for i in range(lax.axis_size(axis))])  41.6 us
    pallas_call x1, Pallas kernels, per_device(): call(weight_kernel, [shape((local, hidden), BF16)] * 3, 24, n_f=n_f)  3.46 us
    unnamed x12, local copies, waits for them, and re-layouts  3.08 us
  transfers between devices with their start and end apart: 55, of which 20 were waited for; matrix products, arithmetic and copies ran while one was open for 0% of the time, Pallas kernels for 6%

profile of v1, /device:TPU:0, one launch (start us, length us, event | category | flops | bytes accessed | tf_op | source)
XLA Modules:
  0.0 127.5 jit_solution(2450899724358979990)
XLA Ops:
  1.7 3.0 %collective-permute-start.13 = (bf16[128,768]{1,0:T(8,128)(2,1)S(1)}, bf16[128,768]{1,0:T(8,128)(2,1)S(1)}, u32[]{:S(2)}, u32[]{:S(2)}) collective-permute-start(bf16[128,768]{1,0:T(8,128)(2,1)S(1)} %get-tuple-element.51.refs_12_), channel_id=1, source_target_pairs={{0,16},{4,20},{8,24},{12,28},{16,0},{20,4},{24,8},{28,12},{1,17},{... | collective-permute-start | bytes 589832 | tf_op jit(solution)/shard_map/ppermute | solution.py:33
  11.0 1.6 %collective-permute-start = (bf16[64,2048]{1,0:T(8,128)(2,1)S(1)}, bf16[64,2048]{1,0:T(8,128)(2,1)S(1)}, u32[]{:S(2)}, u32[]{:S(2)}) collective-permute-start(bf16[64,2048]{1,0:T(8,128)(2,1)S(1)} %get-tuple-element.30), channel_id=1, source_target_pairs={{0,1},{1,0},{2,3},{3,2},{4,5},{5,4},{6,7},{7,6},{8,9},{9,8},{10,11... | collective-permute-start | bytes 786440 | tf_op jit(solution)/shard_map/ppermute | solution.py:33
  12.7 2.6 %collective-permute-start.1 = (bf16[64,2048]{1,0:T(8,128)(2,1)S(1)}, bf16[64,2048]{1,0:T(8,128)(2,1)S(1)}, u32[]{:S(2)}, u32[]{:S(2)}) collective-permute-start(bf16[64,2048]{1,0:T(8,128)(2,1)S(1)} %get-tuple-element.31), channel_id=1, source_target_pairs={{0,2},{1,3},{2,0},{3,1},{4,6},{5,7},{6,4},{7,5},{8,10},{9,11},{10,... | collective-permute-start | bytes 786440 | tf_op jit(solution)/shard_map/ppermute | solution.py:33
  15.8 1.9 %collective-permute-start.2 = (bf16[64,2048]{1,0:T(8,128)(2,1)S(1)}, bf16[64,2048]{1,0:T(8,128)(2,1)S(1)}, u32[]{:S(2)}, u32[]{:S(2)}) collective-permute-start(bf16[64,2048]{1,0:T(8,128)(2,1)S(1)} %get-tuple-element.32), channel_id=1, source_target_pairs={{0,3},{1,2},{2,1},{3,0},{4,7},{5,6},{6,5},{7,4},{8,11},{9,10},{10,... | collective-permute-start | bytes 786440 | tf_op jit(solution)/shard_map/ppermute | solution.py:33
  17.7 4.1 %collective-permute-done.4.refs_6_ = bf16[128,768]{1,0:T(8,128)(2,1)S(1)} collective-permute-done((bf16[128,768]{1,0:T(8,128)(2,1)S(1)}, bf16[128,768]{1,0:T(8,128)(2,1)S(1)}, u32[]{:S(2)}, u32[]{:S(2)}) %collective-permute-start.4) | collective-permute-done | bytes 196640 | tf_op jit(solution)/shard_map/ppermute | solution.py:33
  22.3 2.3 %collective-permute-done.refs_1_ = bf16[64,2048]{1,0:T(8,128)(2,1)S(1)} collective-permute-done((bf16[64,2048]{1,0:T(8,128)(2,1)S(1)}, bf16[64,2048]{1,0:T(8,128)(2,1)S(1)}, u32[]{:S(2)}, u32[]{:S(2)}) %collective-permute-start) | collective-permute-done | bytes 262176 | tf_op jit(solution)/shard_map/ppermute | solution.py:33
  26.1 7.8 %collective-permute-done.1.refs_2_ = bf16[64,2048]{1,0:T(8,128)(2,1)S(1)} collective-permute-done((bf16[64,2048]{1,0:T(8,128)(2,1)S(1)}, bf16[64,2048]{1,0:T(8,128)(2,1)S(1)}, u32[]{:S(2)}, u32[]{:S(2)}) %collective-permute-start.1) | collective-permute-done | bytes 262176 | tf_op jit(solution)/shard_map/ppermute | solution.py:33
  36.8 4.6 %collective-permute-done.8.refs_10_ = bf16[128,768]{1,0:T(8,128)(2,1)S(1)} collective-permute-done((bf16[128,768]{1,0:T(8,128)(2,1)S(1)}, bf16[128,768]{1,0:T(8,128)(2,1)S(1)}, u32[]{:S(2)}, u32[]{:S(2)}) %collective-permute-start.8) | collective-permute-done | bytes 196640 | tf_op jit(solution)/shard_map/ppermute | solution.py:33
  43.5 4.5 %collective-permute-done.18.refs_6_.refs_5_ = bf16[256,768]{1,0:T(8,128)(2,1)S(1)} collective-permute-done((bf16[256,768]{1,0:T(8,128)(2,1)S(1)}, bf16[256,768]{1,0:T(8,128)(2,1)S(1)}, u32[]{:S(2)}, u32[]{:S(2)}) %collective-permute-start.18) | collective-permute-done | bytes 393248 | tf_op jit(solution)/shard_map/ppermute | solution.py:33
  49.4 3.7 %collective-permute-done.27.refs_16_.refs_15_ = bf16[256,768]{1,0:T(8,128)(2,1)S(1)} collective-permute-done((bf16[256,768]{1,0:T(8,128)(2,1)S(1)}, bf16[256,768]{1,0:T(8,128)(2,1)S(1)}, u32[]{:S(2)}, u32[]{:S(2)}) %collective-permute-start.27) | collective-permute-done | bytes 393248 | tf_op jit(solution)/shard_map/ppermute | solution.py:33
  53.1 3.3 %collective-permute-done.25.refs_14_.refs_13_ = bf16[256,768]{1,0:T(8,128)(2,1)S(1)} collective-permute-done((bf16[256,768]{1,0:T(8,128)(2,1)S(1)}, bf16[256,768]{1,0:T(8,128)(2,1)S(1)}, u32[]{:S(2)}, u32[]{:S(2)}) %collective-permute-start.25) | collective-permute-done | bytes 393248 | tf_op jit(solution)/shard_map/ppermute | solution.py:33
  57.9 4.2 %collective-permute-done.35.refs_2_ = bf16[2,256,256]{2,1,0:T(8,128)(2,1)S(1)} collective-permute-done((bf16[2,256,256]{2,1,0:T(8,128)(2,1)S(1)}, bf16[2,256,256]{2,1,0:T(8,128)(2,1)S(1)}, u32[]{:S(2)}, u32[]{:S(2)}) %collective-permute-start.35) | collective-permute-done | bytes 262176 | tf_op jit(solution)/shard_map/ppermute | solution.py:33
  62.9 12.7 %collective-permute-done.39.refs_6_ = bf16[2,256,256]{2,1,0:T(8,128)(2,1)S(1)} collective-permute-done((bf16[2,256,256]{2,1,0:T(8,128)(2,1)S(1)}, bf16[2,256,256]{2,1,0:T(8,128)(2,1)S(1)}, u32[]{:S(2)}, u32[]{:S(2)}) %collective-permute-start.39) | collective-permute-done | bytes 262176 | tf_op jit(solution)/shard_map/ppermute | solution.py:33
  81.5 2.2 %shard_map.113 = (bf16[32,2176]{1,0:T(8,128)(2,1)S(1)}, bf16[32,2176]{1,0:T(8,128)(2,1)S(1)}, bf16[32,2176]{1,0:T(8,128)(2,1)S(1)}, bf16[32,2176]{1,0:T(8,128)(2,1)S(1)}) custom-call(bf16[64,2304]{1,0:T(8,128)(2,1)S(1)} %get-tuple-element.35.refs_0_.refs_8_, bf16[64,2304]{1,0:T(8,128)(2,1)S(1)} %get-tuple-element.36.refs_1_.refs_16_, ...), custom_call_target="tpu_custom_call" | custom-call | tf_op jit(solution)/shard_map/pallas_call | solution.py:249
  83.6 4.8 %collective-permute-start.31 = (bf16[32,2176]{1,0:T(8,128)(2,1)S(1)}, bf16[32,2176]{1,0:T(8,128)(2,1)S(1)}, u32[]{:S(2)}, u32[]{:S(2)}) collective-permute-start(bf16[32,2176]{1,0:T(8,128)(2,1)S(1)} %get-tuple-element.39), channel_id=1, source_target_pairs={{0,1},{1,0},{2,3},{3,2},{4,5},{5,4},{6,7},{7,6},{8,9},{9,8},{10,11... | collective-permute-start | bytes 417800 | tf_op jit(solution)/shard_map/ppermute | solution.py:33
  91.0 1.6 %collective-permute-done.31.refs_1_ = bf16[32,2176]{1,0:T(8,128)(2,1)S(1)} collective-permute-done((bf16[32,2176]{1,0:T(8,128)(2,1)S(1)}, bf16[32,2176]{1,0:T(8,128)(2,1)S(1)}, u32[]{:S(2)}, u32[]{:S(2)}) %collective-permute-start.31) | collective-permute-done | bytes 139296 | tf_op jit(solution)/shard_map/ppermute | solution.py:33
  92.6 2.7 %collective-permute-start.32 = (bf16[32,2176]{1,0:T(8,128)(2,1)S(1)}, bf16[32,2176]{1,0:T(8,128)(2,1)S(1)}, u32[]{:S(2)}, u32[]{:S(2)}) collective-permute-start(bf16[32,2176]{1,0:T(8,128)(2,1)S(1)} %get-tuple-element.40), channel_id=1, source_target_pairs={{0,2},{1,3},{2,0},{3,1},{4,6},{5,7},{6,4},{7,5},{8,10},{9,11},{10,... | collective-permute-start | bytes 417800 | tf_op jit(solution)/shard_map/ppermute | solution.py:33
  95.3 6.5 %collective-permute-done.32.refs_2_ = bf16[32,2176]{1,0:T(8,128)(2,1)S(1)} collective-permute-done((bf16[32,2176]{1,0:T(8,128)(2,1)S(1)}, bf16[32,2176]{1,0:T(8,128)(2,1)S(1)}, u32[]{:S(2)}, u32[]{:S(2)}) %collective-permute-start.32) | collective-permute-done | bytes 139296 | tf_op jit(solution)/shard_map/ppermute | solution.py:33
  101.8 2.8 %collective-permute-start.33 = (bf16[32,2176]{1,0:T(8,128)(2,1)S(1)}, bf16[32,2176]{1,0:T(8,128)(2,1)S(1)}, u32[]{:S(2)}, u32[]{:S(2)}) collective-permute-start(bf16[32,2176]{1,0:T(8,128)(2,1)S(1)} %get-tuple-element.41), channel_id=1, source_target_pairs={{0,3},{1,2},{2,1},{3,0},{4,7},{5,6},{6,5},{7,4},{8,11},{9,10},{10,... | collective-permute-start | bytes 417800 | tf_op jit(solution)/shard_map/ppermute | solution.py:33
  104.6 4.1 %collective-permute-done.33.refs_3_ = bf16[32,2176]{1,0:T(8,128)(2,1)S(1)} collective-permute-done((bf16[32,2176]{1,0:T(8,128)(2,1)S(1)}, bf16[32,2176]{1,0:T(8,128)(2,1)S(1)}, u32[]{:S(2)}, u32[]{:S(2)}) %collective-permute-start.33) | collective-permute-done | bytes 139296 | tf_op jit(solution)/shard_map/ppermute | solution.py:33
  112.8 4.7 %collective-permute-done.49.refs_18_ = bf16[64,2304]{1,0:T(8,128)(2,1)S(1)} collective-permute-done((bf16[64,2304]{1,0:T(8,128)(2,1)S(1)}, bf16[64,2304]{1,0:T(8,128)(2,1)S(1)}, u32[]{:S(2)}, u32[]{:S(2)}) %collective-permute-start.49) | collective-permute-done | bytes 294944 | tf_op jit(solution)/shard_map/ppermute | solution.py:33
  118.8 3.1 %collective-permute-done.53.refs_22_ = bf16[64,2304]{1,0:T(8,128)(2,1)S(1)} collective-permute-done((bf16[64,2304]{1,0:T(8,128)(2,1)S(1)}, bf16[64,2304]{1,0:T(8,128)(2,1)S(1)}, u32[]{:S(2)}, u32[]{:S(2)}) %collective-permute-start.53) | collective-permute-done | bytes 294944 | tf_op jit(solution)/shard_map/ppermute | solution.py:33
  122.0 2.0 %shard_map.114 = (bf16[256,2048]{1,0:T(8,128)(2,1)}, bf16[8,256]{1,0:T(8,128)(2,1)}) custom-call(s32[2]{0:T(128)S(1)} %pad_add_fusion.pos, s32[8,256]{1,0:T(8,128)S(1)} %bitcast.25, bf16[8,256]{1,0:T(8,128)(2,1)S(1)} %bitcast.27, bf16[128,256]{1,0:T(8,128)(2,1)S(1)} %get-tuple-element.28.select, bf16[32,2176]{1,0:T(8,128)(2,1)S(1)} %get-tuple-element.38.refs_0_, ...), custom_call_target="tpu_custom_call" | custom-call | tf_op jit(solution)/shard_map/pallas_call | solution.py:253
  124.0 3.5 %shard_map.116 = (bf16[256,768]{1,0:T(8,128)(2,1)}, bf16[256,768]{1,0:T(8,128)(2,1)}, bf16[256,768]{1,0:T(8,128)(2,1)}) custom-call(bf16[2,256,256]{2,1,0:T(8,128)(2,1)S(1)} %get-tuple-element.44.refs_0_, bf16[2,256,256]{2,1,0:T(8,128)(2,1)S(1)} %collective-permute-done.34.refs_1_, bf16[2,256,256]{2,1,0:T(8,128)(2,1)S(1)} %collective-permute-done.35.refs_2_, ...), custom_call_target="tpu_custom_call" | custom-call | tf_op jit(solution)/shard_map/pallas_call | solution.py:257
  (107 shorter events, 32.5 us)
Async XLA Ops:
  11.0 13.6 %collective-permute-start = (bf16[64,2048]{1,0:T(8,128)(2,1)S(1)}, bf16[64,2048]{1,0:T(8,128)(2,1)S(1)}, u32[]{:S(2)}, u32[]{:S(2)}) collective-permute-start(bf16[64,2048]{1,0:T(8,128)(2,1)S(1)} %get-tuple-element.30), channel_id=1, source_target_pairs={{0,1},{1,0},{2,3},{3,2},{4,5},{5,4},{6,7},{7,6},{8,9},{9,8},{10,11... | collective-permute-start | bytes 786440 | tf_op jit(solution)/shard_map/ppermute | solution.py:33
  12.7 21.3 %collective-permute-start.1 = (bf16[64,2048]{1,0:T(8,128)(2,1)S(1)}, bf16[64,2048]{1,0:T(8,128)(2,1)S(1)}, u32[]{:S(2)}, u32[]{:S(2)}) collective-permute-start(bf16[64,2048]{1,0:T(8,128)(2,1)S(1)} %get-tuple-element.31), channel_id=1, source_target_pairs={{0,2},{1,3},{2,0},{3,1},{4,6},{5,7},{6,4},{7,5},{8,10},{9,11},{10,... | collective-permute-start | bytes 786440 | tf_op jit(solution)/shard_map/ppermute | solution.py:33
  15.8 18.2 %collective-permute-start.2 = (bf16[64,2048]{1,0:T(8,128)(2,1)S(1)}, bf16[64,2048]{1,0:T(8,128)(2,1)S(1)}, u32[]{:S(2)}, u32[]{:S(2)}) collective-permute-start(bf16[64,2048]{1,0:T(8,128)(2,1)S(1)} %get-tuple-element.32), channel_id=1, source_target_pairs={{0,3},{1,2},{2,1},{3,0},{4,7},{5,6},{6,5},{7,4},{8,11},{9,10},{10,... | collective-permute-start | bytes 786440 | tf_op jit(solution)/shard_map/ppermute | solution.py:33
  21.7 12.8 %collective-permute-start.15 = (bf16[128,768]{1,0:T(8,128)(2,1)S(1)}, bf16[128,768]{1,0:T(8,128)(2,1)S(1)}, u32[]{:S(2)}, u32[]{:S(2)}) collective-permute-start(bf16[128,768]{1,0:T(8,128)(2,1)S(1)} %collective-permute-done.13.refs_16_), channel_id=1, source_target_pairs={{0,8},{4,12},{8,0},{12,4},{16,24},{20,28},{24,16},{28,20},{1,9},{5... | collective-permute-start | bytes 589832 | tf_op jit(solution)/shard_map/ppermute | solution.py:33
  22.3 13.7 %collective-permute-start.14 = (bf16[128,768]{1,0:T(8,128)(2,1)S(1)}, bf16[128,768]{1,0:T(8,128)(2,1)S(1)}, u32[]{:S(2)}, u32[]{:S(2)}) collective-permute-start(bf16[128,768]{1,0:T(8,128)(2,1)S(1)} %collective-permute-done.13.refs_16_), channel_id=1, source_target_pairs={{0,4},{4,0},{8,12},{12,8},{16,20},{20,16},{24,28},{28,24},{1,5},{5... | collective-permute-start | bytes 589832 | tf_op jit(solution)/shard_map/ppermute | solution.py:33
  24.6 18.8 %collective-permute-start.20 = (bf16[256,768]{1,0:T(8,128)(2,1)S(1)}, bf16[256,768]{1,0:T(8,128)(2,1)S(1)}, u32[]{:S(2)}, u32[]{:S(2)}) collective-permute-start(bf16[256,768]{1,0:T(8,128)(2,1)S(1)} %bitcast.14), channel_id=1, source_target_pairs={{0,16},{4,20},{8,24},{12,28},{16,0},{20,4},{24,8},{28,12},{1,17},{... | collective-permute-start | bytes 1179656 | tf_op jit(solution)/shard_map/ppermute | solution.py:33
  36.0 12.0 %collective-permute-start.18 = (bf16[256,768]{1,0:T(8,128)(2,1)S(1)}, bf16[256,768]{1,0:T(8,128)(2,1)S(1)}, u32[]{:S(2)}, u32[]{:S(2)}) collective-permute-start(bf16[256,768]{1,0:T(8,128)(2,1)S(1)} %bitcast.15), channel_id=1, source_target_pairs={{0,8},{4,12},{8,0},{12,4},{16,24},{20,28},{24,16},{28,20},{1,9},{5... | collective-permute-start | bytes 1179656 | tf_op jit(solution)/shard_map/ppermute | solution.py:33
  36.6 11.9 %collective-permute-start.17 = (bf16[256,768]{1,0:T(8,128)(2,1)S(1)}, bf16[256,768]{1,0:T(8,128)(2,1)S(1)}, u32[]{:S(2)}, u32[]{:S(2)}) collective-permute-start(bf16[256,768]{1,0:T(8,128)(2,1)S(1)} %bitcast.16), channel_id=1, source_target_pairs={{0,4},{4,0},{8,12},{12,8},{16,20},{20,16},{24,28},{28,24},{1,5},{5... | collective-permute-start | bytes 1179656 | tf_op jit(solution)/shard_map/ppermute | solution.py:33
  41.4 11.8 %collective-permute-start.27 = (bf16[256,768]{1,0:T(8,128)(2,1)S(1)}, bf16[256,768]{1,0:T(8,128)(2,1)S(1)}, u32[]{:S(2)}, u32[]{:S(2)}) collective-permute-start(bf16[256,768]{1,0:T(8,128)(2,1)S(1)} %bitcast.19), channel_id=1, source_target_pairs={{0,16},{4,20},{8,24},{12,28},{16,0},{20,4},{24,8},{28,12},{1,17},{... | collective-permute-start | bytes 1179656 | tf_op jit(solution)/shard_map/ppermute | solution.py:33
  42.9 13.5 %collective-permute-start.25 = (bf16[256,768]{1,0:T(8,128)(2,1)S(1)}, bf16[256,768]{1,0:T(8,128)(2,1)S(1)}, u32[]{:S(2)}, u32[]{:S(2)}) collective-permute-start(bf16[256,768]{1,0:T(8,128)(2,1)S(1)} %bitcast.20), channel_id=1, source_target_pairs={{0,8},{4,12},{8,0},{12,4},{16,24},{20,28},{24,16},{28,20},{1,9},{5... | collective-permute-start | bytes 1179656 | tf_op jit(solution)/shard_map/ppermute | solution.py:33
  43.4 13.9 %collective-permute-start.24 = (bf16[256,768]{1,0:T(8,128)(2,1)S(1)}, bf16[256,768]{1,0:T(8,128)(2,1)S(1)}, u32[]{:S(2)}, u32[]{:S(2)}) collective-permute-start(bf16[256,768]{1,0:T(8,128)(2,1)S(1)} %bitcast.21), channel_id=1, source_target_pairs={{0,4},{4,0},{8,12},{12,8},{16,20},{20,16},{24,28},{28,24},{1,5},{5... | collective-permute-start | bytes 1179656 | tf_op jit(solution)/shard_map/ppermute | solution.py:33
  48.0 14.0 %collective-permute-start.35 = (bf16[2,256,256]{2,1,0:T(8,128)(2,1)S(1)}, bf16[2,256,256]{2,1,0:T(8,128)(2,1)S(1)}, u32[]{:S(2)}, u32[]{:S(2)}) collective-permute-start(bf16[2,256,256]{2,1,0:T(8,128)(2,1)S(1)} %get-tuple-element.45), channel_id=1, source_target_pairs={{0,8},{4,12},{8,0},{12,4},{16,24},{20,28},{24,16},{28,20},{1,9},{5... | collective-permute-start | bytes 786440 | tf_op jit(solution)/shard_map/ppermute | solution.py:33
  48.5 14.4 %collective-permute-start.37 = (bf16[2,256,256]{2,1,0:T(8,128)(2,1)S(1)}, bf16[2,256,256]{2,1,0:T(8,128)(2,1)S(1)}, u32[]{:S(2)}, u32[]{:S(2)}) collective-permute-start(bf16[2,256,256]{2,1,0:T(8,128)(2,1)S(1)} %get-tuple-element.46), channel_id=1, source_target_pairs={{0,16},{4,20},{8,24},{12,28},{16,0},{20,4},{24,8},{28,12},{1,17},{... | collective-permute-start | bytes 786440 | tf_op jit(solution)/shard_map/ppermute | solution.py:33
  53.1 23.0 %collective-permute-start.21 = (bf16[256,768]{1,0:T(8,128)(2,1)S(1)}, bf16[256,768]{1,0:T(8,128)(2,1)S(1)}, u32[]{:S(2)}, u32[]{:S(2)}) collective-permute-start(bf16[256,768]{1,0:T(8,128)(2,1)S(1)} %collective-permute-done.20.refs_8_.refs_7_), channel_id=1, source_target_pairs={{0,4},{4,0},{8,12},{12,8},{16,20},{20,16},{24,28},{28,24},{1,5},{5... | collective-permute-start | bytes 1179656 | tf_op jit(solution)/shard_map/ppermute | solution.py:33
  56.4 19.8 %collective-permute-start.22 = (bf16[256,768]{1,0:T(8,128)(2,1)S(1)}, bf16[256,768]{1,0:T(8,128)(2,1)S(1)}, u32[]{:S(2)}, u32[]{:S(2)}) collective-permute-start(bf16[256,768]{1,0:T(8,128)(2,1)S(1)} %collective-permute-done.18.refs_6_.refs_5_), channel_id=1, source_target_pairs={{0,16},{4,20},{8,24},{12,28},{16,0},{20,4},{24,8},{28,12},{1,17},{... | collective-permute-start | bytes 1179656 | tf_op jit(solution)/shard_map/ppermute | solution.py:33
  57.3 19.3 %collective-permute-start.29 = (bf16[256,768]{1,0:T(8,128)(2,1)S(1)}, bf16[256,768]{1,0:T(8,128)(2,1)S(1)}, u32[]{:S(2)}, u32[]{:S(2)}) collective-permute-start(bf16[256,768]{1,0:T(8,128)(2,1)S(1)} %collective-permute-done.27.refs_16_.refs_15_), channel_id=1, source_target_pairs={{0,8},{4,12},{8,0},{12,4},{16,24},{20,28},{24,16},{28,20},{1,9},{5... | collective-permute-start | bytes 1179656 | tf_op jit(solution)/shard_map/ppermute | solution.py:33
  62.0 13.6 %collective-permute-start.39 = (bf16[2,256,256]{2,1,0:T(8,128)(2,1)S(1)}, bf16[2,256,256]{2,1,0:T(8,128)(2,1)S(1)}, u32[]{:S(2)}, u32[]{:S(2)}) collective-permute-start(bf16[2,256,256]{2,1,0:T(8,128)(2,1)S(1)} %get-tuple-element.47), channel_id=1, source_target_pairs={{0,24},{4,28},{8,16},{12,20},{16,8},{20,12},{24,0},{28,4},{1,25},{... | collective-permute-start | bytes 786440 | tf_op jit(solution)/shard_map/ppermute | solution.py:33
  62.9 12.7 %collective-permute-start.16 = (bf16[128,768]{1,0:T(8,128)(2,1)S(1)}, bf16[128,768]{1,0:T(8,128)(2,1)S(1)}, u32[]{:S(2)}, u32[]{:S(2)}) collective-permute-start(bf16[128,768]{1,0:T(8,128)(2,1)S(1)} %collective-permute-done.15.refs_18_), channel_id=1, source_target_pairs={{0,4},{4,0},{8,12},{12,8},{16,20},{20,16},{24,28},{28,24},{1,5},{5... | collective-permute-start | bytes 589832 | tf_op jit(solution)/shard_map/ppermute | solution.py:33
  78.5 11.5 %collective-permute-start.36 = (bf16[2,256,256]{2,1,0:T(8,128)(2,1)S(1)}, bf16[2,256,256]{2,1,0:T(8,128)(2,1)S(1)}, u32[]{:S(2)}, u32[]{:S(2)}) collective-permute-start(bf16[2,256,256]{2,1,0:T(8,128)(2,1)S(1)} %collective-permute-done.35.refs_2_), channel_id=1, source_target_pairs={{0,4},{4,0},{8,12},{12,8},{16,20},{20,16},{24,28},{28,24},{1,5},{5... | collective-permute-start | bytes 786440 | tf_op jit(solution)/shard_map/ppermute | solution.py:33
  79.0 11.4 %collective-permute-start.38 = (bf16[2,256,256]{2,1,0:T(8,128)(2,1)S(1)}, bf16[2,256,256]{2,1,0:T(8,128)(2,1)S(1)}, u32[]{:S(2)}, u32[]{:S(2)}) collective-permute-start(bf16[2,256,256]{2,1,0:T(8,128)(2,1)S(1)} %collective-permute-done.37.refs_4_), channel_id=1, source_target_pairs={{0,4},{4,0},{8,12},{12,8},{16,20},{20,16},{24,28},{28,24},{1,5},{5... | collective-permute-start | bytes 786440 | tf_op jit(solution)/shard_map/ppermute | solution.py:33
  88.4 20.9 %collective-permute-start.44 = (bf16[64,2304]{1,0:T(8,128)(2,1)S(1)}, bf16[64,2304]{1,0:T(8,128)(2,1)S(1)}, u32[]{:S(2)}, u32[]{:S(2)}) collective-permute-start(bf16[64,2304]{1,0:T(8,128)(2,1)S(1)} %get-tuple-element.35.refs_0_.refs_8_), channel_id=1, source_target_pairs={{0,16},{4,20},{8,24},{12,28},{16,0},{20,4},{24,8},{28,12},{1,17},{... | collective-permute-start | bytes 884744 | tf_op jit(solution)/shard_map/ppermute | solution.py:33
  89.9 19.4 %collective-permute-start.42 = (bf16[64,2304]{1,0:T(8,128)(2,1)S(1)}, bf16[64,2304]{1,0:T(8,128)(2,1)S(1)}, u32[]{:S(2)}, u32[]{:S(2)}) collective-permute-start(bf16[64,2304]{1,0:T(8,128)(2,1)S(1)} %get-tuple-element.35.refs_0_.refs_8_), channel_id=1, source_target_pairs={{0,8},{4,12},{8,0},{12,4},{16,24},{20,28},{24,16},{28,20},{1,9},{5... | collective-permute-start | bytes 884744 | tf_op jit(solution)/shard_map/ppermute | solution.py:33
  90.5 19.4 %collective-permute-start.41 = (bf16[64,2304]{1,0:T(8,128)(2,1)S(1)}, bf16[64,2304]{1,0:T(8,128)(2,1)S(1)}, u32[]{:S(2)}, u32[]{:S(2)}) collective-permute-start(bf16[64,2304]{1,0:T(8,128)(2,1)S(1)} %get-tuple-element.35.refs_0_.refs_8_), channel_id=1, source_target_pairs={{0,4},{4,0},{8,12},{12,8},{16,20},{20,16},{24,28},{28,24},{1,5},{5... | collective-permute-start | bytes 884744 | tf_op jit(solution)/shard_map/ppermute | solution.py:33
  90.5 20.9 %collective-permute-start.51 = (bf16[64,2304]{1,0:T(8,128)(2,1)S(1)}, bf16[64,2304]{1,0:T(8,128)(2,1)S(1)}, u32[]{:S(2)}, u32[]{:S(2)}) collective-permute-start(bf16[64,2304]{1,0:T(8,128)(2,1)S(1)} %get-tuple-element.36.refs_1_.refs_16_), channel_id=1, source_target_pairs={{0,16},{4,20},{8,24},{12,28},{16,0},{20,4},{24,8},{28,12},{1,17},{... | collective-permute-start | bytes 884744 | tf_op jit(solution)/shard_map/ppermute | solution.py:33
  (37 other events, 255.5 us)

commit v2 on v1

v2 whole, which is shorter than its diff:
```python
import functools

import jax
import jax.numpy as jnp
from jax import lax
from jax.experimental import pallas as pl
from jax.experimental.pallas import tpu as pltpu
from jax.sharding import PartitionSpec as P

MOST = 32
F32 = jnp.float32
BF16 = jnp.bfloat16
MIB = 1024 * 1024


def mm(left, right):
    return lax.dot_general(left, right, (((1,), (0,)), ((), ())), preferred_element_type=F32)


def mm_lead(left, right):
    return lax.dot_general(left, right, (((0,), (0,)), ((), ())), preferred_element_type=F32)


def mm_trail(left, right):
    return lax.dot_general(left, right, (((1,), (1,)), ((), ())), preferred_element_type=F32)


def hop(x, axis, offset):
    return lax.ppermute(x, axis, [(i, i ^ offset) for i in range(lax.axis_size(axis))])


class Copies:
    def __init__(self, sems):
        self.sems, self.made, self.waited = sems, [], 0

    def start(self, source, target):
        self.made.append(pltpu.make_async_copy(source, target, self.sems.at[len(self.made)]))
        self.made[-1].start()

    def wait(self, count=None):
        for copy in self.made[self.waited : None if count is None else self.waited + count]:
            copy.wait()
            self.waited += 1


def split_kernel(gate, up, down, first, second, sems):
    width = gate.shape[0]
    half = width // 2
    fetch = Copies(sems)
    fetch.start(gate, first.at[:width])
    fetch.start(down.at[:half], first.at[width:])
    fetch.start(up, second.at[:width])
    fetch.start(down.at[half:], second.at[width:])
    fetch.wait()


def prep_kernel(pos, ids, gates, tokens_in, grads_in, *refs, n_f, n_e):
    sends, select = refs[:n_e], refs[n_e]
    tokens, grads, sems = refs[n_e + 1 :]
    fetch = [
        pltpu.make_async_copy(tokens_in, tokens, sems.at[0]),
        pltpu.make_async_copy(grads_in, grads, sems.at[1]),
    ]
    for copy in fetch:
        copy.start()
    f, e = pos[0], pos[1]
    tok = ids.shape[1]
    width = tokens.shape[1] // n_f
    rows = max(16, n_e)
    row = lax.broadcasted_iota(jnp.int32, (rows, tok), 0)
    chosen = []
    weight = []
    stacked = jnp.zeros((rows, tok), F32)
    for k in range(n_e):
        match = ids[...] == (e ^ k)
        chosen.append(jnp.max(jnp.where(match, 1.0, 0.0), axis=0, keepdims=True))
        weight.append(jnp.sum(jnp.where(match, gates[...].astype(F32), 0.0), axis=0, keepdims=True))
        stacked = jnp.where(row == k, chosen[k], stacked)
    before = lax.broadcasted_iota(jnp.int32, (tok, tok), 0) < lax.broadcasted_iota(jnp.int32, (tok, tok), 1)
    slot = mm(stacked.astype(BF16), jnp.where(before, 1.0, 0.0).astype(BF16))
    want = lax.broadcasted_iota(jnp.int32, (MOST, tok), 0).astype(F32)
    picks = []
    scaled = []
    for k in range(n_e):
        hit = jnp.where(want == slot[k : k + 1], chosen[k], 0.0)
        picks.append(hit)
        scaled.append(hit * weight[k])
    picks = jnp.concatenate(picks, axis=0).astype(BF16)
    scaled = jnp.concatenate(scaled, axis=0).astype(BF16)
    select[...] = picks
    for copy in fetch:
        copy.wait()
    for j in range(n_f):
        at = pl.ds(pl.multiple_of((f ^ j) * width, width), width)
        here = slice(j // 2 * width, (j // 2 + 1) * width)
        x = mm(picks, tokens[:, at]).astype(BF16)
        q = mm(scaled, grads[:, at]).astype(BF16)
        for k in range(n_e):
            sends[k][j % 2, :MOST, here] = x[k * MOST : (k + 1) * MOST]
            sends[k][j % 2, MOST:, here] = q[k * MOST : (k + 1) * MOST]


def pack_kernel(*refs, n_e):
    sides = refs[:n_e], refs[n_e : 2 * n_e]
    outs = refs[2 * n_e :]
    width = outs[0].shape[2]
    rows = n_e * MOST
    for i, out in enumerate(outs):
        here = slice((i + 1) * width, (i + 2) * width)
        for side in range(2):
            for k in range(n_e):
                out[side, k * MOST : (k + 1) * MOST] = sides[side][k][side, :MOST, here]
                out[side, rows + k * MOST : rows + (k + 1) * MOST] = sides[side][k][side, MOST:, here]


def forward_kernel(*refs, n_e, entries, carried):
    sides = refs[:n_e], refs[n_e : 2 * n_e]
    refs = refs[2 * n_e :]
    if carried:
        total_in, refs = refs[0], refs[1:]
    count = len(entries)
    firsts, seconds, refs = refs[:count], refs[count : 2 * count], refs[2 * count :]
    outs, (gate, up, down, sems) = refs[:-4], refs[-4:]
    hidden = gate.shape[1]
    width = gate.shape[0] // count
    half = width // 2
    fetch = Copies(sems)
    for i in range(count):
        fetch.start(firsts[i].at[:width], gate.at[pl.ds(i * width, width)])
        fetch.start(seconds[i].at[:width], up.at[pl.ds(i * width, width)])
        fetch.start(firsts[i].at[width:], down.at[pl.ds(i * width, half)])
        fetch.start(seconds[i].at[width:], down.at[pl.ds(i * width + half, half)])

    def rows_of(part):
        return jnp.concatenate(
            [
                jnp.concatenate([sides[side][k][side, part, i * width : (i + 1) * width] for i in entries], axis=1)
                for side in range(2)
                for k in range(n_e)
            ],
            axis=0,
        )

    x, q = rows_of(slice(0, MOST)), rows_of(slice(MOST, 2 * MOST))
    fetch.wait()
    rows = n_e * MOST
    for at, (left, right) in enumerate(((x, gate), (x, up), (q, down))):
        here = slice(at * hidden, (at + 1) * hidden)
        part = mm(left, right[...])
        if carried:
            part = part + total_in[:, here]
            outs[0][:, here] = part[:rows]
            outs[1][:, here] = part[rows:].astype(BF16)
        else:
            outs[0][:, here] = part


def delta_kernel(own, got, first, second, pick_out):
    hidden = own.shape[1] // 3
    a, b, r = (
        own[:, at * hidden : (at + 1) * hidden] + got[:, at * hidden : (at + 1) * hidden].astype(F32) for at in range(3)
    )
    s = jax.nn.sigmoid(a)
    silu = a * s
    h = (silu * b).astype(BF16)
    pick = jnp.sum(h.astype(F32) * r, axis=1, keepdims=True)
    da = (r * b * s * (1.0 + a * (1.0 - s))).astype(BF16)
    du = (r * silu).astype(BF16)
    half = a.shape[0] // 2
    for out, rows in ((first, slice(0, half)), (second, slice(half, 2 * half))):
        out[:, :hidden] = da[rows]
        out[:, hidden : 2 * hidden] = du[rows]
        out[:, 2 * hidden :] = h[rows]
    coarse = pick.astype(BF16)
    fine = (pick - coarse.astype(F32)).astype(BF16)
    wide = pick_out.shape
    lane = lax.broadcasted_iota(jnp.int32, wide, 1)
    pick_out[...] = jnp.where(
        lane < wide[1] // 2, jnp.broadcast_to(coarse.astype(F32), wide), jnp.broadcast_to(fine.astype(F32), wide)
    ).astype(BF16)


def back_kernel(first, second, first_other, second_other, pick, *refs, n, n_e):
    firsts, seconds, outs = refs[:n], refs[n : 2 * n], refs[2 * n : 2 * n + n_e]
    gate, up, sems = refs[2 * n + n_e :]
    hidden = gate.shape[2]
    width = gate.shape[1]
    fetch = Copies(sems)
    for i in range(n):
        fetch.start(firsts[i].at[:width], gate.at[i])
        fetch.start(seconds[i].at[:width], up.at[i])
    parts = (first, second, first_other, second_other)
    da = jnp.concatenate([p[:, :hidden] for p in parts], axis=0)
    du = jnp.concatenate([p[:, hidden : 2 * hidden] for p in parts], axis=0)
    for i in range(n):
        fetch.wait(2)
        c = (mm_trail(da, gate[i]) + mm_trail(du, up[i])).astype(BF16)
        here = slice(i * width, (i + 1) * width)
        for side in range(2):
            for k in range(n_e):
                at = (side * n_e + k) * MOST
                outs[k][side, :, here] = c[at : at + MOST]
    for side in range(2):
        for k in range(n_e):
            outs[k][side, :, n * width :] = pick[k * MOST : (k + 1) * MOST]


def weight_kernel(*refs, n_e, entries, carried):
    if 0 in entries:
        sides, refs = (refs[:n_e], refs[n_e : 2 * n_e]), refs[2 * n_e :]
    if carried:
        total_in, refs = refs[0], refs[1:]
    far = [i for i in entries if i]
    got, deltas = refs[: len(far)], refs[len(far) : len(far) + 4 * len(entries)]
    outs, (x, q, d, sems) = refs[len(far) + 4 * len(entries) : -4], refs[-4:]
    width, hidden = x.shape[1], d.shape[1] // 3
    rows = n_e * MOST
    fetch = Copies(sems)
    for i, p in enumerate(deltas):
        fetch.start(p, d.at[pl.ds(i * rows // 2, rows // 2)])
    for place, i in enumerate(entries):
        if i == 0:
            continue
        for side in range(2):
            at = pl.ds((2 * place + side) * rows, rows)
            fetch.start(got[far.index(i)].at[side, :rows], x.at[at])
            fetch.start(got[far.index(i)].at[side, rows:], q.at[at])
    if 0 in entries:
        for side in range(2):
            for k in range(n_e):
                at = slice(side * rows + k * MOST, side * rows + (k + 1) * MOST)
                x[at] = sides[side][k][side, :MOST, :width]
                q[at] = sides[side][k][side, MOST:, :width]
    fetch.wait()
    for at, left in enumerate((x, x, q)):
        here = slice(at * hidden, (at + 1) * hidden)
        part = mm_lead(left[...], d[:, here])
        if carried:
            outs[at][...] = (total_in[:, here] + part).astype(BF16)
        else:
            outs[0][:, here] = part


def final_kernel(pos, ids, gates, select, *refs, n_f, n_e):
    mine, other, (in_grad, gate_grad) = refs[:n_e], refs[n_e : 2 * n_e], refs[2 * n_e :]
    f, e = pos[0], pos[1]
    width = in_grad.shape[1] // n_f
    total = n_f // 2 * width
    for j in range(n_f):
        at = pl.ds(pl.multiple_of((f ^ j) * width, width), width)
        here = slice(j // 2 * width, (j // 2 + 1) * width)
        c = jnp.concatenate([(other if j % 2 else mine)[k][j % 2, :, here] for k in range(n_e)], axis=0)
        in_grad[:, at] = mm_lead(select[...], c).astype(BF16)
    half = (mine[0].shape[2] - total) // 2
    found = jnp.zeros(ids.shape, F32)
    for k in range(n_e):
        pick = mine[k][0, :, total : total + 1].astype(F32) + mine[k][0, :, total + half : total + half + 1].astype(F32)
        hit = select[k * MOST : (k + 1) * MOST].astype(F32)
        value = jnp.sum(hit * pick, axis=0, keepdims=True)
        found = found + jnp.where(ids[...] == (e ^ k), value, 0.0)
    gate_grad[...] = (found / gates[...].astype(F32)).astype(BF16)


def call(kernel, args, places, outs, mib, scratch=(), places_out=None, **static):
    spaces = {"s": pltpu.SMEM, "v": pltpu.VMEM, "a": pl.ANY}
    return pl.pallas_call(
        functools.partial(kernel, **static),
        out_shape=outs,
        in_specs=[pl.BlockSpec(memory_space=spaces[p]) for p in places],
        **({"out_specs": [pl.BlockSpec(memory_space=spaces[p]) for p in places_out]} if places_out else {}),
        scratch_shapes=scratch,
        compiler_params=pltpu.CompilerParams(vmem_limit_bytes=mib * MIB),
    )(*args)


def low_bit(o):
    return o & -o


def high_bit(o):
    return 1 << (o.bit_length() - 1)


def after(x, *needs):
    return lax.optimization_barrier((x, *needs))[0] if needs else x


def to_neighbours(first, second, bits):
    first_at, second_at = {0: first}, {0: second}
    for bit in bits:
        if bit == bits[0]:
            first_at[bit] = hop(first, "fsdp", bit)
        else:
            second_at[bit] = hop(second, "fsdp", bit)
    for bit in bits:
        if bit == bits[0]:
            second_at[bit] = hop(second, "fsdp", bit)
        else:
            first_at[bit] = hop(first, "fsdp", bit)
    return first_at, second_at


def to_others(first_at, second_at, routed, waits):
    for o in routed:
        first_at[o] = hop(after(first_at[o ^ high_bit(o)], *waits[0]), "fsdp", high_bit(o))
        second_at[o] = hop(after(second_at[o ^ low_bit(o)], *waits[1]), "fsdp", low_bit(o))


def per_device(tokens, out_grad, expert_ids, gate_probs, w_gate, w_up, w_down):
    tok, model = tokens.shape
    local, _, hidden = w_gate.shape
    n_f, n_e = lax.axis_size("fsdp"), lax.axis_size("ep")
    rows = n_e * MOST
    n = n_f // 2
    bits = [1 << i for i in range(1, n_f.bit_length() - 1)]
    routed = [o for o in range(2, n_f, 2) if o != low_bit(o)]
    shape = jax.ShapeDtypeStruct

    piece = shape((local + local // 2, hidden), BF16)
    pieces = call(
        split_kernel, (w_gate[:, 0], w_up[:, 0], w_down[:, 0]), "aaa", [piece] * 2, 8, [pltpu.SemaphoreType.DMA((4,))], places_out="aa"
    )
    weights = to_neighbours(*pieces, bits)

    pos = jnp.stack([lax.axis_index("fsdp"), lax.axis_index("ep")]).astype(jnp.int32)
    ids, gates = expert_ids.T, gate_probs.T
    *sends, select = call(
        prep_kernel,
        (pos, ids, gates, tokens, out_grad),
        "svvaa",
        [shape((2, 2 * MOST, model // 2), BF16)] * n_e + [shape((rows, tok), BF16)],
        16,
        [pltpu.VMEM(tokens.shape, BF16)] * 2 + [pltpu.SemaphoreType.DMA((2,))],
        n_f=n_f,
        n_e=n_e,
    )
    mine = [sends[0]] + [None] * (n_e - 1)
    early = [(), (weights[0][bits[0]],), (weights[1][bits[-1]],)]
    for turn, k in enumerate(range(n_e - 1, 0, -1)):
        mine[k] = hop(after(sends[k], *(early[turn] if turn < 3 else (mine[k + 3],))), "ep", k)
    to_others(*weights, routed, ((mine[-1],), (mine[1],)))
    weights = [[w[o] for o in range(0, n_f, 2)] for w in weights]
    other = [hop(m, "fsdp", 1) for m in mine]
    both = (*mine, *other)

    packed = call(
        pack_kernel, both, "v" * 2 * n_e, [shape((2, 2 * rows, local), BF16)] * (n - 1), 16, n_e=n_e
    )
    got = [hop(p, "fsdp", 2 * i + 2) for i, p in enumerate(packed)]

    def forward(entries, carried):
        pieces = [w[i] for w in weights for i in entries]
        size = len(entries) * local
        return call(
            forward_kernel,
            (*both, *carried, *pieces),
            "v" * (2 * n_e + len(carried)) + "a" * len(pieces),
            [shape((rows, 3 * hidden), F32), shape((rows, 3 * hidden), BF16)]
            if carried
            else [shape((2 * rows, 3 * hidden), F32)],
            24,
            [pltpu.VMEM((size, hidden), BF16)] * 3 + [pltpu.SemaphoreType.DMA((4 * len(entries),))],
            n_e=n_e,
            entries=entries,
            carried=bool(carried),
        )

    late = [o // 2 for o in routed]
    own, theirs = forward(late, forward([i for i in range(n) if i not in late], ()))
    first, second, pick = call(
        delta_kernel,
        (own, hop(theirs, "fsdp", 1)),
        "vv",
        [shape((rows // 2, 3 * hidden), BF16)] * 2 + [shape((rows, 128), BF16)],
        16,
    )

    firsts, seconds = to_neighbours(first, second, bits)
    first_other, second_other = hop(first, "fsdp", 1), hop(second, "fsdp", 1)

    backs = call(
        back_kernel,
        (first, second, first_other, second_other, pick, *weights[0], *weights[1]),
        "vvvvv" + "a" * 2 * n,
        [shape((2, MOST, model // 2 + 128), BF16)] * n_e,
        16,
        [pltpu.VMEM((n, local, hidden), BF16)] * 2 + [pltpu.SemaphoreType.DMA((2 * n,))],
        n=n,
        n_e=n_e,
    )
    back = [backs[0]] + [None] * (n_e - 1)
    early = [(), (firsts[bits[0]],), (seconds[bits[-1]],)]
    for turn, k in enumerate(range(n_e - 1, 0, -1)):
        back[k] = hop(after(backs[k], *(early[turn] if turn < 3 else (back[k + 3],))), "ep", k)
    to_others(firsts, seconds, routed, ((back[-1],), (back[1],)))
    backs = (*back, *(hop(b, "fsdp", 1) for b in back))
    in_grad, gate_grad = call(
        final_kernel,
        (pos, ids, gates, select, *backs),
        "svvv" + "v" * 2 * n_e,
        [shape((tok, model), BF16), shape(ids.shape, BF16)],
        16,
        n_f=n_f,
        n_e=n_e,
    )

    firsts_other, seconds_other = {0: first_other}, {0: second_other}
    for o in bits + routed:
        firsts_other[o], seconds_other[o] = hop(firsts[o], "fsdp", 1), hop(seconds[o], "fsdp", 1)

    def weight_sums(entries, carried):
        far = [got[i - 1] for i in entries if i]
        deltas = [at[2 * i] for i in entries for at in (firsts, seconds, firsts_other, seconds_other)]
        size = 2 * rows * len(entries)
        near = both if 0 in entries else ()
        return call(
            weight_kernel,
            (*near, *carried, *far, *deltas),
            "v" * (len(near) + len(carried)) + "a" * (len(far) + len(deltas)),
            [shape((local, hidden), BF16)] * 3 if carried else [shape((local, 3 * hidden), F32)],
            24,
            [pltpu.VMEM((size, local), BF16)] * 2
            + [pltpu.VMEM((size, 3 * hidden), BF16), pltpu.SemaphoreType.DMA((4 * len(far) + len(deltas),))],
            n_e=n_e,
            entries=entries,
            carried=bool(carried),
        )

    grads = weight_sums(late, weight_sums([i for i in range(n) if i not in late], ()))
    return (in_grad, gate_grad.T, *(g[:, None] for g in grads))


def solution(mesh):
    tok = P(("fsdp", "ep"), None)
    weight = P("fsdp", "ep", None)
    return jax.shard_map(
        per_device,
        mesh=mesh,
        in_specs=(tok, tok, tok, tok, weight, weight, weight),
        out_specs=(tok, tok, weight, weight, weight),
        check_vma=False,
    )
```

time: 128 us -> 110 us (0.86)
  waiting for transfers between devices: 70.3 us -> 42.7 us
  Pallas kernels: 10.6 us -> 18.9 us
  local copies, waits for them, and re-layouts: 4.13 us -> 6.82 us
  starting transfers between devices: 41.6 us -> 40.3 us
    ppermute x55 -> x38, waiting for transfers between devices: 70.3 us -> 42.7 us  [hop(): lax.ppermute(x, axis, [(i, i ^ offset) for i in range(lax.axis_size(axis))])]
    pallas_call x7 -> x10, Pallas kernels: 10.6 us -> 18.9 us  [call(): pl.pallas_call(functools.partial(kernel, **static), out_shape=outs, in_sp...]
    unnamed x12 -> x18, local copies, waits for them, and re-layouts: 3.08 us -> 6.82 us
    ppermute x55 -> x38, starting transfers between devices: 41.6 us -> 40.3 us  [hop(): lax.ppermute(x, axis, [(i, i ^ offset) for i in range(lax.axis_size(axis))])]
  transfers between devices with their start and end apart: 55 -> 38, of which waited for: 20 -> 13; matrix products, arithmetic and copies ran while one was open for 0% -> 0% of each run, Pallas kernels for 6% -> 13%
where the time goes in v2:
time: 110 us; the launch traced here: 109 us
  waiting for transfers between devices  42.7 us (39%)
  starting transfers between devices  40.3 us (37%)
  Pallas kernels  18.9 us (17%)
  local copies, waits for them, and re-layouts  6.82 us (6%)
    ppermute x38, waiting for transfers between devices, hop(): lax.ppermute(x, axis, [(i, i ^ offset) for i in range(lax.axis_size(axis))])  42.7 us
    ppermute x38, starting transfers between devices, hop(): lax.ppermute(x, axis, [(i, i ^ offset) for i in range(lax.axis_size(axis))])  40.3 us
    pallas_call x10, Pallas kernels, call(): pl.pallas_call(functools.partial(kernel, **static), out_shape=outs, in_sp...  18.9 us
    unnamed x18, local copies, waits for them, and re-layouts  6.82 us
  transfers between devices with their start and end apart: 38, of which 13 were waited for; matrix products, arithmetic and copies ran while one was open for 0% of the time, Pallas kernels for 13%

profile of v2, /device:TPU:0, one launch (start us, length us, event | category | flops | bytes accessed | tf_op | source)
XLA Modules:
  0.0 109.5 jit_solution(50079352373849063)
XLA Ops:
  4.5 3.0 %collective-permute-start = (bf16[384,768]{1,0:T(8,128)(2,1)S(1)}, bf16[384,768]{1,0:T(8,128)(2,1)S(1)}, u32[]{:S(2)}, u32[]{:S(2)}) collective-permute-start(bf16[384,768]{1,0:T(8,128)(2,1)S(1)} %get-tuple-element.40.refs_11_.refs_4_), channel_id=1, source_target_pairs={{0,16},{4,20},{8,24},{12,28},{16,0},{20,4},{24,8},{28,12},{1,17},{... | collective-permute-start | bytes 1769480 | tf_op jit(solution)/shard_map/ppermute | solution.py:29
  14.3 3.7 %collective-permute-start.4 = (bf16[2,64,1024]{2,1,0:T(8,128)(2,1)S(1)}, bf16[2,64,1024]{2,1,0:T(8,128)(2,1)S(1)}, u32[]{:S(2)}, u32[]{:S(2)}) collective-permute-start(bf16[2,64,1024]{2,1,0:T(8,128)(2,1)S(1)} %get-tuple-element.45), channel_id=1, source_target_pairs={{0,3},{1,2},{2,1},{3,0},{4,7},{5,6},{6,5},{7,4},{8,11},{9,10},{10,... | collective-permute-start | bytes 786440 | tf_op jit(solution)/shard_map/ppermute | solution.py:29
  18.0 2.9 %collective-permute-done.refs_13_.refs_6_ = bf16[384,768]{1,0:T(8,128)(2,1)S(1)} collective-permute-done((bf16[384,768]{1,0:T(8,128)(2,1)S(1)}, bf16[384,768]{1,0:T(8,128)(2,1)S(1)}, u32[]{:S(2)}, u32[]{:S(2)}) %collective-permute-start) | collective-permute-done | bytes 589856 | tf_op jit(solution)/shard_map/ppermute | solution.py:29
  20.9 1.8 %collective-permute-start.1 = (bf16[2,64,1024]{2,1,0:T(8,128)(2,1)S(1)}, bf16[2,64,1024]{2,1,0:T(8,128)(2,1)S(1)}, u32[]{:S(2)}, u32[]{:S(2)}) collective-permute-start(bf16[2,64,1024]{2,1,0:T(8,128)(2,1)S(1)} %get-tuple-element.41), channel_id=1, source_target_pairs={{0,1},{1,0},{2,3},{3,2},{4,5},{5,4},{6,7},{7,6},{8,9},{9,8},{10,11... | collective-permute-start | bytes 786440 | tf_op jit(solution)/shard_map/ppermute | solution.py:29
  22.7 1.5 %collective-permute-start.9 = (bf16[384,768]{1,0:T(8,128)(2,1)S(1)}, bf16[384,768]{1,0:T(8,128)(2,1)S(1)}, u32[]{:S(2)}, u32[]{:S(2)}) collective-permute-start(bf16[384,768]{1,0:T(8,128)(2,1)S(1)} %get-tuple-element.43.refs_8_.refs_0_), channel_id=1, source_target_pairs={{0,16},{4,20},{8,24},{12,28},{16,0},{20,4},{24,8},{28,12},{1,17},{... | collective-permute-start | bytes 1769480 | tf_op jit(solution)/shard_map/ppermute | solution.py:29
  26.2 3.2 %collective-permute-done.1.refs_1_ = bf16[2,64,1024]{2,1,0:T(8,128)(2,1)S(1)} collective-permute-done((bf16[2,64,1024]{2,1,0:T(8,128)(2,1)S(1)}, bf16[2,64,1024]{2,1,0:T(8,128)(2,1)S(1)}, u32[]{:S(2)}, u32[]{:S(2)}) %collective-permute-start.1) | collective-permute-done | bytes 262176 | tf_op jit(solution)/shard_map/ppermute | solution.py:29
  31.3 2.6 %collective-permute-start.3 = (bf16[2,64,1024]{2,1,0:T(8,128)(2,1)S(1)}, bf16[2,64,1024]{2,1,0:T(8,128)(2,1)S(1)}, u32[]{:S(2)}, u32[]{:S(2)}) collective-permute-start(bf16[2,64,1024]{2,1,0:T(8,128)(2,1)S(1)} %get-tuple-element.44), channel_id=1, source_target_pairs={{0,2},{1,3},{2,0},{3,1},{4,6},{5,7},{6,4},{7,5},{8,10},{9,11},{10,... | collective-permute-start | bytes 786440 | tf_op jit(solution)/shard_map/ppermute | solution.py:29
  33.9 5.1 %collective-permute-done.9.refs_10_.refs_2_ = bf16[384,768]{1,0:T(8,128)(2,1)S(1)} collective-permute-done((bf16[384,768]{1,0:T(8,128)(2,1)S(1)}, bf16[384,768]{1,0:T(8,128)(2,1)S(1)}, u32[]{:S(2)}, u32[]{:S(2)}) %collective-permute-start.9) | collective-permute-done | bytes 589856 | tf_op jit(solution)/shard_map/ppermute | solution.py:29
  39.0 5.4 %collective-permute-done.3.refs_2_ = bf16[2,64,1024]{2,1,0:T(8,128)(2,1)S(1)} collective-permute-done((bf16[2,64,1024]{2,1,0:T(8,128)(2,1)S(1)}, bf16[2,64,1024]{2,1,0:T(8,128)(2,1)S(1)}, u32[]{:S(2)}, u32[]{:S(2)}) %collective-permute-start.3) | collective-permute-done | bytes 262176 | tf_op jit(solution)/shard_map/ppermute | solution.py:29
  44.4 1.5 %collective-permute-done.7.refs_6_ = bf16[2,64,1024]{2,1,0:T(8,128)(2,1)S(1)} collective-permute-done((bf16[2,64,1024]{2,1,0:T(8,128)(2,1)S(1)}, bf16[2,64,1024]{2,1,0:T(8,128)(2,1)S(1)}, u32[]{:S(2)}, u32[]{:S(2)}) %collective-permute-start.7) | collective-permute-done | bytes 262176 | tf_op jit(solution)/shard_map/ppermute | solution.py:29
  45.9 3.9 %shard_map.112.refs_8_ = f32[256,2304]{1,0:T(8,128)S(1)} custom-call(bf16[2,64,1024]{2,1,0:T(8,128)(2,1)S(1)} %get-tuple-element.38.refs_0_, bf16[2,64,1024]{2,1,0:T(8,128)(2,1)S(1)} %collective-permute-done.1.refs_1_, bf16[2,64,1024]{2,1,0:T(8,128)(2,1)S(1)} %collective-permute-done.3.refs_2_, bf16[2,64,1024]{2,1,0:T(8,128)(2,1)S(1)} %collective-permute-done.4.refs_3_, ...), custom_call_target="tpu_custom_call" | custom-call | tf_op jit(solution)/shard_map/pallas_call | solution.py:266
  49.9 2.8 %collective-permute-done.12.refs_10_.refs_7_ = bf16[384,768]{1,0:T(8,128)(2,1)S(1)} collective-permute-done((bf16[384,768]{1,0:T(8,128)(2,1)S(1)}, bf16[384,768]{1,0:T(8,128)(2,1)S(1)}, u32[]{:S(2)}, u32[]{:S(2)}) %collective-permute-start.12) | collective-permute-done | bytes 589856 | tf_op jit(solution)/shard_map/ppermute | solution.py:29
  54.2 2.0 %collective-permute-done.13.got = bf16[128,2304]{1,0:T(8,128)(2,1)S(1)} collective-permute-done((bf16[128,2304]{1,0:T(8,128)(2,1)S(1)}, bf16[128,2304]{1,0:T(8,128)(2,1)S(1)}, u32[]{:S(2)}, u32[]{:S(2)}) %collective-permute-start.13) | collective-permute-done | bytes 589856 | tf_op jit(solution)/shard_map/ppermute | solution.py:29
  57.8 1.6 %collective-permute-start.25 = (bf16[2,256,256]{2,1,0:T(8,128)(2,1)S(1)}, bf16[2,256,256]{2,1,0:T(8,128)(2,1)S(1)}, u32[]{:S(2)}, u32[]{:S(2)}) collective-permute-start(bf16[2,256,256]{2,1,0:T(8,128)(2,1)S(1)} %get-tuple-element.61), channel_id=1, source_target_pairs={{0,8},{4,12},{8,0},{12,4},{16,24},{20,28},{24,16},{28,20},{1,9},{5... | collective-permute-start | bytes 786440 | tf_op jit(solution)/shard_map/ppermute | solution.py:29
  62.9 4.0 %shard_map.115 = (bf16[2,32,1152]{2,1,0:T(8,128)(2,1)S(1)}, bf16[2,32,1152]{2,1,0:T(8,128)(2,1)S(1)}, bf16[2,32,1152]{2,1,0:T(8,128)(2,1)S(1)}, bf16[2,32,1152]{2,1,0:T(8,128)(2,1)S(1)}) custom-call(bf16[64,2304]{1,0:T(8,128)(2,1)S(1)} %get-tuple-element.50.first.refs_10_, bf16[64,2304]{1,0:T(8,128)(2,1)S(1)} %get-tuple-element.51.second.refs_11_, ...), custom_call_target="tpu_custom_call" | custom-call | tf_op jit(solution)/shard_map/pallas_call | solution.py:266
  67.6 4.8 %collective-permute-start.17 = (bf16[2,32,1152]{2,1,0:T(8,128)(2,1)S(1)}, bf16[2,32,1152]{2,1,0:T(8,128)(2,1)S(1)}, u32[]{:S(2)}, u32[]{:S(2)}) collective-permute-start(bf16[2,32,1152]{2,1,0:T(8,128)(2,1)S(1)} %get-tuple-element.55), channel_id=1, source_target_pairs={{0,1},{1,0},{2,3},{3,2},{4,5},{5,4},{6,7},{7,6},{8,9},{9,8},{10,11... | collective-permute-start | bytes 442376 | tf_op jit(solution)/shard_map/ppermute | solution.py:29
  72.7 4.3 %collective-permute-start.20 = (bf16[2,32,1152]{2,1,0:T(8,128)(2,1)S(1)}, bf16[2,32,1152]{2,1,0:T(8,128)(2,1)S(1)}, u32[]{:S(2)}, u32[]{:S(2)}) collective-permute-start(bf16[2,32,1152]{2,1,0:T(8,128)(2,1)S(1)} %get-tuple-element.58), channel_id=1, source_target_pairs={{0,3},{1,2},{2,1},{3,0},{4,7},{5,6},{6,5},{7,4},{8,11},{9,10},{10,... | collective-permute-start | bytes 442376 | tf_op jit(solution)/shard_map/ppermute | solution.py:29
  77.0 3.1 %collective-permute-start.19 = (bf16[2,32,1152]{2,1,0:T(8,128)(2,1)S(1)}, bf16[2,32,1152]{2,1,0:T(8,128)(2,1)S(1)}, u32[]{:S(2)}, u32[]{:S(2)}) collective-permute-start(bf16[2,32,1152]{2,1,0:T(8,128)(2,1)S(1)} %get-tuple-element.57), channel_id=1, source_target_pairs={{0,2},{1,3},{2,0},{3,1},{4,6},{5,7},{6,4},{7,5},{8,10},{9,11},{10,... | collective-permute-start | bytes 442376 | tf_op jit(solution)/shard_map/ppermute | solution.py:29
  82.3 7.5 %collective-permute-done.19.refs_2_ = bf16[2,32,1152]{2,1,0:T(8,128)(2,1)S(1)} collective-permute-done((bf16[2,32,1152]{2,1,0:T(8,128)(2,1)S(1)}, bf16[2,32,1152]{2,1,0:T(8,128)(2,1)S(1)}, u32[]{:S(2)}, u32[]{:S(2)}) %collective-permute-start.19) | collective-permute-done | bytes 147488 | tf_op jit(solution)/shard_map/ppermute | solution.py:29
  91.5 6.4 %collective-permute-done.35.refs_3_ = bf16[64,2304]{1,0:T(8,128)(2,1)S(1)} collective-permute-done((bf16[64,2304]{1,0:T(8,128)(2,1)S(1)}, bf16[64,2304]{1,0:T(8,128)(2,1)S(1)}, u32[]{:S(2)}, u32[]{:S(2)}) %collective-permute-start.35) | collective-permute-done | bytes 294944 | tf_op jit(solution)/shard_map/ppermute | solution.py:29
  98.6 2.8 %shard_map.118.refs_0_ = f32[256,2304]{1,0:T(8,128)S(1)} custom-call(bf16[2,64,1024]{2,1,0:T(8,128)(2,1)S(1)} %get-tuple-element.38.refs_0_, bf16[2,64,1024]{2,1,0:T(8,128)(2,1)S(1)} %collective-permute-done.1.refs_1_, bf16[2,64,1024]{2,1,0:T(8,128)(2,1)S(1)} %collective-permute-done.3.refs_2_, bf16[2,64,1024]{2,1,0:T(8,128)(2,1)S(1)} %collective-permute-done.4.refs_3_, ...), custom_call_target="tpu_custom_call" | custom-call | tf_op jit(solution)/shard_map/pallas_call | solution.py:266
  101.4 2.0 %shard_map.116 = (bf16[256,2048]{1,0:T(8,128)(2,1)}, bf16[8,256]{1,0:T(8,128)(2,1)}) custom-call(s32[2]{0:T(128)S(1)} %pad_add_fusion.pos, s32[8,256]{1,0:T(8,128)S(1)} %bitcast.15, bf16[8,256]{1,0:T(8,128)(2,1)S(1)} %bitcast.17, bf16[128,256]{1,0:T(8,128)(2,1)S(1)} %get-tuple-element.37.select, bf16[2,32,1152]{2,1,0:T(8,128)(2,1)S(1)} %get-tuple-element.53.refs_0_, ...), custom_call_target="tpu_custom_call" | custom-call | tf_op jit(solution)/shard_map/pallas_call | solution.py:266
  103.4 4.1 %collective-permute-done.33.refs_1_ = bf16[2,256,256]{2,1,0:T(8,128)(2,1)S(1)} collective-permute-done((bf16[2,256,256]{2,1,0:T(8,128)(2,1)S(1)}, bf16[2,256,256]{2,1,0:T(8,128)(2,1)S(1)}, u32[]{:S(2)}, u32[]{:S(2)}) %collective-permute-start.33) | collective-permute-done | bytes 262176 | tf_op jit(solution)/shard_map/ppermute | solution.py:29
  107.5 2.0 %shard_map.119 = (bf16[256,768]{1,0:T(8,128)(2,1)}, bf16[256,768]{1,0:T(8,128)(2,1)}, bf16[256,768]{1,0:T(8,128)(2,1)}) custom-call(f32[256,2304]{1,0:T(8,128)S(1)} %shard_map.118.refs_0_, bf16[2,256,256]{2,1,0:T(8,128)(2,1)S(1)} %collective-permute-done.33.refs_1_, bf16[64,2304]{1,0:T(8,128)(2,1)S(1)} %collective-permute-done.34.refs_2_, ...), custom_call_target="tpu_custom_call" | custom-call | tf_op jit(solution)/shard_map/pallas_call | solution.py:266
  (81 shorter events, 26.8 us)
Async XLA Ops:
  4.5 16.4 %collective-permute-start = (bf16[384,768]{1,0:T(8,128)(2,1)S(1)}, bf16[384,768]{1,0:T(8,128)(2,1)S(1)}, u32[]{:S(2)}, u32[]{:S(2)}) collective-permute-start(bf16[384,768]{1,0:T(8,128)(2,1)S(1)} %get-tuple-element.40.refs_11_.refs_4_), channel_id=1, source_target_pairs={{0,16},{4,20},{8,24},{12,28},{16,0},{20,4},{24,8},{28,12},{1,17},{... | collective-permute-start | bytes 1769480 | tf_op jit(solution)/shard_map/ppermute | solution.py:29
  7.6 17.2 %collective-permute-start.2 = (bf16[384,768]{1,0:T(8,128)(2,1)S(1)}, bf16[384,768]{1,0:T(8,128)(2,1)S(1)}, u32[]{:S(2)}, u32[]{:S(2)}) collective-permute-start(bf16[384,768]{1,0:T(8,128)(2,1)S(1)} %get-tuple-element.43.refs_8_.refs_0_), channel_id=1, source_target_pairs={{0,8},{4,12},{8,0},{12,4},{16,24},{20,28},{24,16},{28,20},{1,9},{5... | collective-permute-start | bytes 1769480 | tf_op jit(solution)/shard_map/ppermute | solution.py:29
  14.3 9.9 %collective-permute-start.4 = (bf16[2,64,1024]{2,1,0:T(8,128)(2,1)S(1)}, bf16[2,64,1024]{2,1,0:T(8,128)(2,1)S(1)}, u32[]{:S(2)}, u32[]{:S(2)}) collective-permute-start(bf16[2,64,1024]{2,1,0:T(8,128)(2,1)S(1)} %get-tuple-element.45), channel_id=1, source_target_pairs={{0,3},{1,2},{2,1},{3,0},{4,7},{5,6},{6,5},{7,4},{8,11},{9,10},{10,... | collective-permute-start | bytes 786440 | tf_op jit(solution)/shard_map/ppermute | solution.py:29
  20.9 8.6 %collective-permute-start.1 = (bf16[2,64,1024]{2,1,0:T(8,128)(2,1)S(1)}, bf16[2,64,1024]{2,1,0:T(8,128)(2,1)S(1)}, u32[]{:S(2)}, u32[]{:S(2)}) collective-permute-start(bf16[2,64,1024]{2,1,0:T(8,128)(2,1)S(1)} %get-tuple-element.41), channel_id=1, source_target_pairs={{0,1},{1,0},{2,3},{3,2},{4,5},{5,4},{6,7},{7,6},{8,9},{9,8},{10,11... | collective-permute-start | bytes 786440 | tf_op jit(solution)/shard_map/ppermute | solution.py:29
  22.7 16.3 %collective-permute-start.9 = (bf16[384,768]{1,0:T(8,128)(2,1)S(1)}, bf16[384,768]{1,0:T(8,128)(2,1)S(1)}, u32[]{:S(2)}, u32[]{:S(2)}) collective-permute-start(bf16[384,768]{1,0:T(8,128)(2,1)S(1)} %get-tuple-element.43.refs_8_.refs_0_), channel_id=1, source_target_pairs={{0,16},{4,20},{8,24},{12,28},{16,0},{20,4},{24,8},{28,12},{1,17},{... | collective-permute-start | bytes 1769480 | tf_op jit(solution)/shard_map/ppermute | solution.py:29
  24.7 19.7 %collective-permute-start.10 = (bf16[384,768]{1,0:T(8,128)(2,1)S(1)}, bf16[384,768]{1,0:T(8,128)(2,1)S(1)}, u32[]{:S(2)}, u32[]{:S(2)}) collective-permute-start(bf16[384,768]{1,0:T(8,128)(2,1)S(1)} %get-tuple-element.40.refs_11_.refs_4_), channel_id=1, source_target_pairs={{0,8},{4,12},{8,0},{12,4},{16,24},{20,28},{24,16},{28,20},{1,9},{5... | collective-permute-start | bytes 1769480 | tf_op jit(solution)/shard_map/ppermute | solution.py:29
  29.5 20.4 %collective-permute-start.11 = (bf16[384,768]{1,0:T(8,128)(2,1)S(1)}, bf16[384,768]{1,0:T(8,128)(2,1)S(1)}, u32[]{:S(2)}, u32[]{:S(2)}) collective-permute-start(bf16[384,768]{1,0:T(8,128)(2,1)S(1)} %collective-permute-done.2.refs_9_.refs_1_), channel_id=1, source_target_pairs={{0,16},{4,20},{8,24},{12,28},{16,0},{20,4},{24,8},{28,12},{1,17},{... | collective-permute-start | bytes 1769480 | tf_op jit(solution)/shard_map/ppermute | solution.py:29
  30.0 22.7 %collective-permute-start.12 = (bf16[384,768]{1,0:T(8,128)(2,1)S(1)}, bf16[384,768]{1,0:T(8,128)(2,1)S(1)}, u32[]{:S(2)}, u32[]{:S(2)}) collective-permute-start(bf16[384,768]{1,0:T(8,128)(2,1)S(1)} %collective-permute-done.refs_13_.refs_6_), channel_id=1, source_target_pairs={{0,8},{4,12},{8,0},{12,4},{16,24},{20,28},{24,16},{28,20},{1,9},{5... | collective-permute-start | bytes 1769480 | tf_op jit(solution)/shard_map/ppermute | solution.py:29
  31.3 13.1 %collective-permute-start.3 = (bf16[2,64,1024]{2,1,0:T(8,128)(2,1)S(1)}, bf16[2,64,1024]{2,1,0:T(8,128)(2,1)S(1)}, u32[]{:S(2)}, u32[]{:S(2)}) collective-permute-start(bf16[2,64,1024]{2,1,0:T(8,128)(2,1)S(1)} %get-tuple-element.44), channel_id=1, source_target_pairs={{0,2},{1,3},{2,0},{3,1},{4,6},{5,7},{6,4},{7,5},{8,10},{9,11},{10,... | collective-permute-start | bytes 786440 | tf_op jit(solution)/shard_map/ppermute | solution.py:29
  57.2 9.9 %collective-permute-start.16 = (bf16[64,2304]{1,0:T(8,128)(2,1)S(1)}, bf16[64,2304]{1,0:T(8,128)(2,1)S(1)}, u32[]{:S(2)}, u32[]{:S(2)}) collective-permute-start(bf16[64,2304]{1,0:T(8,128)(2,1)S(1)} %get-tuple-element.51.second.refs_11_), channel_id=1, source_target_pairs={{0,16},{4,20},{8,24},{12,28},{16,0},{20,4},{24,8},{28,12},{1,17},{... | collective-permute-start | bytes 884744 | tf_op jit(solution)/shard_map/ppermute | solution.py:29
  57.8 9.8 %collective-permute-start.25 = (bf16[2,256,256]{2,1,0:T(8,128)(2,1)S(1)}, bf16[2,256,256]{2,1,0:T(8,128)(2,1)S(1)}, u32[]{:S(2)}, u32[]{:S(2)}) collective-permute-start(bf16[2,256,256]{2,1,0:T(8,128)(2,1)S(1)} %get-tuple-element.61), channel_id=1, source_target_pairs={{0,8},{4,12},{8,0},{12,4},{16,24},{20,28},{24,16},{28,20},{1,9},{5... | collective-permute-start | bytes 786440 | tf_op jit(solution)/shard_map/ppermute | solution.py:29
  59.4 13.3 %collective-permute-start.26 = (bf16[2,256,256]{2,1,0:T(8,128)(2,1)S(1)}, bf16[2,256,256]{2,1,0:T(8,128)(2,1)S(1)}, u32[]{:S(2)}, u32[]{:S(2)}) collective-permute-start(bf16[2,256,256]{2,1,0:T(8,128)(2,1)S(1)} %get-tuple-element.62), channel_id=1, source_target_pairs={{0,16},{4,20},{8,24},{12,28},{16,0},{20,4},{24,8},{28,12},{1,17},{... | collective-permute-start | bytes 786440 | tf_op jit(solution)/shard_map/ppermute | solution.py:29
  60.9 16.1 %collective-permute-start.18 = (bf16[64,2304]{1,0:T(8,128)(2,1)S(1)}, bf16[64,2304]{1,0:T(8,128)(2,1)S(1)}, u32[]{:S(2)}, u32[]{:S(2)}) collective-permute-start(bf16[64,2304]{1,0:T(8,128)(2,1)S(1)} %get-tuple-element.50.first.refs_10_), channel_id=1, source_target_pairs={{0,8},{4,12},{8,0},{12,4},{16,24},{20,28},{24,16},{28,20},{1,9},{5... | collective-permute-start | bytes 884744 | tf_op jit(solution)/shard_map/ppermute | solution.py:29
  61.4 19.7 %collective-permute-start.27 = (bf16[64,2304]{1,0:T(8,128)(2,1)S(1)}, bf16[64,2304]{1,0:T(8,128)(2,1)S(1)}, u32[]{:S(2)}, u32[]{:S(2)}) collective-permute-start(bf16[64,2304]{1,0:T(8,128)(2,1)S(1)} %get-tuple-element.51.second.refs_11_), channel_id=1, source_target_pairs={{0,8},{4,12},{8,0},{12,4},{16,24},{20,28},{24,16},{28,20},{1,9},{5... | collective-permute-start | bytes 884744 | tf_op jit(solution)/shard_map/ppermute | solution.py:29
  67.1 14.6 %collective-permute-start.30 = (bf16[64,2304]{1,0:T(8,128)(2,1)S(1)}, bf16[64,2304]{1,0:T(8,128)(2,1)S(1)}, u32[]{:S(2)}, u32[]{:S(2)}) collective-permute-start(bf16[64,2304]{1,0:T(8,128)(2,1)S(1)} %get-tuple-element.50.first.refs_10_), channel_id=1, source_target_pairs={{0,16},{4,20},{8,24},{12,28},{16,0},{20,4},{24,8},{28,12},{1,17},{... | collective-permute-start | bytes 884744 | tf_op jit(solution)/shard_map/ppermute | solution.py:29
  67.6 9.4 %collective-permute-start.17 = (bf16[2,32,1152]{2,1,0:T(8,128)(2,1)S(1)}, bf16[2,32,1152]{2,1,0:T(8,128)(2,1)S(1)}, u32[]{:S(2)}, u32[]{:S(2)}) collective-permute-start(bf16[2,32,1152]{2,1,0:T(8,128)(2,1)S(1)} %get-tuple-element.55), channel_id=1, source_target_pairs={{0,1},{1,0},{2,3},{3,2},{4,5},{5,4},{6,7},{7,6},{8,9},{9,8},{10,11... | collective-permute-start | bytes 442376 | tf_op jit(solution)/shard_map/ppermute | solution.py:29
  77.0 13.5 %collective-permute-start.28 = (bf16[64,2304]{1,0:T(8,128)(2,1)S(1)}, bf16[64,2304]{1,0:T(8,128)(2,1)S(1)}, u32[]{:S(2)}, u32[]{:S(2)}) collective-permute-start(bf16[64,2304]{1,0:T(8,128)(2,1)S(1)} %collective-permute-done.18.refs_14_), channel_id=1, source_target_pairs={{0,4},{4,0},{8,12},{12,8},{16,20},{20,16},{24,28},{28,24},{1,5},{5... | collective-permute-start | bytes 884744 | tf_op jit(solution)/shard_map/ppermute | solution.py:29
  77.0 12.8 %collective-permute-start.19 = (bf16[2,32,1152]{2,1,0:T(8,128)(2,1)S(1)}, bf16[2,32,1152]{2,1,0:T(8,128)(2,1)S(1)}, u32[]{:S(2)}, u32[]{:S(2)}) collective-permute-start(bf16[2,32,1152]{2,1,0:T(8,128)(2,1)S(1)} %get-tuple-element.57), channel_id=1, source_target_pairs={{0,2},{1,3},{2,0},{3,1},{4,6},{5,7},{6,4},{7,5},{8,10},{9,11},{10,... | collective-permute-start | bytes 442376 | tf_op jit(solution)/shard_map/ppermute | solution.py:29
  81.2 9.3 %collective-permute-start.21 = (bf16[2,32,1152]{2,1,0:T(8,128)(2,1)S(1)}, bf16[2,32,1152]{2,1,0:T(8,128)(2,1)S(1)}, u32[]{:S(2)}, u32[]{:S(2)}) collective-permute-start(bf16[2,32,1152]{2,1,0:T(8,128)(2,1)S(1)} %get-tuple-element.53.refs_0_), channel_id=1, source_target_pairs={{0,4},{4,0},{8,12},{12,8},{16,20},{20,16},{24,28},{28,24},{1,5},{5... | collective-permute-start | bytes 442376 | tf_op jit(solution)/shard_map/ppermute | solution.py:29
  81.2 9.8 %collective-permute-start.29 = (bf16[64,2304]{1,0:T(8,128)(2,1)S(1)}, bf16[64,2304]{1,0:T(8,128)(2,1)S(1)}, u32[]{:S(2)}, u32[]{:S(2)}) collective-permute-start(bf16[64,2304]{1,0:T(8,128)(2,1)S(1)} %collective-permute-done.27.refs_15_), channel_id=1, source_target_pairs={{0,4},{4,0},{8,12},{12,8},{16,20},{20,16},{24,28},{28,24},{1,5},{5... | collective-permute-start | bytes 884744 | tf_op jit(solution)/shard_map/ppermute | solution.py:29
  81.7 9.4 %collective-permute-start.34 = (bf16[64,2304]{1,0:T(8,128)(2,1)S(1)}, bf16[64,2304]{1,0:T(8,128)(2,1)S(1)}, u32[]{:S(2)}, u32[]{:S(2)}) collective-permute-start(bf16[64,2304]{1,0:T(8,128)(2,1)S(1)} %collective-permute-done.18.refs_14_), channel_id=1, source_target_pairs={{0,16},{4,20},{8,24},{12,28},{16,0},{20,4},{24,8},{28,12},{1,17},{... | collective-permute-start | bytes 884744 | tf_op jit(solution)/shard_map/ppermute | solution.py:29
  91.1 16.4 %collective-permute-start.36 = (bf16[64,2304]{1,0:T(8,128)(2,1)S(1)}, bf16[64,2304]{1,0:T(8,128)(2,1)S(1)}, u32[]{:S(2)}, u32[]{:S(2)}) collective-permute-start(bf16[64,2304]{1,0:T(8,128)(2,1)S(1)} %collective-permute-done.34.refs_2_), channel_id=1, source_target_pairs={{0,4},{4,0},{8,12},{12,8},{16,20},{20,16},{24,28},{28,24},{1,5},{5... | collective-permute-start | bytes 884744 | tf_op jit(solution)/shard_map/ppermute | solution.py:29
  97.9 9.6 %collective-permute-start.37 = (bf16[64,2304]{1,0:T(8,128)(2,1)S(1)}, bf16[64,2304]{1,0:T(8,128)(2,1)S(1)}, u32[]{:S(2)}, u32[]{:S(2)}) collective-permute-start(bf16[64,2304]{1,0:T(8,128)(2,1)S(1)} %collective-permute-done.35.refs_3_), channel_id=1, source_target_pairs={{0,4},{4,0},{8,12},{12,8},{16,20},{20,16},{24,28},{28,24},{1,5},{5... | collective-permute-start | bytes 884744 | tf_op jit(solution)/shard_map/ppermute | solution.py:29
  97.9 9.6 %collective-permute-start.33 = (bf16[2,256,256]{2,1,0:T(8,128)(2,1)S(1)}, bf16[2,256,256]{2,1,0:T(8,128)(2,1)S(1)}, u32[]{:S(2)}, u32[]{:S(2)}) collective-permute-start(bf16[2,256,256]{2,1,0:T(8,128)(2,1)S(1)} %get-tuple-element.63), channel_id=1, source_target_pairs={{0,24},{4,28},{8,16},{12,20},{16,8},{20,12},{24,0},{28,4},{1,25},{... | collective-permute-start | bytes 786440 | tf_op jit(solution)/shard_map/ppermute | solution.py:29
  (23 other events, 89.6 us)

commit v3 on v2

v3 whole, which is shorter than its diff:
```python
import functools
import itertools

import jax
import jax.numpy as jnp
from jax import lax
from jax.experimental import pallas as pl
from jax.experimental.pallas import tpu as pltpu
from jax.sharding import PartitionSpec as P

MOST = 32
F32 = jnp.float32
BF16 = jnp.bfloat16
MIB = 1024 * 1024
HINT = pl.CostEstimate(flops=5_000_000_000, bytes_accessed=15_000_000, transcendentals=0)


def mm(left, right):
    return lax.dot_general(left, right, (((1,), (0,)), ((), ())), preferred_element_type=F32)


def mm_lead(left, right):
    return lax.dot_general(left, right, (((0,), (0,)), ((), ())), preferred_element_type=F32)


def mm_trail(left, right):
    return lax.dot_general(left, right, (((1,), (1,)), ((), ())), preferred_element_type=F32)


def hop(x, axis, offset):
    return lax.ppermute(x, axis, [(i, i ^ offset) for i in range(lax.axis_size(axis))])


def flips(position, core, bits):
    return sum(2 << (bits - 1 - b if core else b) for b in range(bits) if position >> b & 1)


def mirror(position, bits):
    return flips(position, 1, bits) // 2


def slice_of(f, side, position, n_f):
    bits = n_f.bit_length() - 2
    even, odd = flips(position, 0, bits), flips(position, 1, bits)
    return f ^ side ^ (even + ((f ^ side) & 1) * (odd - even))


class Copies:
    def __init__(self, sems):
        self.sems, self.made, self.waited = sems, [], 0

    def start(self, source, target):
        self.made.append(pltpu.make_async_copy(source, target, self.sems.at[len(self.made)]))
        self.made[-1].start()

    def wait(self, count=None):
        for copy in self.made[self.waited : None if count is None else self.waited + count]:
            copy.wait()
            self.waited += 1


def stack_kernel(*refs):
    parts, (out, sems) = refs[:-2], refs[-2:]
    fetch = Copies(sems)
    size = parts[0].shape[0]
    for i, part in enumerate(parts):
        fetch.start(part, out.at[pl.ds(i * size, size)])
    fetch.wait()


def prep_kernel(pos, ids, gates, tokens_in, grads_in, *refs, n_f, n_e):
    sends, select = refs[:n_e], refs[n_e]
    tokens, grads, sems = refs[n_e + 1 :]
    fetch = [
        pltpu.make_async_copy(tokens_in, tokens, sems.at[0]),
        pltpu.make_async_copy(grads_in, grads, sems.at[1]),
    ]
    for copy in fetch:
        copy.start()
    f, e = pos[0], pos[1]
    tok = ids.shape[1]
    width = tokens.shape[1] // n_f
    rows = max(16, n_e)
    row = lax.broadcasted_iota(jnp.int32, (rows, tok), 0)
    chosen = []
    weight = []
    stacked = jnp.zeros((rows, tok), F32)
    for k in range(n_e):
        match = ids[...] == (e ^ k)
        chosen.append(jnp.max(jnp.where(match, 1.0, 0.0), axis=0, keepdims=True))
        weight.append(jnp.sum(jnp.where(match, gates[...].astype(F32), 0.0), axis=0, keepdims=True))
        stacked = jnp.where(row == k, chosen[k], stacked)
    before = lax.broadcasted_iota(jnp.int32, (tok, tok), 0) < lax.broadcasted_iota(jnp.int32, (tok, tok), 1)
    slot = mm(stacked.astype(BF16), jnp.where(before, 1.0, 0.0).astype(BF16))
    want = lax.broadcasted_iota(jnp.int32, (MOST, tok), 0).astype(F32)
    picks = []
    scaled = []
    for k in range(n_e):
        hit = jnp.where(want == slot[k : k + 1], chosen[k], 0.0)
        picks.append(hit)
        scaled.append(hit * weight[k])
    picks = jnp.concatenate(picks, axis=0).astype(BF16)
    scaled = jnp.concatenate(scaled, axis=0).astype(BF16)
    select[...] = picks
    for copy in fetch:
        copy.wait()
    for side, position in itertools.product(range(2), range(n_f // 2)):
        at = pl.ds(pl.multiple_of(slice_of(f, side, position, n_f) * width, width), width)
        here = slice(position * width, (position + 1) * width)
        x = mm(picks, tokens[:, at]).astype(BF16)
        q = mm(scaled, grads[:, at]).astype(BF16)
        for k in range(n_e):
            sends[k][side, :MOST, here] = x[k * MOST : (k + 1) * MOST]
            sends[k][side, MOST:, here] = q[k * MOST : (k + 1) * MOST]


def pack_kernel(*refs, n_e):
    sides = refs[:n_e], refs[n_e : 2 * n_e]
    outs = refs[2 * n_e :]
    width = outs[0].shape[2]
    rows = n_e * MOST
    for i, out in enumerate(outs):
        here = slice((i + 1) * width, (i + 2) * width)
        for side in range(2):
            for k in range(n_e):
                out[side, k * MOST : (k + 1) * MOST] = sides[side][k][side, :MOST, here]
                out[side, rows + k * MOST : rows + (k + 1) * MOST] = sides[side][k][side, MOST:, here]


def forward_kernel(*refs, n_e, entries, carried):
    sides = refs[:n_e], refs[n_e : 2 * n_e]
    refs = refs[2 * n_e :]
    if carried:
        total_in, refs = refs[0], refs[1:]
    count = len(entries)
    pieces, refs = refs[:count], refs[count:]
    outs, (gate, up, down, sems) = refs[:-4], refs[-4:]
    hidden = gate.shape[1]
    width = gate.shape[0] // count
    fetch = Copies(sems)
    for at, whole in enumerate((gate, up, down)):
        for i in range(count):
            fetch.start(pieces[i].at[pl.ds(at * width, width)], whole.at[pl.ds(i * width, width)])

    def rows_of(part):
        return jnp.concatenate(
            [
                jnp.concatenate([sides[side][k][side, part, i * width : (i + 1) * width] for i in entries], axis=1)
                for side in range(2)
                for k in range(n_e)
            ],
            axis=0,
        )

    x, q = rows_of(slice(0, MOST)), rows_of(slice(MOST, 2 * MOST))
    rows = n_e * MOST
    for at, (left, right) in enumerate(((x, gate), (x, up), (q, down))):
        fetch.wait(count)
        here = slice(at * hidden, (at + 1) * hidden)
        part = mm(left, right[...])
        if carried:
            part = part + total_in[:, here]
            outs[0][:, here] = part[:rows]
            outs[1][:, here] = part[rows:].astype(BF16)
        else:
            outs[0][:, here] = part


def delta_kernel(own, got, deltas, pick_out):
    hidden = own.shape[1] // 3
    a, b, r = (
        own[:, at * hidden : (at + 1) * hidden] + got[:, at * hidden : (at + 1) * hidden].astype(F32) for at in range(3)
    )
    s = jax.nn.sigmoid(a)
    silu = a * s
    h = (silu * b).astype(BF16)
    pick = jnp.sum(h.astype(F32) * r, axis=1, keepdims=True)
    deltas[:, :hidden] = (r * b * s * (1.0 + a * (1.0 - s))).astype(BF16)
    deltas[:, hidden : 2 * hidden] = (r * silu).astype(BF16)
    deltas[:, 2 * hidden :] = h
    coarse = pick.astype(BF16)
    fine = (pick - coarse.astype(F32)).astype(BF16)
    wide = pick_out.shape
    lane = lax.broadcasted_iota(jnp.int32, wide, 1)
    pick_out[...] = jnp.where(
        lane < wide[1] // 2, jnp.broadcast_to(coarse.astype(F32), wide), jnp.broadcast_to(fine.astype(F32), wide)
    ).astype(BF16)


def back_kernel(deltas, deltas_other, pick, *refs, n, n_e):
    pieces, outs, (gate, up, sems) = refs[:n], refs[n : n + n_e], refs[n + n_e :]
    hidden = gate.shape[2]
    width = gate.shape[1]
    fetch = Copies(sems)
    for i in range(n):
        fetch.start(pieces[i].at[:width], gate.at[i])
        fetch.start(pieces[i].at[pl.ds(width, width)], up.at[i])
    da = jnp.concatenate([deltas[:, :hidden], deltas_other[:, :hidden]], axis=0)
    du = jnp.concatenate([deltas[:, hidden : 2 * hidden], deltas_other[:, hidden : 2 * hidden]], axis=0)
    for i in range(n):
        fetch.wait(2)
        c = (mm_trail(da, gate[i]) + mm_trail(du, up[i])).astype(BF16)
        here = slice(i * width, (i + 1) * width)
        for side in range(2):
            for k in range(n_e):
                at = (side * n_e + k) * MOST
                outs[k][side, :, here] = c[at : at + MOST]
    for side in range(2):
        for k in range(n_e):
            outs[k][side, :, n * width :] = pick[k * MOST : (k + 1) * MOST]


def weight_kernel(*refs, n_e, entries, carried):
    if 0 in entries:
        sides, refs = (refs[:n_e], refs[n_e : 2 * n_e]), refs[2 * n_e :]
    if carried:
        total_in, refs = refs[0], refs[1:]
    far = [i for i in entries if i]
    got, deltas = refs[: len(far)], refs[len(far) : len(far) + 2 * len(entries)]
    outs, (x, q, d, sems) = refs[len(far) + 2 * len(entries) : -4], refs[-4:]
    width, hidden = x.shape[1], d.shape[1] // 3
    rows = n_e * MOST
    fetch = Copies(sems)
    for i, p in enumerate(deltas):
        fetch.start(p, d.at[pl.ds(i * rows, rows)])
    for place, i in enumerate(entries):
        if i == 0:
            continue
        for side in range(2):
            at = pl.ds((2 * place + side) * rows, rows)
            fetch.start(got[far.index(i)].at[side, :rows], x.at[at])
            fetch.start(got[far.index(i)].at[side, rows:], q.at[at])
    if 0 in entries:
        for side in range(2):
            for k in range(n_e):
                at = slice(side * rows + k * MOST, side * rows + (k + 1) * MOST)
                x[at] = sides[side][k][side, :MOST, :width]
                q[at] = sides[side][k][side, MOST:, :width]
    fetch.wait()
    for at, left in enumerate((x, x, q)):
        here = slice(at * hidden, (at + 1) * hidden)
        part = mm_lead(left[...], d[:, here])
        if carried:
            outs[at][...] = (total_in[:, here] + part).astype(BF16)
        else:
            outs[0][:, here] = part


def final_kernel(pos, ids, gates, select, *refs, n_f, n_e):
    mine, other, (in_grad, gate_grad) = refs[:n_e], refs[n_e : 2 * n_e], refs[2 * n_e :]
    f, e = pos[0], pos[1]
    width = in_grad.shape[1] // n_f
    total = n_f // 2 * width
    for side, position in itertools.product(range(2), range(n_f // 2)):
        at = pl.ds(pl.multiple_of(slice_of(f, side, position, n_f) * width, width), width)
        here = slice(position * width, (position + 1) * width)
        c = jnp.concatenate([(mine, other)[side][k][side, :, here] for k in range(n_e)], axis=0)
        in_grad[:, at] = mm_lead(select[...], c).astype(BF16)
    half = (mine[0].shape[2] - total) // 2
    found = jnp.zeros(ids.shape, F32)
    for k in range(n_e):
        pick = mine[k][0, :, total : total + 1].astype(F32) + mine[k][0, :, total + half : total + half + 1].astype(F32)
        hit = select[k * MOST : (k + 1) * MOST].astype(F32)
        value = jnp.sum(hit * pick, axis=0, keepdims=True)
        found = found + jnp.where(ids[...] == (e ^ k), value, 0.0)
    gate_grad[...] = (found / gates[...].astype(F32)).astype(BF16)


def call(kernel, args, places, outs, mib, scratch=(), places_out=None, hint=False, **static):
    args = [pltpu.with_memory_space_constraint(x, pltpu.HBM) if p == "h" else x for x, p in zip(args, places)]
    spaces = {"s": pltpu.SMEM, "v": pltpu.VMEM, "a": pl.ANY, "h": pltpu.HBM}
    return pl.pallas_call(
        functools.partial(kernel, **static),
        out_shape=outs,
        in_specs=[pl.BlockSpec(memory_space=spaces[p]) for p in places],
        **({"out_specs": pl.BlockSpec(memory_space=spaces[places_out])} if places_out else {}),
        scratch_shapes=scratch,
        **({"cost_estimate": HINT} if hint else {}),
        compiler_params=pltpu.CompilerParams(vmem_limit_bytes=mib * MIB),
    )(*args)


def after(x, *needs):
    return lax.optimization_barrier((x, *needs))[0] if needs else x


def to(x, position):
    n_f = lax.axis_size("fsdp")
    bits = n_f.bit_length() - 2
    return lax.ppermute(x, "fsdp", [(i, i ^ flips(position, i & 1, bits)) for i in range(n_f)])


def top(position):
    return 1 << (position.bit_length() - 1)


def per_device(tokens, out_grad, expert_ids, gate_probs, w_gate, w_up, w_down):
    tok, model = tokens.shape
    local, _, hidden = w_gate.shape
    n_f, n_e = lax.axis_size("fsdp"), lax.axis_size("ep")
    rows = n_e * MOST
    n = n_f // 2
    bits = n.bit_length() - 1
    near = [1 << b for b in range(bits)]
    late = [p for p in range(1, n) if p not in near]
    early = [0, *near]
    shape = jax.ShapeDtypeStruct

    weights = {
        0: call(
            stack_kernel,
            (w_gate[:, 0], w_up[:, 0], w_down[:, 0]),
            "hhh",
            shape((3 * local, hidden), BF16),
            8,
            [pltpu.SemaphoreType.DMA((3,))],
            places_out="a",
        )
    }
    for p in near:
        weights[p] = to(weights[0], p)

    pos = jnp.stack([lax.axis_index("fsdp"), lax.axis_index("ep")]).astype(jnp.int32)
    ids, gates = expert_ids.T, gate_probs.T
    *sends, select = call(
        prep_kernel,
        (pos, ids, gates, tokens, out_grad),
        "svvhh",
        [shape((2, 2 * MOST, model // 2), BF16)] * n_e + [shape((rows, tok), BF16)],
        16,
        [pltpu.VMEM(tokens.shape, BF16)] * 2 + [pltpu.SemaphoreType.DMA((2,))],
        n_f=n_f,
        n_e=n_e,
    )
    mine = [sends[0]] + [hop(sends[k], "ep", k) for k in range(1, n_e)]
    other = [hop(after(mine[0], weights[near[-1]]), "fsdp", 1)] + [hop(m, "fsdp", 1) for m in mine[1:]]
    both = (*mine, *other)
    for p in late:
        weights[p] = to(after(weights[p ^ top(p)], mine[1]), top(p))

    packed = call(pack_kernel, both, "v" * 2 * n_e, [shape((2, 2 * rows, local), BF16)] * (n - 1), 16, hint=True, n_e=n_e)
    got = [to(x, i + 1) for i, x in enumerate(packed)]

    def forward(entries, carried):
        pieces = [weights[p] for p in entries]
        size = len(entries) * local
        return call(
            forward_kernel,
            (*both, *carried, *pieces),
            "v" * (2 * n_e + len(carried)) + "a" * len(pieces),
            [shape((rows, 3 * hidden), F32), shape((rows, 3 * hidden), BF16)]
            if carried
            else [shape((2 * rows, 3 * hidden), F32)],
            24,
            [pltpu.VMEM((size, hidden), BF16)] * 3 + [pltpu.SemaphoreType.DMA((3 * len(entries),))],
            n_e=n_e,
            entries=entries,
            carried=bool(carried),
        )

    part = forward(early, ())[0]
    own, theirs = forward(late, [after(part, *got)])
    deltas0, pick = call(
        delta_kernel, (own, hop(theirs, "fsdp", 1)), "vv", [shape((rows, 3 * hidden), BF16), shape((rows, 128), BF16)], 16
    )
    deltas = {0: deltas0}
    for p in near:
        deltas[p] = to(deltas0, p)
    deltas_other = {0: hop(deltas0, "fsdp", 1)}

    backs = call(
        back_kernel,
        (deltas[0], deltas_other[0], pick, *(weights[p] for p in range(n))),
        "vvv" + "a" * n,
        [shape((2, MOST, model // 2 + 128), BF16)] * n_e,
        16,
        [pltpu.VMEM((n, local, hidden), BF16)] * 2 + [pltpu.SemaphoreType.DMA((2 * n,))],
        n=n,
        n_e=n_e,
    )
    back = [backs[0]] + [hop(backs[k], "ep", k) for k in range(1, n_e)]
    for p in late:
        deltas[p] = to(after(deltas[p ^ top(p)], back[1]), top(p))
    for p in near:
        deltas_other[p] = hop(after(deltas[p], *back[1:3]), "fsdp", 1)

    def weight_sums(entries, carried):
        far = [got[p - 1] for p in entries if p]
        parts = [x for p in entries for x in (deltas[p], deltas_other[mirror(p, bits)])]
        size = 2 * rows * len(entries)
        here = both if 0 in entries else ()
        return call(
            weight_kernel,
            (*here, *carried, *far, *parts),
            "v" * (len(here) + len(carried)) + "a" * (len(far) + len(parts)),
            [shape((local, hidden), BF16)] * 3 if carried else [shape((local, 3 * hidden), F32)],
            24,
            [pltpu.VMEM((size, local), BF16)] * 2
            + [pltpu.VMEM((size, 3 * hidden), BF16), pltpu.SemaphoreType.DMA((4 * len(far) + len(parts),))],
            n_e=n_e,
            entries=entries,
            carried=bool(carried),
        )

    part = weight_sums(early, ())[0]
    back_other = [hop(after(x, part) if k == n_e - 1 else x, "fsdp", 1) for k, x in enumerate(back)]
    in_grad, gate_grad = call(
        final_kernel,
        (pos, ids, gates, select, *back, *back_other),
        "svvv" + "v" * 2 * n_e,
        [shape((tok, model), BF16), shape(ids.shape, BF16)],
        16,
        n_f=n_f,
        n_e=n_e,
    )

    for p in late:
        deltas_other[p] = hop(after(deltas[p], part, *back_other), "fsdp", 1)
    grads = weight_sums(late, [after(part, in_grad)])
    return (in_grad, gate_grad.T, *(g[:, None] for g in grads))


def solution(mesh):
    tok = P(("fsdp", "ep"), None)
    weight = P("fsdp", "ep", None)
    return jax.shard_map(
        per_device,
        mesh=mesh,
        in_specs=(tok, tok, tok, tok, weight, weight, weight),
        out_specs=(tok, tok, weight, weight, weight),
        check_vma=False,
    )
```

time: 110 us -> 96.1 us (0.87)
  starting transfers between devices: 40.3 us -> 27.8 us
  local copies, waits for them, and re-layouts: 6.82 us -> 0.01 us
  waiting for transfers between devices: 42.7 us -> 47.3 us
    ppermute x0 -> x9, waiting for transfers between devices: none -> 32.2 us  [to(): lax.ppermute(x, 'fsdp', [(i, i ^ flips(position, i & 1, bits)) for i in r...]
    ppermute x38 -> x19, waiting for transfers between devices: 42.7 us -> 15.2 us  [hop(): lax.ppermute(x, axis, [(i, i ^ offset) for i in range(lax.axis_size(axis))])]
    ppermute x38 -> x19, starting transfers between devices: 40.3 us -> 13.7 us  [hop(): lax.ppermute(x, axis, [(i, i ^ offset) for i in range(lax.axis_size(axis))])]
    ppermute x0 -> x9, starting transfers between devices: none -> 14.1 us  [to(): lax.ppermute(x, 'fsdp', [(i, i ^ flips(position, i & 1, bits)) for i in r...]
    unnamed x18 -> x4, local copies, waits for them, and re-layouts: 6.82 us -> 0.01 us
  transfers between devices with their start and end apart: 38 -> 28, of which waited for: 13 -> 14; matrix products, arithmetic and copies ran while one was open for 0% -> 0% of each run, Pallas kernels for 13% -> 15%
where the time goes in v3:
time: 96.1 us; the launch traced here: 95.9 us
  waiting for transfers between devices  47.3 us (49%)
  starting transfers between devices  27.8 us (29%)
  Pallas kernels  19.9 us (21%)
    ppermute x9, waiting for transfers between devices, to(): lax.ppermute(x, 'fsdp', [(i, i ^ flips(position, i & 1, bits)) for i in r...  32.2 us
    pallas_call x10, Pallas kernels, call(): pl.pallas_call(functools.partial(kernel, **static), out_shape=outs, in_sp...  19.9 us
    ppermute x19, waiting for transfers between devices, hop(): lax.ppermute(x, axis, [(i, i ^ offset) for i in range(lax.axis_size(axis))])  15.2 us
    ppermute x9, starting transfers between devices, to(): lax.ppermute(x, 'fsdp', [(i, i ^ flips(position, i & 1, bits)) for i in r...  14.1 us
    ppermute x19, starting transfers between devices, hop(): lax.ppermute(x, axis, [(i, i ^ offset) for i in range(lax.axis_size(axis))])  13.7 us
  transfers between devices with their start and end apart: 28, of which 14 were waited for; matrix products, arithmetic and copies ran while one was open for 0% of the time, Pallas kernels for 15%

profile of v3, /device:TPU:0, one launch (start us, length us, event | category | flops | bytes accessed | tf_op | source)
XLA Modules:
  0.0 95.9 jit_solution(8930530447476873689)
XLA Ops:
  1.9 3.0 %collective-permute-start.8 = (bf16[768,768]{1,0:T(8,128)(2,1)S(1)}, bf16[768,768]{1,0:T(8,128)(2,1)S(1)}, u32[]{:S(2)}, u32[]{:S(2)}) collective-permute-start(bf16[768,768]{1,0:T(8,128)(2,1)S(1)} %shard_map.111.refs_8_.refs_0_), channel_id=1, source_target_pairs={{0,8},{4,20},{8,0},{12,28},{16,24},{20,4},{24,16},{28,12},{1,9},{5... | collective-permute-start | bytes 3538952 | tf_op jit(solution)/shard_map/ppermute | solution.py:290
  4.9 1.5 %collective-permute-start.3 = (bf16[768,768]{1,0:T(8,128)(2,1)S(1)}, bf16[768,768]{1,0:T(8,128)(2,1)S(1)}, u32[]{:S(2)}, u32[]{:S(2)}) collective-permute-start(bf16[768,768]{1,0:T(8,128)(2,1)S(1)} %shard_map.111.refs_8_.refs_0_), channel_id=1, source_target_pairs={{0,16},{4,12},{8,24},{12,4},{16,0},{20,28},{24,8},{28,20},{1,17},{... | collective-permute-start | bytes 3538952 | tf_op jit(solution)/shard_map/ppermute | solution.py:290
  6.5 2.6 %shard_map.110 = (bf16[2,64,1024]{2,1,0:T(8,128)(2,1)S(1)}, bf16[2,64,1024]{2,1,0:T(8,128)(2,1)S(1)}, bf16[2,64,1024]{2,1,0:T(8,128)(2,1)S(1)}, bf16[2,64,1024]{2,1,0:T(8,128)(2,1)S(1)}, bf16[128,256]{1,0:T(8,128)(2,1)S(1)}) custom-call(s32[2]{0:T(128)S(1)} %pad_add_fusion.pos, s32[8,256]{1,0:T(8,128)S(1)} %bitcast.11, bf16[8,256]{1,0:T(8,128)(2,1)S(1)} %bitcast.13, ...), custom_call_target="tpu_custom_call" | custom-call | tf_op jit(solution)/shard_map/pallas_call | solution.py:272
  9.1 1.6 %collective-permute-start = (bf16[2,64,1024]{2,1,0:T(8,128)(2,1)S(1)}, bf16[2,64,1024]{2,1,0:T(8,128)(2,1)S(1)}, u32[]{:S(2)}, u32[]{:S(2)}) collective-permute-start(bf16[2,64,1024]{2,1,0:T(8,128)(2,1)S(1)} %get-tuple-element.37), channel_id=1, source_target_pairs={{0,1},{1,0},{2,3},{3,2},{4,5},{5,4},{6,7},{7,6},{8,9},{9,8},{10,11... | collective-permute-start | bytes 786440 | tf_op jit(solution)/shard_map/ppermute | solution.py:31
  10.8 2.6 %collective-permute-start.1 = (bf16[2,64,1024]{2,1,0:T(8,128)(2,1)S(1)}, bf16[2,64,1024]{2,1,0:T(8,128)(2,1)S(1)}, u32[]{:S(2)}, u32[]{:S(2)}) collective-permute-start(bf16[2,64,1024]{2,1,0:T(8,128)(2,1)S(1)} %get-tuple-element.38), channel_id=1, source_target_pairs={{0,2},{1,3},{2,0},{3,1},{4,6},{5,7},{6,4},{7,5},{8,10},{9,11},{10,... | collective-permute-start | bytes 786440 | tf_op jit(solution)/shard_map/ppermute | solution.py:31
  13.6 7.7 %collective-permute-done.refs_1_ = bf16[2,64,1024]{2,1,0:T(8,128)(2,1)S(1)} collective-permute-done((bf16[2,64,1024]{2,1,0:T(8,128)(2,1)S(1)}, bf16[2,64,1024]{2,1,0:T(8,128)(2,1)S(1)}, u32[]{:S(2)}, u32[]{:S(2)}) %collective-permute-start) | collective-permute-done | bytes 262176 | tf_op jit(solution)/shard_map/ppermute | solution.py:31
  21.2 10.0 %collective-permute-done.8.refs_9_.refs_1_ = bf16[768,768]{1,0:T(8,128)(2,1)S(1)} collective-permute-done((bf16[768,768]{1,0:T(8,128)(2,1)S(1)}, bf16[768,768]{1,0:T(8,128)(2,1)S(1)}, u32[]{:S(2)}, u32[]{:S(2)}) %collective-permute-start.8) | collective-permute-done | bytes 1179680 | tf_op jit(solution)/shard_map/ppermute | solution.py:290
  31.2 1.6 %collective-permute-start.12 = (bf16[768,768]{1,0:T(8,128)(2,1)S(1)}, bf16[768,768]{1,0:T(8,128)(2,1)S(1)}, u32[]{:S(2)}, u32[]{:S(2)}) collective-permute-start(bf16[768,768]{1,0:T(8,128)(2,1)S(1)} %collective-permute-done.8.refs_9_.refs_1_), channel_id=1, source_target_pairs={{0,16},{4,12},{8,24},{12,4},{16,0},{20,28},{24,8},{28,20},{1,17},{... | collective-permute-start | bytes 3538952 | tf_op jit(solution)/shard_map/ppermute | solution.py:290
  35.5 1.7 %collective-permute-start.9 = (bf16[2,256,256]{2,1,0:T(8,128)(2,1)S(1)}, bf16[2,256,256]{2,1,0:T(8,128)(2,1)S(1)}, u32[]{:S(2)}, u32[]{:S(2)}) collective-permute-start(bf16[2,256,256]{2,1,0:T(8,128)(2,1)S(1)} %get-tuple-element.41), channel_id=1, source_target_pairs={{0,8},{4,20},{8,0},{12,28},{16,24},{20,4},{24,16},{28,12},{1,9},{5... | collective-permute-start | bytes 786440 | tf_op jit(solution)/shard_map/ppermute | solution.py:290
  39.0 3.4 %shard_map.112.refs_8_ = f32[256,2304]{1,0:T(8,128)S(1)} custom-call(bf16[2,64,1024]{2,1,0:T(8,128)(2,1)S(1)} %get-tuple-element.40.refs_0_, bf16[2,64,1024]{2,1,0:T(8,128)(2,1)S(1)} %collective-permute-done.refs_1_, bf16[2,64,1024]{2,1,0:T(8,128)(2,1)S(1)} %collective-permute-done.1.refs_2_, bf16[2,64,1024]{2,1,0:T(8,128)(2,1)S(1)} %collective-permute-done.2.refs_3_, ...), custom_call_target="tpu_custom_call" | custom-call | tf_op jit(solution)/shard_map/pallas_call | solution.py:272
  42.5 2.3 %collective-permute-done.9.refs_8_ = bf16[2,256,256]{2,1,0:T(8,128)(2,1)S(1)} collective-permute-done((bf16[2,256,256]{2,1,0:T(8,128)(2,1)S(1)}, bf16[2,256,256]{2,1,0:T(8,128)(2,1)S(1)}, u32[]{:S(2)}, u32[]{:S(2)}) %collective-permute-start.9) | collective-permute-done | bytes 262176 | tf_op jit(solution)/shard_map/ppermute | solution.py:290
  44.8 13.8 %collective-permute-done.10.refs_9_ = bf16[2,256,256]{2,1,0:T(8,128)(2,1)S(1)} collective-permute-done((bf16[2,256,256]{2,1,0:T(8,128)(2,1)S(1)}, bf16[2,256,256]{2,1,0:T(8,128)(2,1)S(1)}, u32[]{:S(2)}, u32[]{:S(2)}) %collective-permute-start.10) | collective-permute-done | bytes 262176 | tf_op jit(solution)/shard_map/ppermute | solution.py:290
  60.2 2.0 %collective-permute-done.13.got = bf16[128,2304]{1,0:T(8,128)(2,1)S(1)} collective-permute-done((bf16[128,2304]{1,0:T(8,128)(2,1)S(1)}, bf16[128,2304]{1,0:T(8,128)(2,1)S(1)}, u32[]{:S(2)}, u32[]{:S(2)}) %collective-permute-start.13) | collective-permute-done | bytes 589856 | tf_op jit(solution)/shard_map/ppermute | solution.py:31
  62.9 2.5 %collective-permute-start.21 = (bf16[128,2304]{1,0:T(8,128)(2,1)S(1)}, bf16[128,2304]{1,0:T(8,128)(2,1)S(1)}, u32[]{:S(2)}, u32[]{:S(2)}) collective-permute-start(bf16[128,2304]{1,0:T(8,128)(2,1)S(1)} %get-tuple-element.48.deltas.refs_10_), channel_id=1, source_target_pairs={{0,8},{4,20},{8,0},{12,28},{16,24},{20,4},{24,16},{28,12},{1,9},{5... | collective-permute-start | bytes 1769480 | tf_op jit(solution)/shard_map/ppermute | solution.py:290
  66.1 4.0 %shard_map.116 = (bf16[2,32,1152]{2,1,0:T(8,128)(2,1)S(1)}, bf16[2,32,1152]{2,1,0:T(8,128)(2,1)S(1)}, bf16[2,32,1152]{2,1,0:T(8,128)(2,1)S(1)}, bf16[2,32,1152]{2,1,0:T(8,128)(2,1)S(1)}) custom-call(bf16[128,2304]{1,0:T(8,128)(2,1)S(1)} %get-tuple-element.48.deltas.refs_10_, bf16[128,2304]{1,0:T(8,128)(2,1)S(1)} %collective-permute-done.14.deltas_other.refs_11_, ...), custom_call_target="tpu_custom_call" | custom-call | tf_op jit(solution)/shard_map/pallas_call | solution.py:272
  70.0 1.6 %collective-permute-start.15 = (bf16[2,32,1152]{2,1,0:T(8,128)(2,1)S(1)}, bf16[2,32,1152]{2,1,0:T(8,128)(2,1)S(1)}, u32[]{:S(2)}, u32[]{:S(2)}) collective-permute-start(bf16[2,32,1152]{2,1,0:T(8,128)(2,1)S(1)} %get-tuple-element.51), channel_id=1, source_target_pairs={{0,1},{1,0},{2,3},{3,2},{4,5},{5,4},{6,7},{7,6},{8,9},{9,8},{10,11... | collective-permute-start | bytes 442376 | tf_op jit(solution)/shard_map/ppermute | solution.py:31
  71.7 2.6 %collective-permute-start.16 = (bf16[2,32,1152]{2,1,0:T(8,128)(2,1)S(1)}, bf16[2,32,1152]{2,1,0:T(8,128)(2,1)S(1)}, u32[]{:S(2)}, u32[]{:S(2)}) collective-permute-start(bf16[2,32,1152]{2,1,0:T(8,128)(2,1)S(1)} %get-tuple-element.52), channel_id=1, source_target_pairs={{0,2},{1,3},{2,0},{3,1},{4,6},{5,7},{6,4},{7,5},{8,10},{9,11},{10,... | collective-permute-start | bytes 442376 | tf_op jit(solution)/shard_map/ppermute | solution.py:31
  74.3 5.0 %collective-permute-done.21.refs_12_ = bf16[128,2304]{1,0:T(8,128)(2,1)S(1)} collective-permute-done((bf16[128,2304]{1,0:T(8,128)(2,1)S(1)}, bf16[128,2304]{1,0:T(8,128)(2,1)S(1)}, u32[]{:S(2)}, u32[]{:S(2)}) %collective-permute-start.21) | collective-permute-done | bytes 589856 | tf_op jit(solution)/shard_map/ppermute | solution.py:290
  79.3 1.8 %collective-permute-done.16.refs_2_ = bf16[2,32,1152]{2,1,0:T(8,128)(2,1)S(1)} collective-permute-done((bf16[2,32,1152]{2,1,0:T(8,128)(2,1)S(1)}, bf16[2,32,1152]{2,1,0:T(8,128)(2,1)S(1)}, u32[]{:S(2)}, u32[]{:S(2)}) %collective-permute-start.16) | collective-permute-done | bytes 147488 | tf_op jit(solution)/shard_map/ppermute | solution.py:31
  82.9 2.5 %collective-permute-start.17 = (bf16[2,32,1152]{2,1,0:T(8,128)(2,1)S(1)}, bf16[2,32,1152]{2,1,0:T(8,128)(2,1)S(1)}, u32[]{:S(2)}, u32[]{:S(2)}) collective-permute-start(bf16[2,32,1152]{2,1,0:T(8,128)(2,1)S(1)} %get-tuple-element.53), channel_id=1, source_target_pairs={{0,3},{1,2},{2,1},{3,0},{4,7},{5,6},{6,5},{7,4},{8,11},{9,10},{10,... | collective-permute-start | bytes 442376 | tf_op jit(solution)/shard_map/ppermute | solution.py:31
  86.0 2.7 %shard_map.117.refs_0_ = f32[256,2304]{1,0:T(8,128)S(1)} custom-call(bf16[2,64,1024]{2,1,0:T(8,128)(2,1)S(1)} %get-tuple-element.40.refs_0_, bf16[2,64,1024]{2,1,0:T(8,128)(2,1)S(1)} %collective-permute-done.refs_1_, bf16[2,64,1024]{2,1,0:T(8,128)(2,1)S(1)} %collective-permute-done.1.refs_2_, bf16[2,64,1024]{2,1,0:T(8,128)(2,1)S(1)} %collective-permute-done.2.refs_3_, ...), custom_call_target="tpu_custom_call" | custom-call | tf_op jit(solution)/shard_map/pallas_call | solution.py:272
  88.7 1.8 %collective-permute-done.17.refs_3_ = bf16[2,32,1152]{2,1,0:T(8,128)(2,1)S(1)} collective-permute-done((bf16[2,32,1152]{2,1,0:T(8,128)(2,1)S(1)}, bf16[2,32,1152]{2,1,0:T(8,128)(2,1)S(1)}, u32[]{:S(2)}, u32[]{:S(2)}) %collective-permute-start.17) | collective-permute-done | bytes 147488 | tf_op jit(solution)/shard_map/ppermute | solution.py:31
  92.0 2.0 %shard_map.118 = (bf16[256,2048]{1,0:T(8,128)(2,1)}, bf16[8,256]{1,0:T(8,128)(2,1)}) custom-call(s32[2]{0:T(128)S(1)} %pad_add_fusion.pos, s32[8,256]{1,0:T(8,128)S(1)} %bitcast.12, bf16[8,256]{1,0:T(8,128)(2,1)S(1)} %bitcast.14, bf16[128,256]{1,0:T(8,128)(2,1)S(1)} %get-tuple-element.35.select, bf16[2,32,1152]{2,1,0:T(8,128)(2,1)S(1)} %get-tuple-element.50.refs_0_, ...), custom_call_target="tpu_custom_call" | custom-call | tf_op jit(solution)/shard_map/pallas_call | solution.py:272
  94.0 2.0 %shard_map.119 = (bf16[256,768]{1,0:T(8,128)(2,1)}, bf16[256,768]{1,0:T(8,128)(2,1)}, bf16[256,768]{1,0:T(8,128)(2,1)}) custom-call(f32[256,2304]{1,0:T(8,128)S(1)} %shard_map.117.refs_0_, bf16[2,256,256]{2,1,0:T(8,128)(2,1)S(1)} %collective-permute-done.11.refs_1_, bf16[128,2304]{1,0:T(8,128)(2,1)S(1)} %collective-permute-done.26.refs_2_, ...), custom_call_target="tpu_custom_call" | custom-call | tf_op jit(solution)/shard_map/pallas_call | solution.py:272
  (47 shorter events, 13.0 us)
Async XLA Ops:
  1.9 29.3 %collective-permute-start.8 = (bf16[768,768]{1,0:T(8,128)(2,1)S(1)}, bf16[768,768]{1,0:T(8,128)(2,1)S(1)}, u32[]{:S(2)}, u32[]{:S(2)}) collective-permute-start(bf16[768,768]{1,0:T(8,128)(2,1)S(1)} %shard_map.111.refs_8_.refs_0_), channel_id=1, source_target_pairs={{0,8},{4,20},{8,0},{12,28},{16,24},{20,4},{24,16},{28,12},{1,9},{5... | collective-permute-start | bytes 3538952 | tf_op jit(solution)/shard_map/ppermute | solution.py:290
  4.9 28.4 %collective-permute-start.3 = (bf16[768,768]{1,0:T(8,128)(2,1)S(1)}, bf16[768,768]{1,0:T(8,128)(2,1)S(1)}, u32[]{:S(2)}, u32[]{:S(2)}) collective-permute-start(bf16[768,768]{1,0:T(8,128)(2,1)S(1)} %shard_map.111.refs_8_.refs_0_), channel_id=1, source_target_pairs={{0,16},{4,12},{8,24},{12,4},{16,0},{20,28},{24,8},{28,20},{1,17},{... | collective-permute-start | bytes 3538952 | tf_op jit(solution)/shard_map/ppermute | solution.py:290
  9.1 12.1 %collective-permute-start = (bf16[2,64,1024]{2,1,0:T(8,128)(2,1)S(1)}, bf16[2,64,1024]{2,1,0:T(8,128)(2,1)S(1)}, u32[]{:S(2)}, u32[]{:S(2)}) collective-permute-start(bf16[2,64,1024]{2,1,0:T(8,128)(2,1)S(1)} %get-tuple-element.37), channel_id=1, source_target_pairs={{0,1},{1,0},{2,3},{3,2},{4,5},{5,4},{6,7},{7,6},{8,9},{9,8},{10,11... | collective-permute-start | bytes 786440 | tf_op jit(solution)/shard_map/ppermute | solution.py:31
  10.8 22.0 %collective-permute-start.1 = (bf16[2,64,1024]{2,1,0:T(8,128)(2,1)S(1)}, bf16[2,64,1024]{2,1,0:T(8,128)(2,1)S(1)}, u32[]{:S(2)}, u32[]{:S(2)}) collective-permute-start(bf16[2,64,1024]{2,1,0:T(8,128)(2,1)S(1)} %get-tuple-element.38), channel_id=1, source_target_pairs={{0,2},{1,3},{2,0},{3,1},{4,6},{5,7},{6,4},{7,5},{8,10},{9,11},{10,... | collective-permute-start | bytes 786440 | tf_op jit(solution)/shard_map/ppermute | solution.py:31
  13.3 19.9 %collective-permute-start.2 = (bf16[2,64,1024]{2,1,0:T(8,128)(2,1)S(1)}, bf16[2,64,1024]{2,1,0:T(8,128)(2,1)S(1)}, u32[]{:S(2)}, u32[]{:S(2)}) collective-permute-start(bf16[2,64,1024]{2,1,0:T(8,128)(2,1)S(1)} %get-tuple-element.39), channel_id=1, source_target_pairs={{0,3},{1,2},{2,1},{3,0},{4,7},{5,6},{6,5},{7,4},{8,11},{9,10},{10,... | collective-permute-start | bytes 786440 | tf_op jit(solution)/shard_map/ppermute | solution.py:31
  31.2 27.4 %collective-permute-start.12 = (bf16[768,768]{1,0:T(8,128)(2,1)S(1)}, bf16[768,768]{1,0:T(8,128)(2,1)S(1)}, u32[]{:S(2)}, u32[]{:S(2)}) collective-permute-start(bf16[768,768]{1,0:T(8,128)(2,1)S(1)} %collective-permute-done.8.refs_9_.refs_1_), channel_id=1, source_target_pairs={{0,16},{4,12},{8,24},{12,4},{16,0},{20,28},{24,8},{28,20},{1,17},{... | collective-permute-start | bytes 3538952 | tf_op jit(solution)/shard_map/ppermute | solution.py:290
  33.3 2.1 %collective-permute-start.4 = (bf16[2,64,1024]{2,1,0:T(8,128)(2,1)S(1)}, bf16[2,64,1024]{2,1,0:T(8,128)(2,1)S(1)}, u32[]{:S(2)}, u32[]{:S(2)}) collective-permute-start(bf16[2,64,1024]{2,1,0:T(8,128)(2,1)S(1)} %get-tuple-element.40.refs_0_), channel_id=1, source_target_pairs={{0,4},{4,0},{8,12},{12,8},{16,20},{20,16},{24,28},{28,24},{1,5},{5... | collective-permute-start | bytes 786440 | tf_op jit(solution)/shard_map/ppermute | solution.py:31
  35.5 9.3 %collective-permute-start.9 = (bf16[2,256,256]{2,1,0:T(8,128)(2,1)S(1)}, bf16[2,256,256]{2,1,0:T(8,128)(2,1)S(1)}, u32[]{:S(2)}, u32[]{:S(2)}) collective-permute-start(bf16[2,256,256]{2,1,0:T(8,128)(2,1)S(1)} %get-tuple-element.41), channel_id=1, source_target_pairs={{0,8},{4,20},{8,0},{12,28},{16,24},{20,4},{24,16},{28,12},{1,9},{5... | collective-permute-start | bytes 786440 | tf_op jit(solution)/shard_map/ppermute | solution.py:290
  37.2 21.4 %collective-permute-start.10 = (bf16[2,256,256]{2,1,0:T(8,128)(2,1)S(1)}, bf16[2,256,256]{2,1,0:T(8,128)(2,1)S(1)}, u32[]{:S(2)}, u32[]{:S(2)}) collective-permute-start(bf16[2,256,256]{2,1,0:T(8,128)(2,1)S(1)} %get-tuple-element.42), channel_id=1, source_target_pairs={{0,16},{4,12},{8,24},{12,4},{16,0},{20,28},{24,8},{28,20},{1,17},{... | collective-permute-start | bytes 786440 | tf_op jit(solution)/shard_map/ppermute | solution.py:290
  38.5 20.1 %collective-permute-start.11 = (bf16[2,256,256]{2,1,0:T(8,128)(2,1)S(1)}, bf16[2,256,256]{2,1,0:T(8,128)(2,1)S(1)}, u32[]{:S(2)}, u32[]{:S(2)}) collective-permute-start(bf16[2,256,256]{2,1,0:T(8,128)(2,1)S(1)} %get-tuple-element.43), channel_id=1, source_target_pairs={{0,24},{4,28},{8,16},{12,20},{16,8},{20,12},{24,0},{28,4},{1,25},{... | collective-permute-start | bytes 786440 | tf_op jit(solution)/shard_map/ppermute | solution.py:290
  60.1 2.1 %collective-permute-start.13 = (bf16[128,2304]{1,0:T(8,128)(2,1)S(1)}, bf16[128,2304]{1,0:T(8,128)(2,1)S(1)}, u32[]{:S(2)}, u32[]{:S(2)}) collective-permute-start(bf16[128,2304]{1,0:T(8,128)(2,1)S(1)} %get-tuple-element.47), channel_id=1, source_target_pairs={{0,4},{4,0},{8,12},{12,8},{16,20},{20,16},{24,28},{28,24},{1,5},{5... | collective-permute-start | bytes 1769480 | tf_op jit(solution)/shard_map/ppermute | solution.py:31
  62.7 3.4 %collective-permute-start.14 = (bf16[128,2304]{1,0:T(8,128)(2,1)S(1)}, bf16[128,2304]{1,0:T(8,128)(2,1)S(1)}, u32[]{:S(2)}, u32[]{:S(2)}) collective-permute-start(bf16[128,2304]{1,0:T(8,128)(2,1)S(1)} %get-tuple-element.48.deltas.refs_10_), channel_id=1, source_target_pairs={{0,4},{4,0},{8,12},{12,8},{16,20},{20,16},{24,28},{28,24},{1,5},{5... | collective-permute-start | bytes 1769480 | tf_op jit(solution)/shard_map/ppermute | solution.py:31
  62.9 16.4 %collective-permute-start.21 = (bf16[128,2304]{1,0:T(8,128)(2,1)S(1)}, bf16[128,2304]{1,0:T(8,128)(2,1)S(1)}, u32[]{:S(2)}, u32[]{:S(2)}) collective-permute-start(bf16[128,2304]{1,0:T(8,128)(2,1)S(1)} %get-tuple-element.48.deltas.refs_10_), channel_id=1, source_target_pairs={{0,8},{4,20},{8,0},{12,28},{16,24},{20,4},{24,16},{28,12},{1,9},{5... | collective-permute-start | bytes 1769480 | tf_op jit(solution)/shard_map/ppermute | solution.py:290
  65.3 15.7 %collective-permute-start.22 = (bf16[128,2304]{1,0:T(8,128)(2,1)S(1)}, bf16[128,2304]{1,0:T(8,128)(2,1)S(1)}, u32[]{:S(2)}, u32[]{:S(2)}) collective-permute-start(bf16[128,2304]{1,0:T(8,128)(2,1)S(1)} %get-tuple-element.48.deltas.refs_10_), channel_id=1, source_target_pairs={{0,16},{4,12},{8,24},{12,4},{16,0},{20,28},{24,8},{28,20},{1,17},{... | collective-permute-start | bytes 1769480 | tf_op jit(solution)/shard_map/ppermute | solution.py:290
  70.0 9.2 %collective-permute-start.15 = (bf16[2,32,1152]{2,1,0:T(8,128)(2,1)S(1)}, bf16[2,32,1152]{2,1,0:T(8,128)(2,1)S(1)}, u32[]{:S(2)}, u32[]{:S(2)}) collective-permute-start(bf16[2,32,1152]{2,1,0:T(8,128)(2,1)S(1)} %get-tuple-element.51), channel_id=1, source_target_pairs={{0,1},{1,0},{2,3},{3,2},{4,5},{5,4},{6,7},{7,6},{8,9},{9,8},{10,11... | collective-permute-start | bytes 442376 | tf_op jit(solution)/shard_map/ppermute | solution.py:31
  71.7 9.4 %collective-permute-start.16 = (bf16[2,32,1152]{2,1,0:T(8,128)(2,1)S(1)}, bf16[2,32,1152]{2,1,0:T(8,128)(2,1)S(1)}, u32[]{:S(2)}, u32[]{:S(2)}) collective-permute-start(bf16[2,32,1152]{2,1,0:T(8,128)(2,1)S(1)} %get-tuple-element.52), channel_id=1, source_target_pairs={{0,2},{1,3},{2,0},{3,1},{4,6},{5,7},{6,4},{7,5},{8,10},{9,11},{10,... | collective-permute-start | bytes 442376 | tf_op jit(solution)/shard_map/ppermute | solution.py:31
  81.1 4.3 %collective-permute-start.23 = (bf16[128,2304]{1,0:T(8,128)(2,1)S(1)}, bf16[128,2304]{1,0:T(8,128)(2,1)S(1)}, u32[]{:S(2)}, u32[]{:S(2)}) collective-permute-start(bf16[128,2304]{1,0:T(8,128)(2,1)S(1)} %collective-permute-done.22.refs_14_), channel_id=1, source_target_pairs={{0,4},{4,0},{8,12},{12,8},{16,20},{20,16},{24,28},{28,24},{1,5},{5... | collective-permute-start | bytes 1769480 | tf_op jit(solution)/shard_map/ppermute | solution.py:31
  81.1 4.8 %collective-permute-start.24 = (bf16[128,2304]{1,0:T(8,128)(2,1)S(1)}, bf16[128,2304]{1,0:T(8,128)(2,1)S(1)}, u32[]{:S(2)}, u32[]{:S(2)}) collective-permute-start(bf16[128,2304]{1,0:T(8,128)(2,1)S(1)} %collective-permute-done.21.refs_12_), channel_id=1, source_target_pairs={{0,4},{4,0},{8,12},{12,8},{16,20},{20,16},{24,28},{28,24},{1,5},{5... | collective-permute-start | bytes 1769480 | tf_op jit(solution)/shard_map/ppermute | solution.py:31
  81.6 9.9 %collective-permute-start.26 = (bf16[128,2304]{1,0:T(8,128)(2,1)S(1)}, bf16[128,2304]{1,0:T(8,128)(2,1)S(1)}, u32[]{:S(2)}, u32[]{:S(2)}) collective-permute-start(bf16[128,2304]{1,0:T(8,128)(2,1)S(1)} %collective-permute-done.21.refs_12_), channel_id=1, source_target_pairs={{0,16},{4,12},{8,24},{12,4},{16,0},{20,28},{24,8},{28,20},{1,17},{... | collective-permute-start | bytes 1769480 | tf_op jit(solution)/shard_map/ppermute | solution.py:290
  82.9 7.5 %collective-permute-start.17 = (bf16[2,32,1152]{2,1,0:T(8,128)(2,1)S(1)}, bf16[2,32,1152]{2,1,0:T(8,128)(2,1)S(1)}, u32[]{:S(2)}, u32[]{:S(2)}) collective-permute-start(bf16[2,32,1152]{2,1,0:T(8,128)(2,1)S(1)} %get-tuple-element.53), channel_id=1, source_target_pairs={{0,3},{1,2},{2,1},{3,0},{4,7},{5,6},{6,5},{7,4},{8,11},{9,10},{10,... | collective-permute-start | bytes 442376 | tf_op jit(solution)/shard_map/ppermute | solution.py:31
  85.4 5.1 %collective-permute-start.18 = (bf16[2,32,1152]{2,1,0:T(8,128)(2,1)S(1)}, bf16[2,32,1152]{2,1,0:T(8,128)(2,1)S(1)}, u32[]{:S(2)}, u32[]{:S(2)}) collective-permute-start(bf16[2,32,1152]{2,1,0:T(8,128)(2,1)S(1)} %get-tuple-element.50.refs_0_), channel_id=1, source_target_pairs={{0,4},{4,0},{8,12},{12,8},{16,20},{20,16},{24,28},{28,24},{1,5},{5... | collective-permute-start | bytes 442376 | tf_op jit(solution)/shard_map/ppermute | solution.py:31
  85.4 5.1 %collective-permute-start.19 = (bf16[2,32,1152]{2,1,0:T(8,128)(2,1)S(1)}, bf16[2,32,1152]{2,1,0:T(8,128)(2,1)S(1)}, u32[]{:S(2)}, u32[]{:S(2)}) collective-permute-start(bf16[2,32,1152]{2,1,0:T(8,128)(2,1)S(1)} %collective-permute-done.15.refs_1_), channel_id=1, source_target_pairs={{0,4},{4,0},{8,12},{12,8},{16,20},{20,16},{24,28},{28,24},{1,5},{5... | collective-permute-start | bytes 442376 | tf_op jit(solution)/shard_map/ppermute | solution.py:31
  85.9 4.6 %collective-permute-start.20 = (bf16[2,32,1152]{2,1,0:T(8,128)(2,1)S(1)}, bf16[2,32,1152]{2,1,0:T(8,128)(2,1)S(1)}, u32[]{:S(2)}, u32[]{:S(2)}) collective-permute-start(bf16[2,32,1152]{2,1,0:T(8,128)(2,1)S(1)} %collective-permute-done.16.refs_2_), channel_id=1, source_target_pairs={{0,4},{4,0},{8,12},{12,8},{16,20},{20,16},{24,28},{28,24},{1,5},{5... | collective-permute-start | bytes 442376 | tf_op jit(solution)/shard_map/ppermute | solution.py:31
  91.8 2.2 %collective-permute-start.27 = (bf16[128,2304]{1,0:T(8,128)(2,1)S(1)}, bf16[128,2304]{1,0:T(8,128)(2,1)S(1)}, u32[]{:S(2)}, u32[]{:S(2)}) collective-permute-start(bf16[128,2304]{1,0:T(8,128)(2,1)S(1)} %collective-permute-done.26.refs_2_), channel_id=1, source_target_pairs={{0,4},{4,0},{8,12},{12,8},{16,20},{20,16},{24,28},{28,24},{1,5},{5... | collective-permute-start | bytes 1769480 | tf_op jit(solution)/shard_map/ppermute | solution.py:31
  (6 other events, 18.4 us)

commit v4 on v3

--- a/solution.py
+++ b/solution.py
@@ -133,14 +133,8 @@
     if carried:
         total_in, refs = refs[0], refs[1:]
     count = len(entries)
-    pieces, refs = refs[:count], refs[count:]
-    outs, (gate, up, down, sems) = refs[:-4], refs[-4:]
-    hidden = gate.shape[1]
-    width = gate.shape[0] // count
-    fetch = Copies(sems)
-    for at, whole in enumerate((gate, up, down)):
-        for i in range(count):
-            fetch.start(pieces[i].at[pl.ds(at * width, width)], whole.at[pl.ds(i * width, width)])
+    pieces, outs = refs[:count], refs[count:]
+    width, hidden = pieces[0].shape[0] // 3, pieces[0].shape[1]
 
     def rows_of(part):
         return jnp.concatenate(
@@ -154,10 +148,10 @@
 
     x, q = rows_of(slice(0, MOST)), rows_of(slice(MOST, 2 * MOST))
     rows = n_e * MOST
-    for at, (left, right) in enumerate(((x, gate), (x, up), (q, down))):
-        fetch.wait(count)
+    for at, left in enumerate((x, x, q)):
+        right = jnp.concatenate([p[at * width : (at + 1) * width] for p in pieces], axis=0)
         here = slice(at * hidden, (at + 1) * hidden)
-        part = mm(left, right[...])
+        part = mm(left, right)
         if carried:
             part = part + total_in[:, here]
             outs[0][:, here] = part[:rows]
@@ -188,18 +182,12 @@
 
 
 def back_kernel(deltas, deltas_other, pick, *refs, n, n_e):
-    pieces, outs, (gate, up, sems) = refs[:n], refs[n : n + n_e], refs[n + n_e :]
-    hidden = gate.shape[2]
-    width = gate.shape[1]
-    fetch = Copies(sems)
-    for i in range(n):
-        fetch.start(pieces[i].at[:width], gate.at[i])
-        fetch.start(pieces[i].at[pl.ds(width, width)], up.at[i])
+    pieces, outs = refs[:n], refs[n:]
+    width, hidden = pieces[0].shape[0] // 3, pieces[0].shape[1]
     da = jnp.concatenate([deltas[:, :hidden], deltas_other[:, :hidden]], axis=0)
     du = jnp.concatenate([deltas[:, hidden : 2 * hidden], deltas_other[:, hidden : 2 * hidden]], axis=0)
     for i in range(n):
-        fetch.wait(2)
-        c = (mm_trail(da, gate[i]) + mm_trail(du, up[i])).astype(BF16)
+        c = (mm_trail(da, pieces[i][:width]) + mm_trail(du, pieces[i][width : 2 * width])).astype(BF16)
         here = slice(i * width, (i + 1) * width)
         for side in range(2):
             for k in range(n_e):
@@ -210,36 +198,32 @@
             outs[k][side, :, n * width :] = pick[k * MOST : (k + 1) * MOST]
 
 
-def weight_kernel(*refs, n_e, entries, carried):
+def weight_kernel(*refs, n_e, count, entries, carried):
     if 0 in entries:
         sides, refs = (refs[:n_e], refs[n_e : 2 * n_e]), refs[2 * n_e :]
     if carried:
         total_in, refs = refs[0], refs[1:]
     far = [i for i in entries if i]
     got, deltas = refs[: len(far)], refs[len(far) : len(far) + 2 * len(entries)]
-    outs, (x, q, d, sems) = refs[len(far) + 2 * len(entries) : -4], refs[-4:]
-    width, hidden = x.shape[1], d.shape[1] // 3
+    outs = refs[len(far) + 2 * len(entries) :]
+    hidden = deltas[0].shape[1] // 3
     rows = n_e * MOST
-    fetch = Copies(sems)
-    for i, p in enumerate(deltas):
-        fetch.start(p, d.at[pl.ds(i * rows, rows)])
-    for place, i in enumerate(entries):
-        if i == 0:
-            continue
-        for side in range(2):
-            at = pl.ds((2 * place + side) * rows, rows)
-            fetch.start(got[far.index(i)].at[side, :rows], x.at[at])
-            fetch.start(got[far.index(i)].at[side, rows:], q.at[at])
-    if 0 in entries:
-        for side in range(2):
-            for k in range(n_e):
-                at = slice(side * rows + k * MOST, side * rows + (k + 1) * MOST)
-                x[at] = sides[side][k][side, :MOST, :width]
-                q[at] = sides[side][k][side, MOST:, :width]
-    fetch.wait()
+
+    def rows_of(part):
+        lefts = []
+        for i in entries:
+            for side in range(2):
+                if i:
+                    lefts.append(got[far.index(i)][side, part * rows : (part + 1) * rows])
+                else:
+                    width = sides[0][0].shape[2] // count
+                    lefts += [s[side, part * MOST : (part + 1) * MOST, :width] for s in sides[side]]
+        return jnp.concatenate(lefts, axis=0)
+
+    x, q = rows_of(0), rows_of(1)
     for at, left in enumerate((x, x, q)):
         here = slice(at * hidden, (at + 1) * hidden)
-        part = mm_lead(left[...], d[:, here])
+        part = mm_lead(left, jnp.concatenate([d[:, here] for d in deltas], axis=0))
         if carried:
             outs[at][...] = (total_in[:, here] + part).astype(BF16)
         else:
@@ -251,11 +235,12 @@
     f, e = pos[0], pos[1]
     width = in_grad.shape[1] // n_f
     total = n_f // 2 * width
-    for side, position in itertools.product(range(2), range(n_f // 2)):
-        at = pl.ds(pl.multiple_of(slice_of(f, side, position, n_f) * width, width), width)
-        here = slice(position * width, (position + 1) * width)
-        c = jnp.concatenate([(mine, other)[side][k][side, :, here] for k in range(n_e)], axis=0)
-        in_grad[:, at] = mm_lead(select[...], c).astype(BF16)
+    for side in range(2):
+        c = jnp.concatenate([(mine, other)[side][k][side, :, :total] for k in range(n_e)], axis=0)
+        rows = mm_lead(select[...], c).astype(BF16)
+        for position in range(n_f // 2):
+            at = pl.ds(pl.multiple_of(slice_of(f, side, position, n_f) * width, width), width)
+            in_grad[:, at] = rows[:, position * width : (position + 1) * width]
     half = (mine[0].shape[2] - total) // 2
     found = jnp.zeros(ids.shape, F32)
     for k in range(n_e):
@@ -343,23 +328,21 @@
 
     def forward(entries, carried):
         pieces = [weights[p] for p in entries]
-        size = len(entries) * local
         return call(
             forward_kernel,
             (*both, *carried, *pieces),
-            "v" * (2 * n_e + len(carried)) + "a" * len(pieces),
+            "v" * (2 * n_e + len(carried) + len(pieces)),
             [shape((rows, 3 * hidden), F32), shape((rows, 3 * hidden), BF16)]
             if carried
             else [shape((2 * rows, 3 * hidden), F32)],
-            24,
-            [pltpu.VMEM((size, hidden), BF16)] * 3 + [pltpu.SemaphoreType.DMA((3 * len(entries),))],
+            32,
             n_e=n_e,
             entries=entries,
             carried=bool(carried),
         )
 
     part = forward(early, ())[0]
-    own, theirs = forward(late, [after(part, *got)])
+    own, theirs = forward(late, [after(part, got[0])])
     deltas0, pick = call(
         delta_kernel, (own, hop(theirs, "fsdp", 1)), "vv", [shape((rows, 3 * hidden), BF16), shape((rows, 128), BF16)], 16
     )
@@ -371,39 +354,36 @@
     backs = call(
         back_kernel,
         (deltas[0], deltas_other[0], pick, *(weights[p] for p in range(n))),
-        "vvv" + "a" * n,
+        "v" * (3 + n),
         [shape((2, MOST, model // 2 + 128), BF16)] * n_e,
-        16,
-        [pltpu.VMEM((n, local, hidden), BF16)] * 2 + [pltpu.SemaphoreType.DMA((2 * n,))],
+        24,
         n=n,
         n_e=n_e,
     )
     back = [backs[0]] + [hop(backs[k], "ep", k) for k in range(1, n_e)]
     for p in late:
-        deltas[p] = to(after(deltas[p ^ top(p)], back[1]), top(p))
+        deltas[p] = to(after(deltas[p ^ top(p)], back[1], *got[1:-1]), top(p))
     for p in near:
         deltas_other[p] = hop(after(deltas[p], *back[1:3]), "fsdp", 1)
 
     def weight_sums(entries, carried):
         far = [got[p - 1] for p in entries if p]
         parts = [x for p in entries for x in (deltas[p], deltas_other[mirror(p, bits)])]
-        size = 2 * rows * len(entries)
         here = both if 0 in entries else ()
         return call(
             weight_kernel,
             (*here, *carried, *far, *parts),
-            "v" * (len(here) + len(carried)) + "a" * (len(far) + len(parts)),
+            "v" * (len(here) + len(carried) + len(far) + len(parts)),
             [shape((local, hidden), BF16)] * 3 if carried else [shape((local, 3 * hidden), F32)],
-            24,
-            [pltpu.VMEM((size, local), BF16)] * 2
-            + [pltpu.VMEM((size, 3 * hidden), BF16), pltpu.SemaphoreType.DMA((4 * len(far) + len(parts),))],
+            32,
+            count=n,
             n_e=n_e,
             entries=entries,
             carried=bool(carried),
         )
 
     part = weight_sums(early, ())[0]
-    back_other = [hop(after(x, part) if k == n_e - 1 else x, "fsdp", 1) for k, x in enumerate(back)]
+    back_other = [hop(after(x, part, got[-1]) if k == n_e - 1 else x, "fsdp", 1) for k, x in enumerate(back)]
     in_grad, gate_grad = call(
         final_kernel,
         (pos, ids, gates, select, *back, *back_other),

time: 96.1 us -> 92.5 us (0.963)
  Pallas kernels: 19.9 us -> 11.4 us
  starting transfers between devices: 27.8 us -> 33.6 us
    pallas_call x10, Pallas kernels: 19.9 us -> 11.4 us  [call(): pl.pallas_call(functools.partial(kernel, **static), out_shape=outs, in_sp...]
    ppermute x19, starting transfers between devices: 13.7 us -> 18 us  [hop(): lax.ppermute(x, axis, [(i, i ^ offset) for i in range(lax.axis_size(axis))])]
    ppermute x19, waiting for transfers between devices: 15.2 us -> 13.3 us  [hop(): lax.ppermute(x, axis, [(i, i ^ offset) for i in range(lax.axis_size(axis))])]
    ppermute x9, starting transfers between devices: 14.1 us -> 15.6 us  [to(): lax.ppermute(x, 'fsdp', [(i, i ^ flips(position, i & 1, bits)) for i in r...]
    ppermute x9, waiting for transfers between devices: 32.2 us -> 33.1 us  [to(): lax.ppermute(x, 'fsdp', [(i, i ^ flips(position, i & 1, bits)) for i in r...]
  transfers between devices with their start and end apart: 28 -> 28, of which waited for: 14 -> 16; matrix products, arithmetic and copies ran while one was open for 0% -> 0% of each run, Pallas kernels for 15% -> 9%
where the time goes in v4:
time: 92.5 us; the launch traced here: 92.3 us
  waiting for transfers between devices  46.5 us (50%)
  starting transfers between devices  33.6 us (36%)
  Pallas kernels  11.4 us (12%)
    ppermute x9, waiting for transfers between devices, to(): lax.ppermute(x, 'fsdp', [(i, i ^ flips(position, i & 1, bits)) for i in r...  33.1 us
    ppermute x19, starting transfers between devices, hop(): lax.ppermute(x, axis, [(i, i ^ offset) for i in range(lax.axis_size(axis))])  18 us
    ppermute x9, starting transfers between devices, to(): lax.ppermute(x, 'fsdp', [(i, i ^ flips(position, i & 1, bits)) for i in r...  15.6 us
    ppermute x19, waiting for transfers between devices, hop(): lax.ppermute(x, axis, [(i, i ^ offset) for i in range(lax.axis_size(axis))])  13.3 us
    pallas_call x10, Pallas kernels, call(): pl.pallas_call(functools.partial(kernel, **static), out_shape=outs, in_sp...  11.4 us
  transfers between devices with their start and end apart: 28, of which 16 were waited for; matrix products, arithmetic and copies ran while one was open for 0% of the time, Pallas kernels for 9%

profile of v4, /device:TPU:0, one launch (start us, length us, event | category | flops | bytes accessed | tf_op | source)
XLA Modules:
  0.0 92.3 jit_solution(5438712871244262837)
XLA Ops:
  1.9 3.0 %collective-permute-start.8 = (bf16[768,768]{1,0:T(8,128)(2,1)S(1)}, bf16[768,768]{1,0:T(8,128)(2,1)S(1)}, u32[]{:S(2)}, u32[]{:S(2)}) collective-permute-start(bf16[768,768]{1,0:T(8,128)(2,1)S(1)} %shard_map.111.refs_8_.refs_0_), channel_id=1, source_target_pairs={{0,8},{4,20},{8,0},{12,28},{16,24},{20,4},{24,16},{28,12},{1,9},{5... | collective-permute-start | bytes 3538952 | tf_op jit(solution)/shard_map/ppermute | solution.py:275
  4.9 1.5 %collective-permute-start.3 = (bf16[768,768]{1,0:T(8,128)(2,1)S(1)}, bf16[768,768]{1,0:T(8,128)(2,1)S(1)}, u32[]{:S(2)}, u32[]{:S(2)}) collective-permute-start(bf16[768,768]{1,0:T(8,128)(2,1)S(1)} %shard_map.111.refs_8_.refs_0_), channel_id=1, source_target_pairs={{0,16},{4,12},{8,24},{12,4},{16,0},{20,28},{24,8},{28,20},{1,17},{... | collective-permute-start | bytes 3538952 | tf_op jit(solution)/shard_map/ppermute | solution.py:275
  6.5 2.6 %shard_map.110 = (bf16[2,64,1024]{2,1,0:T(8,128)(2,1)S(1)}, bf16[2,64,1024]{2,1,0:T(8,128)(2,1)S(1)}, bf16[2,64,1024]{2,1,0:T(8,128)(2,1)S(1)}, bf16[2,64,1024]{2,1,0:T(8,128)(2,1)S(1)}, bf16[128,256]{1,0:T(8,128)(2,1)S(1)}) custom-call(s32[2]{0:T(128)S(1)} %pad_add_fusion.pos, s32[8,256]{1,0:T(8,128)S(1)} %bitcast.11, bf16[8,256]{1,0:T(8,128)(2,1)S(1)} %bitcast.13, ...), custom_call_target="tpu_custom_call" | custom-call | tf_op jit(solution)/shard_map/pallas_call | solution.py:257
  9.1 1.6 %collective-permute-start = (bf16[2,64,1024]{2,1,0:T(8,128)(2,1)S(1)}, bf16[2,64,1024]{2,1,0:T(8,128)(2,1)S(1)}, u32[]{:S(2)}, u32[]{:S(2)}) collective-permute-start(bf16[2,64,1024]{2,1,0:T(8,128)(2,1)S(1)} %get-tuple-element.37), channel_id=1, source_target_pairs={{0,1},{1,0},{2,3},{3,2},{4,5},{5,4},{6,7},{7,6},{8,9},{9,8},{10,11... | collective-permute-start | bytes 786440 | tf_op jit(solution)/shard_map/ppermute | solution.py:31
  10.8 2.6 %collective-permute-start.1 = (bf16[2,64,1024]{2,1,0:T(8,128)(2,1)S(1)}, bf16[2,64,1024]{2,1,0:T(8,128)(2,1)S(1)}, u32[]{:S(2)}, u32[]{:S(2)}) collective-permute-start(bf16[2,64,1024]{2,1,0:T(8,128)(2,1)S(1)} %get-tuple-element.38), channel_id=1, source_target_pairs={{0,2},{1,3},{2,0},{3,1},{4,6},{5,7},{6,4},{7,5},{8,10},{9,11},{10,... | collective-permute-start | bytes 786440 | tf_op jit(solution)/shard_map/ppermute | solution.py:31
  13.6 7.7 %collective-permute-done.refs_1_ = bf16[2,64,1024]{2,1,0:T(8,128)(2,1)S(1)} collective-permute-done((bf16[2,64,1024]{2,1,0:T(8,128)(2,1)S(1)}, bf16[2,64,1024]{2,1,0:T(8,128)(2,1)S(1)}, u32[]{:S(2)}, u32[]{:S(2)}) %collective-permute-start) | collective-permute-done | bytes 262176 | tf_op jit(solution)/shard_map/ppermute | solution.py:31
  21.2 10.0 %collective-permute-done.8.refs_9_.refs_1_ = bf16[768,768]{1,0:T(8,128)(2,1)S(1)} collective-permute-done((bf16[768,768]{1,0:T(8,128)(2,1)S(1)}, bf16[768,768]{1,0:T(8,128)(2,1)S(1)}, u32[]{:S(2)}, u32[]{:S(2)}) %collective-permute-start.8) | collective-permute-done | bytes 1179680 | tf_op jit(solution)/shard_map/ppermute | solution.py:275
  31.2 1.6 %collective-permute-start.10 = (bf16[768,768]{1,0:T(8,128)(2,1)S(1)}, bf16[768,768]{1,0:T(8,128)(2,1)S(1)}, u32[]{:S(2)}, u32[]{:S(2)}) collective-permute-start(bf16[768,768]{1,0:T(8,128)(2,1)S(1)} %collective-permute-done.8.refs_9_.refs_1_), channel_id=1, source_target_pairs={{0,16},{4,12},{8,24},{12,4},{16,0},{20,28},{24,8},{28,20},{1,17},{... | collective-permute-start | bytes 3538952 | tf_op jit(solution)/shard_map/ppermute | solution.py:275
  35.5 1.7 %collective-permute-start.9 = (bf16[2,256,256]{2,1,0:T(8,128)(2,1)S(1)}, bf16[2,256,256]{2,1,0:T(8,128)(2,1)S(1)}, u32[]{:S(2)}, u32[]{:S(2)}) collective-permute-start(bf16[2,256,256]{2,1,0:T(8,128)(2,1)S(1)} %get-tuple-element.41), channel_id=1, source_target_pairs={{0,8},{4,20},{8,0},{12,28},{16,24},{20,4},{24,16},{28,12},{1,9},{5... | collective-permute-start | bytes 786440 | tf_op jit(solution)/shard_map/ppermute | solution.py:275
  38.3 6.5 %collective-permute-done.9.refs_8_ = bf16[2,256,256]{2,1,0:T(8,128)(2,1)S(1)} collective-permute-done((bf16[2,256,256]{2,1,0:T(8,128)(2,1)S(1)}, bf16[2,256,256]{2,1,0:T(8,128)(2,1)S(1)}, u32[]{:S(2)}, u32[]{:S(2)}) %collective-permute-start.9) | collective-permute-done | bytes 262176 | tf_op jit(solution)/shard_map/ppermute | solution.py:275
  44.8 5.4 %collective-permute-done.10.refs_9_.refs_3_ = bf16[768,768]{1,0:T(8,128)(2,1)S(1)} collective-permute-done((bf16[768,768]{1,0:T(8,128)(2,1)S(1)}, bf16[768,768]{1,0:T(8,128)(2,1)S(1)}, u32[]{:S(2)}, u32[]{:S(2)}) %collective-permute-start.10) | collective-permute-done | bytes 1179680 | tf_op jit(solution)/shard_map/ppermute | solution.py:275
  50.8 2.0 %collective-permute-done.11.got = bf16[128,2304]{1,0:T(8,128)(2,1)S(1)} collective-permute-done((bf16[128,2304]{1,0:T(8,128)(2,1)S(1)}, bf16[128,2304]{1,0:T(8,128)(2,1)S(1)}, u32[]{:S(2)}, u32[]{:S(2)}) %collective-permute-start.11) | collective-permute-done | bytes 589856 | tf_op jit(solution)/shard_map/ppermute | solution.py:31
  53.4 1.6 %collective-permute-start.21 = (bf16[128,2304]{1,0:T(8,128)(2,1)S(1)}, bf16[128,2304]{1,0:T(8,128)(2,1)S(1)}, u32[]{:S(2)}, u32[]{:S(2)}) collective-permute-start(bf16[128,2304]{1,0:T(8,128)(2,1)S(1)} %get-tuple-element.46.deltas.refs_10_), channel_id=1, source_target_pairs={{0,16},{4,12},{8,24},{12,4},{16,0},{20,28},{24,8},{28,20},{1,17},{... | collective-permute-start | bytes 1769480 | tf_op jit(solution)/shard_map/ppermute | solution.py:275
  55.0 1.6 %collective-permute-start.20 = (bf16[128,2304]{1,0:T(8,128)(2,1)S(1)}, bf16[128,2304]{1,0:T(8,128)(2,1)S(1)}, u32[]{:S(2)}, u32[]{:S(2)}) collective-permute-start(bf16[128,2304]{1,0:T(8,128)(2,1)S(1)} %get-tuple-element.46.deltas.refs_10_), channel_id=1, source_target_pairs={{0,8},{4,20},{8,0},{12,28},{16,24},{20,4},{24,16},{28,12},{1,9},{5... | collective-permute-start | bytes 1769480 | tf_op jit(solution)/shard_map/ppermute | solution.py:275
  57.6 1.6 %collective-permute-start.13 = (bf16[2,32,1152]{2,1,0:T(8,128)(2,1)S(1)}, bf16[2,32,1152]{2,1,0:T(8,128)(2,1)S(1)}, u32[]{:S(2)}, u32[]{:S(2)}) collective-permute-start(bf16[2,32,1152]{2,1,0:T(8,128)(2,1)S(1)} %get-tuple-element.49), channel_id=1, source_target_pairs={{0,1},{1,0},{2,3},{3,2},{4,5},{5,4},{6,7},{7,6},{8,9},{9,8},{10,11... | collective-permute-start | bytes 442376 | tf_op jit(solution)/shard_map/ppermute | solution.py:31
  59.3 2.6 %collective-permute-start.14 = (bf16[2,32,1152]{2,1,0:T(8,128)(2,1)S(1)}, bf16[2,32,1152]{2,1,0:T(8,128)(2,1)S(1)}, u32[]{:S(2)}, u32[]{:S(2)}) collective-permute-start(bf16[2,32,1152]{2,1,0:T(8,128)(2,1)S(1)} %get-tuple-element.50), channel_id=1, source_target_pairs={{0,2},{1,3},{2,0},{3,1},{4,6},{5,7},{6,4},{7,5},{8,10},{9,11},{10,... | collective-permute-start | bytes 442376 | tf_op jit(solution)/shard_map/ppermute | solution.py:31
  63.2 4.8 %collective-permute-done.21.refs_14_ = bf16[128,2304]{1,0:T(8,128)(2,1)S(1)} collective-permute-done((bf16[128,2304]{1,0:T(8,128)(2,1)S(1)}, bf16[128,2304]{1,0:T(8,128)(2,1)S(1)}, u32[]{:S(2)}, u32[]{:S(2)}) %collective-permute-start.21) | collective-permute-done | bytes 589856 | tf_op jit(solution)/shard_map/ppermute | solution.py:275
  68.7 2.6 %collective-permute-done.20.refs_12_ = bf16[128,2304]{1,0:T(8,128)(2,1)S(1)} collective-permute-done((bf16[128,2304]{1,0:T(8,128)(2,1)S(1)}, bf16[128,2304]{1,0:T(8,128)(2,1)S(1)}, u32[]{:S(2)}, u32[]{:S(2)}) %collective-permute-start.20) | collective-permute-done | bytes 589856 | tf_op jit(solution)/shard_map/ppermute | solution.py:275
  72.4 1.6 %collective-permute-start.26 = (bf16[128,2304]{1,0:T(8,128)(2,1)S(1)}, bf16[128,2304]{1,0:T(8,128)(2,1)S(1)}, u32[]{:S(2)}, u32[]{:S(2)}) collective-permute-start(bf16[128,2304]{1,0:T(8,128)(2,1)S(1)} %collective-permute-done.20.refs_12_), channel_id=1, source_target_pairs={{0,16},{4,12},{8,24},{12,4},{16,0},{20,28},{24,8},{28,20},{1,17},{... | collective-permute-start | bytes 1769480 | tf_op jit(solution)/shard_map/ppermute | solution.py:275
  74.0 1.8 %collective-permute-start.24 = (bf16[2,256,256]{2,1,0:T(8,128)(2,1)S(1)}, bf16[2,256,256]{2,1,0:T(8,128)(2,1)S(1)}, u32[]{:S(2)}, u32[]{:S(2)}) collective-permute-start(bf16[2,256,256]{2,1,0:T(8,128)(2,1)S(1)} %get-tuple-element.55), channel_id=1, source_target_pairs={{0,24},{4,28},{8,16},{12,20},{16,8},{20,12},{24,0},{28,4},{1,25},{... | collective-permute-start | bytes 786440 | tf_op jit(solution)/shard_map/ppermute | solution.py:275
  75.8 3.9 %collective-permute-start.15 = (bf16[2,32,1152]{2,1,0:T(8,128)(2,1)S(1)}, bf16[2,32,1152]{2,1,0:T(8,128)(2,1)S(1)}, u32[]{:S(2)}, u32[]{:S(2)}) collective-permute-start(bf16[2,32,1152]{2,1,0:T(8,128)(2,1)S(1)} %get-tuple-element.51), channel_id=1, source_target_pairs={{0,3},{1,2},{2,1},{3,0},{4,7},{5,6},{6,5},{7,4},{8,11},{9,10},{10,... | collective-permute-start | bytes 442376 | tf_op jit(solution)/shard_map/ppermute | solution.py:31
  81.3 2.9 %collective-permute-done.24.refs_1_ = bf16[2,256,256]{2,1,0:T(8,128)(2,1)S(1)} collective-permute-done((bf16[2,256,256]{2,1,0:T(8,128)(2,1)S(1)}, bf16[2,256,256]{2,1,0:T(8,128)(2,1)S(1)}, u32[]{:S(2)}, u32[]{:S(2)}) %collective-permute-start.24) | collective-permute-done | bytes 262176 | tf_op jit(solution)/shard_map/ppermute | solution.py:275
  84.1 3.3 %collective-permute-start.18 = (bf16[2,32,1152]{2,1,0:T(8,128)(2,1)S(1)}, bf16[2,32,1152]{2,1,0:T(8,128)(2,1)S(1)}, u32[]{:S(2)}, u32[]{:S(2)}) collective-permute-start(bf16[2,32,1152]{2,1,0:T(8,128)(2,1)S(1)} %collective-permute-done.14.refs_2_), channel_id=1, source_target_pairs={{0,4},{4,0},{8,12},{12,8},{16,20},{20,16},{24,28},{28,24},{1,5},{5... | collective-permute-start | bytes 442376 | tf_op jit(solution)/shard_map/ppermute | solution.py:31
  89.0 2.0 %shard_map.118 = (bf16[256,2048]{1,0:T(8,128)(2,1)}, bf16[8,256]{1,0:T(8,128)(2,1)}) custom-call(s32[2]{0:T(128)S(1)} %pad_add_fusion.pos, s32[8,256]{1,0:T(8,128)S(1)} %bitcast.12, bf16[8,256]{1,0:T(8,128)(2,1)S(1)} %bitcast.14, bf16[128,256]{1,0:T(8,128)(2,1)S(1)} %get-tuple-element.35.select, bf16[2,32,1152]{2,1,0:T(8,128)(2,1)S(1)} %get-tuple-element.48.refs_0_, ...), custom_call_target="tpu_custom_call" | custom-call | tf_op jit(solution)/shard_map/pallas_call | solution.py:257
  (47 shorter events, 15.3 us)
Async XLA Ops:
  1.9 29.3 %collective-permute-start.8 = (bf16[768,768]{1,0:T(8,128)(2,1)S(1)}, bf16[768,768]{1,0:T(8,128)(2,1)S(1)}, u32[]{:S(2)}, u32[]{:S(2)}) collective-permute-start(bf16[768,768]{1,0:T(8,128)(2,1)S(1)} %shard_map.111.refs_8_.refs_0_), channel_id=1, source_target_pairs={{0,8},{4,20},{8,0},{12,28},{16,24},{20,4},{24,16},{28,12},{1,9},{5... | collective-permute-start | bytes 3538952 | tf_op jit(solution)/shard_map/ppermute | solution.py:275
  4.9 28.4 %collective-permute-start.3 = (bf16[768,768]{1,0:T(8,128)(2,1)S(1)}, bf16[768,768]{1,0:T(8,128)(2,1)S(1)}, u32[]{:S(2)}, u32[]{:S(2)}) collective-permute-start(bf16[768,768]{1,0:T(8,128)(2,1)S(1)} %shard_map.111.refs_8_.refs_0_), channel_id=1, source_target_pairs={{0,16},{4,12},{8,24},{12,4},{16,0},{20,28},{24,8},{28,20},{1,17},{... | collective-permute-start | bytes 3538952 | tf_op jit(solution)/shard_map/ppermute | solution.py:275
  9.1 12.1 %collective-permute-start = (bf16[2,64,1024]{2,1,0:T(8,128)(2,1)S(1)}, bf16[2,64,1024]{2,1,0:T(8,128)(2,1)S(1)}, u32[]{:S(2)}, u32[]{:S(2)}) collective-permute-start(bf16[2,64,1024]{2,1,0:T(8,128)(2,1)S(1)} %get-tuple-element.37), channel_id=1, source_target_pairs={{0,1},{1,0},{2,3},{3,2},{4,5},{5,4},{6,7},{7,6},{8,9},{9,8},{10,11... | collective-permute-start | bytes 786440 | tf_op jit(solution)/shard_map/ppermute | solution.py:31
  10.8 22.0 %collective-permute-start.1 = (bf16[2,64,1024]{2,1,0:T(8,128)(2,1)S(1)}, bf16[2,64,1024]{2,1,0:T(8,128)(2,1)S(1)}, u32[]{:S(2)}, u32[]{:S(2)}) collective-permute-start(bf16[2,64,1024]{2,1,0:T(8,128)(2,1)S(1)} %get-tuple-element.38), channel_id=1, source_target_pairs={{0,2},{1,3},{2,0},{3,1},{4,6},{5,7},{6,4},{7,5},{8,10},{9,11},{10,... | collective-permute-start | bytes 786440 | tf_op jit(solution)/shard_map/ppermute | solution.py:31
  13.3 19.9 %collective-permute-start.2 = (bf16[2,64,1024]{2,1,0:T(8,128)(2,1)S(1)}, bf16[2,64,1024]{2,1,0:T(8,128)(2,1)S(1)}, u32[]{:S(2)}, u32[]{:S(2)}) collective-permute-start(bf16[2,64,1024]{2,1,0:T(8,128)(2,1)S(1)} %get-tuple-element.39), channel_id=1, source_target_pairs={{0,3},{1,2},{2,1},{3,0},{4,7},{5,6},{6,5},{7,4},{8,11},{9,10},{10,... | collective-permute-start | bytes 786440 | tf_op jit(solution)/shard_map/ppermute | solution.py:31
  31.2 19.0 %collective-permute-start.10 = (bf16[768,768]{1,0:T(8,128)(2,1)S(1)}, bf16[768,768]{1,0:T(8,128)(2,1)S(1)}, u32[]{:S(2)}, u32[]{:S(2)}) collective-permute-start(bf16[768,768]{1,0:T(8,128)(2,1)S(1)} %collective-permute-done.8.refs_9_.refs_1_), channel_id=1, source_target_pairs={{0,16},{4,12},{8,24},{12,4},{16,0},{20,28},{24,8},{28,20},{1,17},{... | collective-permute-start | bytes 3538952 | tf_op jit(solution)/shard_map/ppermute | solution.py:275
  33.3 2.1 %collective-permute-start.4 = (bf16[2,64,1024]{2,1,0:T(8,128)(2,1)S(1)}, bf16[2,64,1024]{2,1,0:T(8,128)(2,1)S(1)}, u32[]{:S(2)}, u32[]{:S(2)}) collective-permute-start(bf16[2,64,1024]{2,1,0:T(8,128)(2,1)S(1)} %get-tuple-element.40.refs_0_), channel_id=1, source_target_pairs={{0,4},{4,0},{8,12},{12,8},{16,20},{20,16},{24,28},{28,24},{1,5},{5... | collective-permute-start | bytes 786440 | tf_op jit(solution)/shard_map/ppermute | solution.py:31
  35.5 9.3 %collective-permute-start.9 = (bf16[2,256,256]{2,1,0:T(8,128)(2,1)S(1)}, bf16[2,256,256]{2,1,0:T(8,128)(2,1)S(1)}, u32[]{:S(2)}, u32[]{:S(2)}) collective-permute-start(bf16[2,256,256]{2,1,0:T(8,128)(2,1)S(1)} %get-tuple-element.41), channel_id=1, source_target_pairs={{0,8},{4,20},{8,0},{12,28},{16,24},{20,4},{24,16},{28,12},{1,9},{5... | collective-permute-start | bytes 786440 | tf_op jit(solution)/shard_map/ppermute | solution.py:275
  50.7 2.1 %collective-permute-start.11 = (bf16[128,2304]{1,0:T(8,128)(2,1)S(1)}, bf16[128,2304]{1,0:T(8,128)(2,1)S(1)}, u32[]{:S(2)}, u32[]{:S(2)}) collective-permute-start(bf16[128,2304]{1,0:T(8,128)(2,1)S(1)} %get-tuple-element.45), channel_id=1, source_target_pairs={{0,4},{4,0},{8,12},{12,8},{16,20},{20,16},{24,28},{28,24},{1,5},{5... | collective-permute-start | bytes 1769480 | tf_op jit(solution)/shard_map/ppermute | solution.py:31
  53.2 3.4 %collective-permute-start.12 = (bf16[128,2304]{1,0:T(8,128)(2,1)S(1)}, bf16[128,2304]{1,0:T(8,128)(2,1)S(1)}, u32[]{:S(2)}, u32[]{:S(2)}) collective-permute-start(bf16[128,2304]{1,0:T(8,128)(2,1)S(1)} %get-tuple-element.46.deltas.refs_10_), channel_id=1, source_target_pairs={{0,4},{4,0},{8,12},{12,8},{16,20},{20,16},{24,28},{28,24},{1,5},{5... | collective-permute-start | bytes 1769480 | tf_op jit(solution)/shard_map/ppermute | solution.py:31
  53.4 14.6 %collective-permute-start.21 = (bf16[128,2304]{1,0:T(8,128)(2,1)S(1)}, bf16[128,2304]{1,0:T(8,128)(2,1)S(1)}, u32[]{:S(2)}, u32[]{:S(2)}) collective-permute-start(bf16[128,2304]{1,0:T(8,128)(2,1)S(1)} %get-tuple-element.46.deltas.refs_10_), channel_id=1, source_target_pairs={{0,16},{4,12},{8,24},{12,4},{16,0},{20,28},{24,8},{28,20},{1,17},{... | collective-permute-start | bytes 1769480 | tf_op jit(solution)/shard_map/ppermute | solution.py:275
  55.0 16.3 %collective-permute-start.20 = (bf16[128,2304]{1,0:T(8,128)(2,1)S(1)}, bf16[128,2304]{1,0:T(8,128)(2,1)S(1)}, u32[]{:S(2)}, u32[]{:S(2)}) collective-permute-start(bf16[128,2304]{1,0:T(8,128)(2,1)S(1)} %get-tuple-element.46.deltas.refs_10_), channel_id=1, source_target_pairs={{0,8},{4,20},{8,0},{12,28},{16,24},{20,4},{24,16},{28,12},{1,9},{5... | collective-permute-start | bytes 1769480 | tf_op jit(solution)/shard_map/ppermute | solution.py:275
  57.6 10.3 %collective-permute-start.13 = (bf16[2,32,1152]{2,1,0:T(8,128)(2,1)S(1)}, bf16[2,32,1152]{2,1,0:T(8,128)(2,1)S(1)}, u32[]{:S(2)}, u32[]{:S(2)}) collective-permute-start(bf16[2,32,1152]{2,1,0:T(8,128)(2,1)S(1)} %get-tuple-element.49), channel_id=1, source_target_pairs={{0,1},{1,0},{2,3},{3,2},{4,5},{5,4},{6,7},{7,6},{8,9},{9,8},{10,11... | collective-permute-start | bytes 442376 | tf_op jit(solution)/shard_map/ppermute | solution.py:31
  59.3 9.4 %collective-permute-start.14 = (bf16[2,32,1152]{2,1,0:T(8,128)(2,1)S(1)}, bf16[2,32,1152]{2,1,0:T(8,128)(2,1)S(1)}, u32[]{:S(2)}, u32[]{:S(2)}) collective-permute-start(bf16[2,32,1152]{2,1,0:T(8,128)(2,1)S(1)} %get-tuple-element.50), channel_id=1, source_target_pairs={{0,2},{1,3},{2,0},{3,1},{4,6},{5,7},{6,4},{7,5},{8,10},{9,11},{10,... | collective-permute-start | bytes 442376 | tf_op jit(solution)/shard_map/ppermute | solution.py:31
  61.9 10.6 %collective-permute-start.19 = (bf16[2,256,256]{2,1,0:T(8,128)(2,1)S(1)}, bf16[2,256,256]{2,1,0:T(8,128)(2,1)S(1)}, u32[]{:S(2)}, u32[]{:S(2)}) collective-permute-start(bf16[2,256,256]{2,1,0:T(8,128)(2,1)S(1)} %get-tuple-element.52), channel_id=1, source_target_pairs={{0,16},{4,12},{8,24},{12,4},{16,0},{20,28},{24,8},{28,20},{1,17},{... | collective-permute-start | bytes 786440 | tf_op jit(solution)/shard_map/ppermute | solution.py:275
  68.7 11.0 %collective-permute-start.22 = (bf16[128,2304]{1,0:T(8,128)(2,1)S(1)}, bf16[128,2304]{1,0:T(8,128)(2,1)S(1)}, u32[]{:S(2)}, u32[]{:S(2)}) collective-permute-start(bf16[128,2304]{1,0:T(8,128)(2,1)S(1)} %collective-permute-done.21.refs_14_), channel_id=1, source_target_pairs={{0,4},{4,0},{8,12},{12,8},{16,20},{20,16},{24,28},{28,24},{1,5},{5... | collective-permute-start | bytes 1769480 | tf_op jit(solution)/shard_map/ppermute | solution.py:31
  71.2 8.4 %collective-permute-start.23 = (bf16[128,2304]{1,0:T(8,128)(2,1)S(1)}, bf16[128,2304]{1,0:T(8,128)(2,1)S(1)}, u32[]{:S(2)}, u32[]{:S(2)}) collective-permute-start(bf16[128,2304]{1,0:T(8,128)(2,1)S(1)} %collective-permute-done.20.refs_12_), channel_id=1, source_target_pairs={{0,4},{4,0},{8,12},{12,8},{16,20},{20,16},{24,28},{28,24},{1,5},{5... | collective-permute-start | bytes 1769480 | tf_op jit(solution)/shard_map/ppermute | solution.py:31
  72.4 16.0 %collective-permute-start.26 = (bf16[128,2304]{1,0:T(8,128)(2,1)S(1)}, bf16[128,2304]{1,0:T(8,128)(2,1)S(1)}, u32[]{:S(2)}, u32[]{:S(2)}) collective-permute-start(bf16[128,2304]{1,0:T(8,128)(2,1)S(1)} %collective-permute-done.20.refs_12_), channel_id=1, source_target_pairs={{0,16},{4,12},{8,24},{12,4},{16,0},{20,28},{24,8},{28,20},{1,17},{... | collective-permute-start | bytes 1769480 | tf_op jit(solution)/shard_map/ppermute | solution.py:275
  74.0 10.1 %collective-permute-start.24 = (bf16[2,256,256]{2,1,0:T(8,128)(2,1)S(1)}, bf16[2,256,256]{2,1,0:T(8,128)(2,1)S(1)}, u32[]{:S(2)}, u32[]{:S(2)}) collective-permute-start(bf16[2,256,256]{2,1,0:T(8,128)(2,1)S(1)} %get-tuple-element.55), channel_id=1, source_target_pairs={{0,24},{4,28},{8,16},{12,20},{16,8},{20,12},{24,0},{28,4},{1,25},{... | collective-permute-start | bytes 786440 | tf_op jit(solution)/shard_map/ppermute | solution.py:275
  75.8 11.6 %collective-permute-start.15 = (bf16[2,32,1152]{2,1,0:T(8,128)(2,1)S(1)}, bf16[2,32,1152]{2,1,0:T(8,128)(2,1)S(1)}, u32[]{:S(2)}, u32[]{:S(2)}) collective-permute-start(bf16[2,32,1152]{2,1,0:T(8,128)(2,1)S(1)} %get-tuple-element.51), channel_id=1, source_target_pairs={{0,3},{1,2},{2,1},{3,0},{4,7},{5,6},{6,5},{7,4},{8,11},{9,10},{10,... | collective-permute-start | bytes 442376 | tf_op jit(solution)/shard_map/ppermute | solution.py:31
  79.6 7.8 %collective-permute-start.16 = (bf16[2,32,1152]{2,1,0:T(8,128)(2,1)S(1)}, bf16[2,32,1152]{2,1,0:T(8,128)(2,1)S(1)}, u32[]{:S(2)}, u32[]{:S(2)}) collective-permute-start(bf16[2,32,1152]{2,1,0:T(8,128)(2,1)S(1)} %get-tuple-element.48.refs_0_), channel_id=1, source_target_pairs={{0,4},{4,0},{8,12},{12,8},{16,20},{20,16},{24,28},{28,24},{1,5},{5... | collective-permute-start | bytes 442376 | tf_op jit(solution)/shard_map/ppermute | solution.py:31
  79.6 7.8 %collective-permute-start.17 = (bf16[2,32,1152]{2,1,0:T(8,128)(2,1)S(1)}, bf16[2,32,1152]{2,1,0:T(8,128)(2,1)S(1)}, u32[]{:S(2)}, u32[]{:S(2)}) collective-permute-start(bf16[2,32,1152]{2,1,0:T(8,128)(2,1)S(1)} %collective-permute-done.13.refs_1_), channel_id=1, source_target_pairs={{0,4},{4,0},{8,12},{12,8},{16,20},{20,16},{24,28},{28,24},{1,5},{5... | collective-permute-start | bytes 442376 | tf_op jit(solution)/shard_map/ppermute | solution.py:31
  84.1 4.3 %collective-permute-start.18 = (bf16[2,32,1152]{2,1,0:T(8,128)(2,1)S(1)}, bf16[2,32,1152]{2,1,0:T(8,128)(2,1)S(1)}, u32[]{:S(2)}, u32[]{:S(2)}) collective-permute-start(bf16[2,32,1152]{2,1,0:T(8,128)(2,1)S(1)} %collective-permute-done.14.refs_2_), channel_id=1, source_target_pairs={{0,4},{4,0},{8,12},{12,8},{16,20},{20,16},{24,28},{28,24},{1,5},{5... | collective-permute-start | bytes 442376 | tf_op jit(solution)/shard_map/ppermute | solution.py:31
  88.8 2.2 %collective-permute-start.27 = (bf16[128,2304]{1,0:T(8,128)(2,1)S(1)}, bf16[128,2304]{1,0:T(8,128)(2,1)S(1)}, u32[]{:S(2)}, u32[]{:S(2)}) collective-permute-start(bf16[128,2304]{1,0:T(8,128)(2,1)S(1)} %collective-permute-done.26.refs_2_), channel_id=1, source_target_pairs={{0,4},{4,0},{8,12},{12,8},{16,20},{20,16},{24,28},{28,24},{1,5},{5... | collective-permute-start | bytes 1769480 | tf_op jit(solution)/shard_map/ppermute | solution.py:31
  (6 other events, 18.4 us)

commit v5 on v4

--- a/solution.py
+++ b/solution.py
@@ -383,7 +383,7 @@
         )
 
     part = weight_sums(early, ())[0]
-    back_other = [hop(after(x, part, got[-1]) if k == n_e - 1 else x, "fsdp", 1) for k, x in enumerate(back)]
+    back_other = [hop(after(x, part) if k == n_e - 1 else x, "fsdp", 1) for k, x in enumerate(back)]
     in_grad, gate_grad = call(
         final_kernel,
         (pos, ids, gates, select, *back, *back_other),
@@ -395,8 +395,8 @@
     )
 
     for p in late:
-        deltas_other[p] = hop(after(deltas[p], part, *back_other), "fsdp", 1)
-    grads = weight_sums(late, [after(part, in_grad)])
+        deltas_other[p] = hop(after(deltas[p], part, in_grad, got[-1]), "fsdp", 1)
+    grads = weight_sums(late, [part])
     return (in_grad, gate_grad.T, *(g[:, None] for g in grads))
 
 

time: 92.5 us -> 91.4 us (0.988)
  starting transfers between devices: 33.6 us -> 30.4 us
  waiting for transfers between devices: 46.5 us -> 48.7 us
    ppermute x19, starting transfers between devices: 18 us -> 14.6 us  [hop(): lax.ppermute(x, axis, [(i, i ^ offset) for i in range(lax.axis_size(axis))])]
    ppermute x19, waiting for transfers between devices: 13.3 us -> 15.9 us  [hop(): lax.ppermute(x, axis, [(i, i ^ offset) for i in range(lax.axis_size(axis))])]
  transfers between devices with their start and end apart: 28 -> 28, of which waited for: 16 -> 19; matrix products, arithmetic and copies ran while one was open for 0% -> 0% of each run, Pallas kernels for 9% -> 9%
where the time goes in v5:
time: 91.4 us; the launch traced here: 91.3 us
  waiting for transfers between devices  48.7 us (53%)
  starting transfers between devices  30.4 us (33%)
  Pallas kernels  11.4 us (12%)
    ppermute x9, waiting for transfers between devices, to(): lax.ppermute(x, 'fsdp', [(i, i ^ flips(position, i & 1, bits)) for i in r...  32.8 us
    ppermute x19, waiting for transfers between devices, hop(): lax.ppermute(x, axis, [(i, i ^ offset) for i in range(lax.axis_size(axis))])  15.9 us
    ppermute x9, starting transfers between devices, to(): lax.ppermute(x, 'fsdp', [(i, i ^ flips(position, i & 1, bits)) for i in r...  15.7 us
    ppermute x19, starting transfers between devices, hop(): lax.ppermute(x, axis, [(i, i ^ offset) for i in range(lax.axis_size(axis))])  14.6 us
    pallas_call x10, Pallas kernels, call(): pl.pallas_call(functools.partial(kernel, **static), out_shape=outs, in_sp...  11.4 us
  transfers between devices with their start and end apart: 28, of which 19 were waited for; matrix products, arithmetic and copies ran while one was open for 0% of the time, Pallas kernels for 9%

profile of v5, /device:TPU:0, one launch (start us, length us, event | category | flops | bytes accessed | tf_op | source)
XLA Modules:
  0.0 91.3 jit_solution(4330084341170303511)
XLA Ops:
  1.9 3.0 %collective-permute-start.8 = (bf16[768,768]{1,0:T(8,128)(2,1)S(1)}, bf16[768,768]{1,0:T(8,128)(2,1)S(1)}, u32[]{:S(2)}, u32[]{:S(2)}) collective-permute-start(bf16[768,768]{1,0:T(8,128)(2,1)S(1)} %shard_map.111.refs_8_.refs_0_), channel_id=1, source_target_pairs={{0,8},{4,20},{8,0},{12,28},{16,24},{20,4},{24,16},{28,12},{1,9},{5... | collective-permute-start | bytes 3538952 | tf_op jit(solution)/shard_map/ppermute | solution.py:275
  4.9 1.5 %collective-permute-start.3 = (bf16[768,768]{1,0:T(8,128)(2,1)S(1)}, bf16[768,768]{1,0:T(8,128)(2,1)S(1)}, u32[]{:S(2)}, u32[]{:S(2)}) collective-permute-start(bf16[768,768]{1,0:T(8,128)(2,1)S(1)} %shard_map.111.refs_8_.refs_0_), channel_id=1, source_target_pairs={{0,16},{4,12},{8,24},{12,4},{16,0},{20,28},{24,8},{28,20},{1,17},{... | collective-permute-start | bytes 3538952 | tf_op jit(solution)/shard_map/ppermute | solution.py:275
  6.5 2.6 %shard_map.110 = (bf16[2,64,1024]{2,1,0:T(8,128)(2,1)S(1)}, bf16[2,64,1024]{2,1,0:T(8,128)(2,1)S(1)}, bf16[2,64,1024]{2,1,0:T(8,128)(2,1)S(1)}, bf16[2,64,1024]{2,1,0:T(8,128)(2,1)S(1)}, bf16[128,256]{1,0:T(8,128)(2,1)S(1)}) custom-call(s32[2]{0:T(128)S(1)} %pad_add_fusion.pos, s32[8,256]{1,0:T(8,128)S(1)} %bitcast.11, bf16[8,256]{1,0:T(8,128)(2,1)S(1)} %bitcast.13, ...), custom_call_target="tpu_custom_call" | custom-call | tf_op jit(solution)/shard_map/pallas_call | solution.py:257
  9.1 1.6 %collective-permute-start = (bf16[2,64,1024]{2,1,0:T(8,128)(2,1)S(1)}, bf16[2,64,1024]{2,1,0:T(8,128)(2,1)S(1)}, u32[]{:S(2)}, u32[]{:S(2)}) collective-permute-start(bf16[2,64,1024]{2,1,0:T(8,128)(2,1)S(1)} %get-tuple-element.36), channel_id=1, source_target_pairs={{0,1},{1,0},{2,3},{3,2},{4,5},{5,4},{6,7},{7,6},{8,9},{9,8},{10,11... | collective-permute-start | bytes 786440 | tf_op jit(solution)/shard_map/ppermute | solution.py:31
  10.8 2.6 %collective-permute-start.1 = (bf16[2,64,1024]{2,1,0:T(8,128)(2,1)S(1)}, bf16[2,64,1024]{2,1,0:T(8,128)(2,1)S(1)}, u32[]{:S(2)}, u32[]{:S(2)}) collective-permute-start(bf16[2,64,1024]{2,1,0:T(8,128)(2,1)S(1)} %get-tuple-element.37), channel_id=1, source_target_pairs={{0,2},{1,3},{2,0},{3,1},{4,6},{5,7},{6,4},{7,5},{8,10},{9,11},{10,... | collective-permute-start | bytes 786440 | tf_op jit(solution)/shard_map/ppermute | solution.py:31
  13.6 7.7 %collective-permute-done.refs_1_ = bf16[2,64,1024]{2,1,0:T(8,128)(2,1)S(1)} collective-permute-done((bf16[2,64,1024]{2,1,0:T(8,128)(2,1)S(1)}, bf16[2,64,1024]{2,1,0:T(8,128)(2,1)S(1)}, u32[]{:S(2)}, u32[]{:S(2)}) %collective-permute-start) | collective-permute-done | bytes 262176 | tf_op jit(solution)/shard_map/ppermute | solution.py:31
  21.2 10.0 %collective-permute-done.8.refs_9_.refs_1_ = bf16[768,768]{1,0:T(8,128)(2,1)S(1)} collective-permute-done((bf16[768,768]{1,0:T(8,128)(2,1)S(1)}, bf16[768,768]{1,0:T(8,128)(2,1)S(1)}, u32[]{:S(2)}, u32[]{:S(2)}) %collective-permute-start.8) | collective-permute-done | bytes 1179680 | tf_op jit(solution)/shard_map/ppermute | solution.py:275
  31.2 1.6 %collective-permute-start.10 = (bf16[768,768]{1,0:T(8,128)(2,1)S(1)}, bf16[768,768]{1,0:T(8,128)(2,1)S(1)}, u32[]{:S(2)}, u32[]{:S(2)}) collective-permute-start(bf16[768,768]{1,0:T(8,128)(2,1)S(1)} %collective-permute-done.8.refs_9_.refs_1_), channel_id=1, source_target_pairs={{0,16},{4,12},{8,24},{12,4},{16,0},{20,28},{24,8},{28,20},{1,17},{... | collective-permute-start | bytes 3538952 | tf_op jit(solution)/shard_map/ppermute | solution.py:275
  35.5 1.7 %collective-permute-start.9 = (bf16[2,256,256]{2,1,0:T(8,128)(2,1)S(1)}, bf16[2,256,256]{2,1,0:T(8,128)(2,1)S(1)}, u32[]{:S(2)}, u32[]{:S(2)}) collective-permute-start(bf16[2,256,256]{2,1,0:T(8,128)(2,1)S(1)} %get-tuple-element.40), channel_id=1, source_target_pairs={{0,8},{4,20},{8,0},{12,28},{16,24},{20,4},{24,16},{28,12},{1,9},{5... | collective-permute-start | bytes 786440 | tf_op jit(solution)/shard_map/ppermute | solution.py:275
  38.3 6.5 %collective-permute-done.9.refs_8_ = bf16[2,256,256]{2,1,0:T(8,128)(2,1)S(1)} collective-permute-done((bf16[2,256,256]{2,1,0:T(8,128)(2,1)S(1)}, bf16[2,256,256]{2,1,0:T(8,128)(2,1)S(1)}, u32[]{:S(2)}, u32[]{:S(2)}) %collective-permute-start.9) | collective-permute-done | bytes 262176 | tf_op jit(solution)/shard_map/ppermute | solution.py:275
  44.8 5.4 %collective-permute-done.10.refs_9_.refs_3_ = bf16[768,768]{1,0:T(8,128)(2,1)S(1)} collective-permute-done((bf16[768,768]{1,0:T(8,128)(2,1)S(1)}, bf16[768,768]{1,0:T(8,128)(2,1)S(1)}, u32[]{:S(2)}, u32[]{:S(2)}) %collective-permute-start.10) | collective-permute-done | bytes 1179680 | tf_op jit(solution)/shard_map/ppermute | solution.py:275
  50.8 2.0 %collective-permute-done.11.got = bf16[128,2304]{1,0:T(8,128)(2,1)S(1)} collective-permute-done((bf16[128,2304]{1,0:T(8,128)(2,1)S(1)}, bf16[128,2304]{1,0:T(8,128)(2,1)S(1)}, u32[]{:S(2)}, u32[]{:S(2)}) %collective-permute-start.11) | collective-permute-done | bytes 589856 | tf_op jit(solution)/shard_map/ppermute | solution.py:31
  53.4 1.6 %collective-permute-start.21 = (bf16[128,2304]{1,0:T(8,128)(2,1)S(1)}, bf16[128,2304]{1,0:T(8,128)(2,1)S(1)}, u32[]{:S(2)}, u32[]{:S(2)}) collective-permute-start(bf16[128,2304]{1,0:T(8,128)(2,1)S(1)} %get-tuple-element.45.deltas.refs_10_), channel_id=1, source_target_pairs={{0,16},{4,12},{8,24},{12,4},{16,0},{20,28},{24,8},{28,20},{1,17},{... | collective-permute-start | bytes 1769480 | tf_op jit(solution)/shard_map/ppermute | solution.py:275
  55.0 1.6 %collective-permute-start.20 = (bf16[128,2304]{1,0:T(8,128)(2,1)S(1)}, bf16[128,2304]{1,0:T(8,128)(2,1)S(1)}, u32[]{:S(2)}, u32[]{:S(2)}) collective-permute-start(bf16[128,2304]{1,0:T(8,128)(2,1)S(1)} %get-tuple-element.45.deltas.refs_10_), channel_id=1, source_target_pairs={{0,8},{4,20},{8,0},{12,28},{16,24},{20,4},{24,16},{28,12},{1,9},{5... | collective-permute-start | bytes 1769480 | tf_op jit(solution)/shard_map/ppermute | solution.py:275
  57.6 1.6 %collective-permute-start.13 = (bf16[2,32,1152]{2,1,0:T(8,128)(2,1)S(1)}, bf16[2,32,1152]{2,1,0:T(8,128)(2,1)S(1)}, u32[]{:S(2)}, u32[]{:S(2)}) collective-permute-start(bf16[2,32,1152]{2,1,0:T(8,128)(2,1)S(1)} %get-tuple-element.48), channel_id=1, source_target_pairs={{0,1},{1,0},{2,3},{3,2},{4,5},{5,4},{6,7},{7,6},{8,9},{9,8},{10,11... | collective-permute-start | bytes 442376 | tf_op jit(solution)/shard_map/ppermute | solution.py:31
  59.3 2.6 %collective-permute-start.14 = (bf16[2,32,1152]{2,1,0:T(8,128)(2,1)S(1)}, bf16[2,32,1152]{2,1,0:T(8,128)(2,1)S(1)}, u32[]{:S(2)}, u32[]{:S(2)}) collective-permute-start(bf16[2,32,1152]{2,1,0:T(8,128)(2,1)S(1)} %get-tuple-element.49), channel_id=1, source_target_pairs={{0,2},{1,3},{2,0},{3,1},{4,6},{5,7},{6,4},{7,5},{8,10},{9,11},{10,... | collective-permute-start | bytes 442376 | tf_op jit(solution)/shard_map/ppermute | solution.py:31
  63.2 4.8 %collective-permute-done.21.refs_14_ = bf16[128,2304]{1,0:T(8,128)(2,1)S(1)} collective-permute-done((bf16[128,2304]{1,0:T(8,128)(2,1)S(1)}, bf16[128,2304]{1,0:T(8,128)(2,1)S(1)}, u32[]{:S(2)}, u32[]{:S(2)}) %collective-permute-start.21) | collective-permute-done | bytes 589856 | tf_op jit(solution)/shard_map/ppermute | solution.py:275
  68.7 2.6 %collective-permute-done.20.refs_12_ = bf16[128,2304]{1,0:T(8,128)(2,1)S(1)} collective-permute-done((bf16[128,2304]{1,0:T(8,128)(2,1)S(1)}, bf16[128,2304]{1,0:T(8,128)(2,1)S(1)}, u32[]{:S(2)}, u32[]{:S(2)}) %collective-permute-start.20) | collective-permute-done | bytes 589856 | tf_op jit(solution)/shard_map/ppermute | solution.py:275
  72.4 1.6 %collective-permute-start.26 = (bf16[128,2304]{1,0:T(8,128)(2,1)S(1)}, bf16[128,2304]{1,0:T(8,128)(2,1)S(1)}, u32[]{:S(2)}, u32[]{:S(2)}) collective-permute-start(bf16[128,2304]{1,0:T(8,128)(2,1)S(1)} %collective-permute-done.20.refs_12_), channel_id=1, source_target_pairs={{0,16},{4,12},{8,24},{12,4},{16,0},{20,28},{24,8},{28,20},{1,17},{... | collective-permute-start | bytes 1769480 | tf_op jit(solution)/shard_map/ppermute | solution.py:275
  74.0 3.7 %collective-permute-start.15 = (bf16[2,32,1152]{2,1,0:T(8,128)(2,1)S(1)}, bf16[2,32,1152]{2,1,0:T(8,128)(2,1)S(1)}, u32[]{:S(2)}, u32[]{:S(2)}) collective-permute-start(bf16[2,32,1152]{2,1,0:T(8,128)(2,1)S(1)} %get-tuple-element.50), channel_id=1, source_target_pairs={{0,3},{1,2},{2,1},{3,0},{4,7},{5,6},{6,5},{7,4},{8,11},{9,10},{10,... | collective-permute-start | bytes 442376 | tf_op jit(solution)/shard_map/ppermute | solution.py:31
  77.7 1.9 %collective-permute-start.25 = (bf16[2,256,256]{2,1,0:T(8,128)(2,1)S(1)}, bf16[2,256,256]{2,1,0:T(8,128)(2,1)S(1)}, u32[]{:S(2)}, u32[]{:S(2)}) collective-permute-start(bf16[2,256,256]{2,1,0:T(8,128)(2,1)S(1)} %get-tuple-element.57), channel_id=1, source_target_pairs={{0,24},{4,28},{8,16},{12,20},{16,8},{20,12},{24,0},{28,4},{1,25},{... | collective-permute-start | bytes 786440 | tf_op jit(solution)/shard_map/ppermute | solution.py:275
  83.4 2.0 %shard_map.118 = (bf16[256,2048]{1,0:T(8,128)(2,1)}, bf16[8,256]{1,0:T(8,128)(2,1)}) custom-call(s32[2]{0:T(128)S(1)} %pad_add_fusion.pos, s32[8,256]{1,0:T(8,128)S(1)} %bitcast.12, bf16[8,256]{1,0:T(8,128)(2,1)S(1)} %bitcast.14, bf16[128,256]{1,0:T(8,128)(2,1)S(1)} %get-tuple-element.34.select, bf16[2,32,1152]{2,1,0:T(8,128)(2,1)S(1)} %get-tuple-element.47.refs_0_, ...), custom_call_target="tpu_custom_call" | custom-call | tf_op jit(solution)/shard_map/pallas_call | solution.py:257
  85.4 2.1 %collective-permute-done.25.refs_1_ = bf16[2,256,256]{2,1,0:T(8,128)(2,1)S(1)} collective-permute-done((bf16[2,256,256]{2,1,0:T(8,128)(2,1)S(1)}, bf16[2,256,256]{2,1,0:T(8,128)(2,1)S(1)}, u32[]{:S(2)}, u32[]{:S(2)}) %collective-permute-start.25) | collective-permute-done | bytes 262176 | tf_op jit(solution)/shard_map/ppermute | solution.py:275
  87.9 2.0 %collective-permute-done.27.refs_3_ = bf16[128,2304]{1,0:T(8,128)(2,1)S(1)} collective-permute-done((bf16[128,2304]{1,0:T(8,128)(2,1)S(1)}, bf16[128,2304]{1,0:T(8,128)(2,1)S(1)}, u32[]{:S(2)}, u32[]{:S(2)}) %collective-permute-start.27) | collective-permute-done | bytes 589856 | tf_op jit(solution)/shard_map/ppermute | solution.py:31
  (47 shorter events, 16.3 us)
Async XLA Ops:
  1.9 29.3 %collective-permute-start.8 = (bf16[768,768]{1,0:T(8,128)(2,1)S(1)}, bf16[768,768]{1,0:T(8,128)(2,1)S(1)}, u32[]{:S(2)}, u32[]{:S(2)}) collective-permute-start(bf16[768,768]{1,0:T(8,128)(2,1)S(1)} %shard_map.111.refs_8_.refs_0_), channel_id=1, source_target_pairs={{0,8},{4,20},{8,0},{12,28},{16,24},{20,4},{24,16},{28,12},{1,9},{5... | collective-permute-start | bytes 3538952 | tf_op jit(solution)/shard_map/ppermute | solution.py:275
  4.9 28.4 %collective-permute-start.3 = (bf16[768,768]{1,0:T(8,128)(2,1)S(1)}, bf16[768,768]{1,0:T(8,128)(2,1)S(1)}, u32[]{:S(2)}, u32[]{:S(2)}) collective-permute-start(bf16[768,768]{1,0:T(8,128)(2,1)S(1)} %shard_map.111.refs_8_.refs_0_), channel_id=1, source_target_pairs={{0,16},{4,12},{8,24},{12,4},{16,0},{20,28},{24,8},{28,20},{1,17},{... | collective-permute-start | bytes 3538952 | tf_op jit(solution)/shard_map/ppermute | solution.py:275
  9.1 12.1 %collective-permute-start = (bf16[2,64,1024]{2,1,0:T(8,128)(2,1)S(1)}, bf16[2,64,1024]{2,1,0:T(8,128)(2,1)S(1)}, u32[]{:S(2)}, u32[]{:S(2)}) collective-permute-start(bf16[2,64,1024]{2,1,0:T(8,128)(2,1)S(1)} %get-tuple-element.36), channel_id=1, source_target_pairs={{0,1},{1,0},{2,3},{3,2},{4,5},{5,4},{6,7},{7,6},{8,9},{9,8},{10,11... | collective-permute-start | bytes 786440 | tf_op jit(solution)/shard_map/ppermute | solution.py:31
  10.8 22.0 %collective-permute-start.1 = (bf16[2,64,1024]{2,1,0:T(8,128)(2,1)S(1)}, bf16[2,64,1024]{2,1,0:T(8,128)(2,1)S(1)}, u32[]{:S(2)}, u32[]{:S(2)}) collective-permute-start(bf16[2,64,1024]{2,1,0:T(8,128)(2,1)S(1)} %get-tuple-element.37), channel_id=1, source_target_pairs={{0,2},{1,3},{2,0},{3,1},{4,6},{5,7},{6,4},{7,5},{8,10},{9,11},{10,... | collective-permute-start | bytes 786440 | tf_op jit(solution)/shard_map/ppermute | solution.py:31
  13.3 19.9 %collective-permute-start.2 = (bf16[2,64,1024]{2,1,0:T(8,128)(2,1)S(1)}, bf16[2,64,1024]{2,1,0:T(8,128)(2,1)S(1)}, u32[]{:S(2)}, u32[]{:S(2)}) collective-permute-start(bf16[2,64,1024]{2,1,0:T(8,128)(2,1)S(1)} %get-tuple-element.38), channel_id=1, source_target_pairs={{0,3},{1,2},{2,1},{3,0},{4,7},{5,6},{6,5},{7,4},{8,11},{9,10},{10,... | collective-permute-start | bytes 786440 | tf_op jit(solution)/shard_map/ppermute | solution.py:31
  31.2 19.0 %collective-permute-start.10 = (bf16[768,768]{1,0:T(8,128)(2,1)S(1)}, bf16[768,768]{1,0:T(8,128)(2,1)S(1)}, u32[]{:S(2)}, u32[]{:S(2)}) collective-permute-start(bf16[768,768]{1,0:T(8,128)(2,1)S(1)} %collective-permute-done.8.refs_9_.refs_1_), channel_id=1, source_target_pairs={{0,16},{4,12},{8,24},{12,4},{16,0},{20,28},{24,8},{28,20},{1,17},{... | collective-permute-start | bytes 3538952 | tf_op jit(solution)/shard_map/ppermute | solution.py:275
  32.8 1.9 %collective-permute-start.6 = (bf16[2,64,1024]{2,1,0:T(8,128)(2,1)S(1)}, bf16[2,64,1024]{2,1,0:T(8,128)(2,1)S(1)}, u32[]{:S(2)}, u32[]{:S(2)}) collective-permute-start(bf16[2,64,1024]{2,1,0:T(8,128)(2,1)S(1)} %collective-permute-done.1.refs_2_), channel_id=1, source_target_pairs={{0,4},{4,0},{8,12},{12,8},{16,20},{20,16},{24,28},{28,24},{1,5},{5... | collective-permute-start | bytes 786440 | tf_op jit(solution)/shard_map/ppermute | solution.py:31
  33.3 2.1 %collective-permute-start.4 = (bf16[2,64,1024]{2,1,0:T(8,128)(2,1)S(1)}, bf16[2,64,1024]{2,1,0:T(8,128)(2,1)S(1)}, u32[]{:S(2)}, u32[]{:S(2)}) collective-permute-start(bf16[2,64,1024]{2,1,0:T(8,128)(2,1)S(1)} %get-tuple-element.39.refs_0_), channel_id=1, source_target_pairs={{0,4},{4,0},{8,12},{12,8},{16,20},{20,16},{24,28},{28,24},{1,5},{5... | collective-permute-start | bytes 786440 | tf_op jit(solution)/shard_map/ppermute | solution.py:31
  35.5 9.3 %collective-permute-start.9 = (bf16[2,256,256]{2,1,0:T(8,128)(2,1)S(1)}, bf16[2,256,256]{2,1,0:T(8,128)(2,1)S(1)}, u32[]{:S(2)}, u32[]{:S(2)}) collective-permute-start(bf16[2,256,256]{2,1,0:T(8,128)(2,1)S(1)} %get-tuple-element.40), channel_id=1, source_target_pairs={{0,8},{4,20},{8,0},{12,28},{16,24},{20,4},{24,16},{28,12},{1,9},{5... | collective-permute-start | bytes 786440 | tf_op jit(solution)/shard_map/ppermute | solution.py:275
  50.7 2.1 %collective-permute-start.11 = (bf16[128,2304]{1,0:T(8,128)(2,1)S(1)}, bf16[128,2304]{1,0:T(8,128)(2,1)S(1)}, u32[]{:S(2)}, u32[]{:S(2)}) collective-permute-start(bf16[128,2304]{1,0:T(8,128)(2,1)S(1)} %get-tuple-element.44), channel_id=1, source_target_pairs={{0,4},{4,0},{8,12},{12,8},{16,20},{20,16},{24,28},{28,24},{1,5},{5... | collective-permute-start | bytes 1769480 | tf_op jit(solution)/shard_map/ppermute | solution.py:31
  53.2 3.4 %collective-permute-start.12 = (bf16[128,2304]{1,0:T(8,128)(2,1)S(1)}, bf16[128,2304]{1,0:T(8,128)(2,1)S(1)}, u32[]{:S(2)}, u32[]{:S(2)}) collective-permute-start(bf16[128,2304]{1,0:T(8,128)(2,1)S(1)} %get-tuple-element.45.deltas.refs_10_), channel_id=1, source_target_pairs={{0,4},{4,0},{8,12},{12,8},{16,20},{20,16},{24,28},{28,24},{1,5},{5... | collective-permute-start | bytes 1769480 | tf_op jit(solution)/shard_map/ppermute | solution.py:31
  53.4 14.6 %collective-permute-start.21 = (bf16[128,2304]{1,0:T(8,128)(2,1)S(1)}, bf16[128,2304]{1,0:T(8,128)(2,1)S(1)}, u32[]{:S(2)}, u32[]{:S(2)}) collective-permute-start(bf16[128,2304]{1,0:T(8,128)(2,1)S(1)} %get-tuple-element.45.deltas.refs_10_), channel_id=1, source_target_pairs={{0,16},{4,12},{8,24},{12,4},{16,0},{20,28},{24,8},{28,20},{1,17},{... | collective-permute-start | bytes 1769480 | tf_op jit(solution)/shard_map/ppermute | solution.py:275
  55.0 16.3 %collective-permute-start.20 = (bf16[128,2304]{1,0:T(8,128)(2,1)S(1)}, bf16[128,2304]{1,0:T(8,128)(2,1)S(1)}, u32[]{:S(2)}, u32[]{:S(2)}) collective-permute-start(bf16[128,2304]{1,0:T(8,128)(2,1)S(1)} %get-tuple-element.45.deltas.refs_10_), channel_id=1, source_target_pairs={{0,8},{4,20},{8,0},{12,28},{16,24},{20,4},{24,16},{28,12},{1,9},{5... | collective-permute-start | bytes 1769480 | tf_op jit(solution)/shard_map/ppermute | solution.py:275
  57.6 10.3 %collective-permute-start.13 = (bf16[2,32,1152]{2,1,0:T(8,128)(2,1)S(1)}, bf16[2,32,1152]{2,1,0:T(8,128)(2,1)S(1)}, u32[]{:S(2)}, u32[]{:S(2)}) collective-permute-start(bf16[2,32,1152]{2,1,0:T(8,128)(2,1)S(1)} %get-tuple-element.48), channel_id=1, source_target_pairs={{0,1},{1,0},{2,3},{3,2},{4,5},{5,4},{6,7},{7,6},{8,9},{9,8},{10,11... | collective-permute-start | bytes 442376 | tf_op jit(solution)/shard_map/ppermute | solution.py:31
  59.3 9.4 %collective-permute-start.14 = (bf16[2,32,1152]{2,1,0:T(8,128)(2,1)S(1)}, bf16[2,32,1152]{2,1,0:T(8,128)(2,1)S(1)}, u32[]{:S(2)}, u32[]{:S(2)}) collective-permute-start(bf16[2,32,1152]{2,1,0:T(8,128)(2,1)S(1)} %get-tuple-element.49), channel_id=1, source_target_pairs={{0,2},{1,3},{2,0},{3,1},{4,6},{5,7},{6,4},{7,5},{8,10},{9,11},{10,... | collective-permute-start | bytes 442376 | tf_op jit(solution)/shard_map/ppermute | solution.py:31
  61.9 10.6 %collective-permute-start.19 = (bf16[2,256,256]{2,1,0:T(8,128)(2,1)S(1)}, bf16[2,256,256]{2,1,0:T(8,128)(2,1)S(1)}, u32[]{:S(2)}, u32[]{:S(2)}) collective-permute-start(bf16[2,256,256]{2,1,0:T(8,128)(2,1)S(1)} %get-tuple-element.51), channel_id=1, source_target_pairs={{0,16},{4,12},{8,24},{12,4},{16,0},{20,28},{24,8},{28,20},{1,17},{... | collective-permute-start | bytes 786440 | tf_op jit(solution)/shard_map/ppermute | solution.py:275
  68.7 9.1 %collective-permute-start.22 = (bf16[128,2304]{1,0:T(8,128)(2,1)S(1)}, bf16[128,2304]{1,0:T(8,128)(2,1)S(1)}, u32[]{:S(2)}, u32[]{:S(2)}) collective-permute-start(bf16[128,2304]{1,0:T(8,128)(2,1)S(1)} %collective-permute-done.21.refs_14_), channel_id=1, source_target_pairs={{0,4},{4,0},{8,12},{12,8},{16,20},{20,16},{24,28},{28,24},{1,5},{5... | collective-permute-start | bytes 1769480 | tf_op jit(solution)/shard_map/ppermute | solution.py:31
  71.2 8.4 %collective-permute-start.23 = (bf16[128,2304]{1,0:T(8,128)(2,1)S(1)}, bf16[128,2304]{1,0:T(8,128)(2,1)S(1)}, u32[]{:S(2)}, u32[]{:S(2)}) collective-permute-start(bf16[128,2304]{1,0:T(8,128)(2,1)S(1)} %collective-permute-done.20.refs_12_), channel_id=1, source_target_pairs={{0,4},{4,0},{8,12},{12,8},{16,20},{20,16},{24,28},{28,24},{1,5},{5... | collective-permute-start | bytes 1769480 | tf_op jit(solution)/shard_map/ppermute | solution.py:31
  72.4 15.5 %collective-permute-start.26 = (bf16[128,2304]{1,0:T(8,128)(2,1)S(1)}, bf16[128,2304]{1,0:T(8,128)(2,1)S(1)}, u32[]{:S(2)}, u32[]{:S(2)}) collective-permute-start(bf16[128,2304]{1,0:T(8,128)(2,1)S(1)} %collective-permute-done.20.refs_12_), channel_id=1, source_target_pairs={{0,16},{4,12},{8,24},{12,4},{16,0},{20,28},{24,8},{28,20},{1,17},{... | collective-permute-start | bytes 1769480 | tf_op jit(solution)/shard_map/ppermute | solution.py:275
  74.0 7.9 %collective-permute-start.15 = (bf16[2,32,1152]{2,1,0:T(8,128)(2,1)S(1)}, bf16[2,32,1152]{2,1,0:T(8,128)(2,1)S(1)}, u32[]{:S(2)}, u32[]{:S(2)}) collective-permute-start(bf16[2,32,1152]{2,1,0:T(8,128)(2,1)S(1)} %get-tuple-element.50), channel_id=1, source_target_pairs={{0,3},{1,2},{2,1},{3,0},{4,7},{5,6},{6,5},{7,4},{8,11},{9,10},{10,... | collective-permute-start | bytes 442376 | tf_op jit(solution)/shard_map/ppermute | solution.py:31
  77.7 4.1 %collective-permute-start.16 = (bf16[2,32,1152]{2,1,0:T(8,128)(2,1)S(1)}, bf16[2,32,1152]{2,1,0:T(8,128)(2,1)S(1)}, u32[]{:S(2)}, u32[]{:S(2)}) collective-permute-start(bf16[2,32,1152]{2,1,0:T(8,128)(2,1)S(1)} %get-tuple-element.47.refs_0_), channel_id=1, source_target_pairs={{0,4},{4,0},{8,12},{12,8},{16,20},{20,16},{24,28},{28,24},{1,5},{5... | collective-permute-start | bytes 442376 | tf_op jit(solution)/shard_map/ppermute | solution.py:31
  77.7 9.8 %collective-permute-start.25 = (bf16[2,256,256]{2,1,0:T(8,128)(2,1)S(1)}, bf16[2,256,256]{2,1,0:T(8,128)(2,1)S(1)}, u32[]{:S(2)}, u32[]{:S(2)}) collective-permute-start(bf16[2,256,256]{2,1,0:T(8,128)(2,1)S(1)} %get-tuple-element.57), channel_id=1, source_target_pairs={{0,24},{4,28},{8,16},{12,20},{16,8},{20,12},{24,0},{28,4},{1,25},{... | collective-permute-start | bytes 786440 | tf_op jit(solution)/shard_map/ppermute | solution.py:275
  79.6 2.7 %collective-permute-start.17 = (bf16[2,32,1152]{2,1,0:T(8,128)(2,1)S(1)}, bf16[2,32,1152]{2,1,0:T(8,128)(2,1)S(1)}, u32[]{:S(2)}, u32[]{:S(2)}) collective-permute-start(bf16[2,32,1152]{2,1,0:T(8,128)(2,1)S(1)} %collective-permute-done.13.refs_1_), channel_id=1, source_target_pairs={{0,4},{4,0},{8,12},{12,8},{16,20},{20,16},{24,28},{28,24},{1,5},{5... | collective-permute-start | bytes 442376 | tf_op jit(solution)/shard_map/ppermute | solution.py:31
  87.9 2.0 %collective-permute-start.27 = (bf16[128,2304]{1,0:T(8,128)(2,1)S(1)}, bf16[128,2304]{1,0:T(8,128)(2,1)S(1)}, u32[]{:S(2)}, u32[]{:S(2)}) collective-permute-start(bf16[128,2304]{1,0:T(8,128)(2,1)S(1)} %collective-permute-done.26.refs_2_), channel_id=1, source_target_pairs={{0,4},{4,0},{8,12},{12,8},{16,20},{20,16},{24,28},{28,24},{1,5},{5... | collective-permute-start | bytes 1769480 | tf_op jit(solution)/shard_map/ppermute | solution.py:31
  (6 other events, 18.0 us)

commit v6 on v5

--- a/solution.py
+++ b/solution.py
@@ -364,7 +364,7 @@
     for p in late:
         deltas[p] = to(after(deltas[p ^ top(p)], back[1], *got[1:-1]), top(p))
     for p in near:
-        deltas_other[p] = hop(after(deltas[p], *back[1:3]), "fsdp", 1)
+        deltas_other[p] = hop(after(deltas[p], *back[1:4:2]), "fsdp", 1)
 
     def weight_sums(entries, carried):
         far = [got[p - 1] for p in entries if p]
@@ -383,7 +383,7 @@
         )
 
     part = weight_sums(early, ())[0]
-    back_other = [hop(after(x, part) if k == n_e - 1 else x, "fsdp", 1) for k, x in enumerate(back)]
+    back_other = [hop(after(x, part) if k == 2 % n_e else x, "fsdp", 1) for k, x in enumerate(back)]
     in_grad, gate_grad = call(
         final_kernel,
         (pos, ids, gates, select, *back, *back_other),

time: 91.4 us -> 91.4 us (level)
  starting transfers between devices: 30.4 us -> 29.3 us
  waiting for transfers between devices: 48.7 us -> 49.8 us
    ppermute x19, waiting for transfers between devices: 15.9 us -> 18.9 us  [hop(): lax.ppermute(x, axis, [(i, i ^ offset) for i in range(lax.axis_size(axis))])]
    ppermute x9, waiting for transfers between devices: 32.8 us -> 30.9 us  [to(): lax.ppermute(x, 'fsdp', [(i, i ^ flips(position, i & 1, bits)) for i in r...]
    ppermute x19, starting transfers between devices: 14.6 us -> 13.5 us  [hop(): lax.ppermute(x, axis, [(i, i ^ offset) for i in range(lax.axis_size(axis))])]
  transfers between devices with their start and end apart: 28 -> 28, of which waited for: 19 -> 18; matrix products, arithmetic and copies ran while one was open for 0% -> 0% of each run, Pallas kernels for 9% -> 9%
where the time goes in v6:
time: 91.4 us; the launch traced here: 91.3 us
  waiting for transfers between devices  49.8 us (54%)
  starting transfers between devices  29.3 us (32%)
  Pallas kernels  11.4 us (12%)
    ppermute x9, waiting for transfers between devices, to(): lax.ppermute(x, 'fsdp', [(i, i ^ flips(position, i & 1, bits)) for i in r...  30.9 us
    ppermute x19, waiting for transfers between devices, hop(): lax.ppermute(x, axis, [(i, i ^ offset) for i in range(lax.axis_size(axis))])  18.9 us
    ppermute x9, starting transfers between devices, to(): lax.ppermute(x, 'fsdp', [(i, i ^ flips(position, i & 1, bits)) for i in r...  15.8 us
    ppermute x19, starting transfers between devices, hop(): lax.ppermute(x, axis, [(i, i ^ offset) for i in range(lax.axis_size(axis))])  13.5 us
    pallas_call x10, Pallas kernels, call(): pl.pallas_call(functools.partial(kernel, **static), out_shape=outs, in_sp...  11.4 us
  transfers between devices with their start and end apart: 28, of which 18 were waited for; matrix products, arithmetic and copies ran while one was open for 0% of the time, Pallas kernels for 9%

profile of v6, /device:TPU:0, one launch (start us, length us, event | category | flops | bytes accessed | tf_op | source)
XLA Modules:
  0.0 91.3 jit_solution(17511565187732915819)
XLA Ops:
  1.9 3.0 %collective-permute-start.8 = (bf16[768,768]{1,0:T(8,128)(2,1)S(1)}, bf16[768,768]{1,0:T(8,128)(2,1)S(1)}, u32[]{:S(2)}, u32[]{:S(2)}) collective-permute-start(bf16[768,768]{1,0:T(8,128)(2,1)S(1)} %shard_map.111.refs_8_.refs_0_), channel_id=1, source_target_pairs={{0,8},{4,20},{8,0},{12,28},{16,24},{20,4},{24,16},{28,12},{1,9},{5... | collective-permute-start | bytes 3538952 | tf_op jit(solution)/shard_map/ppermute | solution.py:275
  4.9 1.5 %collective-permute-start.3 = (bf16[768,768]{1,0:T(8,128)(2,1)S(1)}, bf16[768,768]{1,0:T(8,128)(2,1)S(1)}, u32[]{:S(2)}, u32[]{:S(2)}) collective-permute-start(bf16[768,768]{1,0:T(8,128)(2,1)S(1)} %shard_map.111.refs_8_.refs_0_), channel_id=1, source_target_pairs={{0,16},{4,12},{8,24},{12,4},{16,0},{20,28},{24,8},{28,20},{1,17},{... | collective-permute-start | bytes 3538952 | tf_op jit(solution)/shard_map/ppermute | solution.py:275
  6.5 2.6 %shard_map.110 = (bf16[2,64,1024]{2,1,0:T(8,128)(2,1)S(1)}, bf16[2,64,1024]{2,1,0:T(8,128)(2,1)S(1)}, bf16[2,64,1024]{2,1,0:T(8,128)(2,1)S(1)}, bf16[2,64,1024]{2,1,0:T(8,128)(2,1)S(1)}, bf16[128,256]{1,0:T(8,128)(2,1)S(1)}) custom-call(s32[2]{0:T(128)S(1)} %pad_add_fusion.pos, s32[8,256]{1,0:T(8,128)S(1)} %bitcast.11, bf16[8,256]{1,0:T(8,128)(2,1)S(1)} %bitcast.13, ...), custom_call_target="tpu_custom_call" | custom-call | tf_op jit(solution)/shard_map/pallas_call | solution.py:257
  9.1 1.6 %collective-permute-start = (bf16[2,64,1024]{2,1,0:T(8,128)(2,1)S(1)}, bf16[2,64,1024]{2,1,0:T(8,128)(2,1)S(1)}, u32[]{:S(2)}, u32[]{:S(2)}) collective-permute-start(bf16[2,64,1024]{2,1,0:T(8,128)(2,1)S(1)} %get-tuple-element.36), channel_id=1, source_target_pairs={{0,1},{1,0},{2,3},{3,2},{4,5},{5,4},{6,7},{7,6},{8,9},{9,8},{10,11... | collective-permute-start | bytes 786440 | tf_op jit(solution)/shard_map/ppermute | solution.py:31
  10.8 2.6 %collective-permute-start.1 = (bf16[2,64,1024]{2,1,0:T(8,128)(2,1)S(1)}, bf16[2,64,1024]{2,1,0:T(8,128)(2,1)S(1)}, u32[]{:S(2)}, u32[]{:S(2)}) collective-permute-start(bf16[2,64,1024]{2,1,0:T(8,128)(2,1)S(1)} %get-tuple-element.37), channel_id=1, source_target_pairs={{0,2},{1,3},{2,0},{3,1},{4,6},{5,7},{6,4},{7,5},{8,10},{9,11},{10,... | collective-permute-start | bytes 786440 | tf_op jit(solution)/shard_map/ppermute | solution.py:31
  13.6 7.7 %collective-permute-done.refs_1_ = bf16[2,64,1024]{2,1,0:T(8,128)(2,1)S(1)} collective-permute-done((bf16[2,64,1024]{2,1,0:T(8,128)(2,1)S(1)}, bf16[2,64,1024]{2,1,0:T(8,128)(2,1)S(1)}, u32[]{:S(2)}, u32[]{:S(2)}) %collective-permute-start) | collective-permute-done | bytes 262176 | tf_op jit(solution)/shard_map/ppermute | solution.py:31
  21.2 10.0 %collective-permute-done.8.refs_9_.refs_1_ = bf16[768,768]{1,0:T(8,128)(2,1)S(1)} collective-permute-done((bf16[768,768]{1,0:T(8,128)(2,1)S(1)}, bf16[768,768]{1,0:T(8,128)(2,1)S(1)}, u32[]{:S(2)}, u32[]{:S(2)}) %collective-permute-start.8) | collective-permute-done | bytes 1179680 | tf_op jit(solution)/shard_map/ppermute | solution.py:275
  31.2 1.6 %collective-permute-start.10 = (bf16[768,768]{1,0:T(8,128)(2,1)S(1)}, bf16[768,768]{1,0:T(8,128)(2,1)S(1)}, u32[]{:S(2)}, u32[]{:S(2)}) collective-permute-start(bf16[768,768]{1,0:T(8,128)(2,1)S(1)} %collective-permute-done.8.refs_9_.refs_1_), channel_id=1, source_target_pairs={{0,16},{4,12},{8,24},{12,4},{16,0},{20,28},{24,8},{28,20},{1,17},{... | collective-permute-start | bytes 3538952 | tf_op jit(solution)/shard_map/ppermute | solution.py:275
  35.5 1.7 %collective-permute-start.9 = (bf16[2,256,256]{2,1,0:T(8,128)(2,1)S(1)}, bf16[2,256,256]{2,1,0:T(8,128)(2,1)S(1)}, u32[]{:S(2)}, u32[]{:S(2)}) collective-permute-start(bf16[2,256,256]{2,1,0:T(8,128)(2,1)S(1)} %get-tuple-element.40), channel_id=1, source_target_pairs={{0,8},{4,20},{8,0},{12,28},{16,24},{20,4},{24,16},{28,12},{1,9},{5... | collective-permute-start | bytes 786440 | tf_op jit(solution)/shard_map/ppermute | solution.py:275
  38.3 6.5 %collective-permute-done.9.refs_8_ = bf16[2,256,256]{2,1,0:T(8,128)(2,1)S(1)} collective-permute-done((bf16[2,256,256]{2,1,0:T(8,128)(2,1)S(1)}, bf16[2,256,256]{2,1,0:T(8,128)(2,1)S(1)}, u32[]{:S(2)}, u32[]{:S(2)}) %collective-permute-start.9) | collective-permute-done | bytes 262176 | tf_op jit(solution)/shard_map/ppermute | solution.py:275
  44.8 5.4 %collective-permute-done.10.refs_9_.refs_3_ = bf16[768,768]{1,0:T(8,128)(2,1)S(1)} collective-permute-done((bf16[768,768]{1,0:T(8,128)(2,1)S(1)}, bf16[768,768]{1,0:T(8,128)(2,1)S(1)}, u32[]{:S(2)}, u32[]{:S(2)}) %collective-permute-start.10) | collective-permute-done | bytes 1179680 | tf_op jit(solution)/shard_map/ppermute | solution.py:275
  50.8 2.0 %collective-permute-done.11.got = bf16[128,2304]{1,0:T(8,128)(2,1)S(1)} collective-permute-done((bf16[128,2304]{1,0:T(8,128)(2,1)S(1)}, bf16[128,2304]{1,0:T(8,128)(2,1)S(1)}, u32[]{:S(2)}, u32[]{:S(2)}) %collective-permute-start.11) | collective-permute-done | bytes 589856 | tf_op jit(solution)/shard_map/ppermute | solution.py:31
  53.4 1.6 %collective-permute-start.20 = (bf16[128,2304]{1,0:T(8,128)(2,1)S(1)}, bf16[128,2304]{1,0:T(8,128)(2,1)S(1)}, u32[]{:S(2)}, u32[]{:S(2)}) collective-permute-start(bf16[128,2304]{1,0:T(8,128)(2,1)S(1)} %get-tuple-element.45.deltas.refs_10_), channel_id=1, source_target_pairs={{0,16},{4,12},{8,24},{12,4},{16,0},{20,28},{24,8},{28,20},{1,17},{... | collective-permute-start | bytes 1769480 | tf_op jit(solution)/shard_map/ppermute | solution.py:275
  55.0 1.6 %collective-permute-start.19 = (bf16[128,2304]{1,0:T(8,128)(2,1)S(1)}, bf16[128,2304]{1,0:T(8,128)(2,1)S(1)}, u32[]{:S(2)}, u32[]{:S(2)}) collective-permute-start(bf16[128,2304]{1,0:T(8,128)(2,1)S(1)} %get-tuple-element.45.deltas.refs_10_), channel_id=1, source_target_pairs={{0,8},{4,20},{8,0},{12,28},{16,24},{20,4},{24,16},{28,12},{1,9},{5... | collective-permute-start | bytes 1769480 | tf_op jit(solution)/shard_map/ppermute | solution.py:275
  57.6 1.6 %collective-permute-start.13 = (bf16[2,32,1152]{2,1,0:T(8,128)(2,1)S(1)}, bf16[2,32,1152]{2,1,0:T(8,128)(2,1)S(1)}, u32[]{:S(2)}, u32[]{:S(2)}) collective-permute-start(bf16[2,32,1152]{2,1,0:T(8,128)(2,1)S(1)} %get-tuple-element.48), channel_id=1, source_target_pairs={{0,1},{1,0},{2,3},{3,2},{4,5},{5,4},{6,7},{7,6},{8,9},{9,8},{10,11... | collective-permute-start | bytes 442376 | tf_op jit(solution)/shard_map/ppermute | solution.py:31
  59.3 2.5 %collective-permute-start.15 = (bf16[2,32,1152]{2,1,0:T(8,128)(2,1)S(1)}, bf16[2,32,1152]{2,1,0:T(8,128)(2,1)S(1)}, u32[]{:S(2)}, u32[]{:S(2)}) collective-permute-start(bf16[2,32,1152]{2,1,0:T(8,128)(2,1)S(1)} %get-tuple-element.50), channel_id=1, source_target_pairs={{0,3},{1,2},{2,1},{3,0},{4,7},{5,6},{6,5},{7,4},{8,11},{9,10},{10,... | collective-permute-start | bytes 442376 | tf_op jit(solution)/shard_map/ppermute | solution.py:31
  63.1 4.9 %collective-permute-done.20.refs_14_ = bf16[128,2304]{1,0:T(8,128)(2,1)S(1)} collective-permute-done((bf16[128,2304]{1,0:T(8,128)(2,1)S(1)}, bf16[128,2304]{1,0:T(8,128)(2,1)S(1)}, u32[]{:S(2)}, u32[]{:S(2)}) %collective-permute-start.20) | collective-permute-done | bytes 589856 | tf_op jit(solution)/shard_map/ppermute | solution.py:275
  68.6 2.7 %collective-permute-done.19.refs_12_ = bf16[128,2304]{1,0:T(8,128)(2,1)S(1)} collective-permute-done((bf16[128,2304]{1,0:T(8,128)(2,1)S(1)}, bf16[128,2304]{1,0:T(8,128)(2,1)S(1)}, u32[]{:S(2)}, u32[]{:S(2)}) %collective-permute-start.19) | collective-permute-done | bytes 589856 | tf_op jit(solution)/shard_map/ppermute | solution.py:275
  72.4 1.6 %collective-permute-start.26 = (bf16[128,2304]{1,0:T(8,128)(2,1)S(1)}, bf16[128,2304]{1,0:T(8,128)(2,1)S(1)}, u32[]{:S(2)}, u32[]{:S(2)}) collective-permute-start(bf16[128,2304]{1,0:T(8,128)(2,1)S(1)} %collective-permute-done.19.refs_12_), channel_id=1, source_target_pairs={{0,16},{4,12},{8,24},{12,4},{16,0},{20,28},{24,8},{28,20},{1,17},{... | collective-permute-start | bytes 1769480 | tf_op jit(solution)/shard_map/ppermute | solution.py:275
  74.0 2.7 %collective-permute-start.14 = (bf16[2,32,1152]{2,1,0:T(8,128)(2,1)S(1)}, bf16[2,32,1152]{2,1,0:T(8,128)(2,1)S(1)}, u32[]{:S(2)}, u32[]{:S(2)}) collective-permute-start(bf16[2,32,1152]{2,1,0:T(8,128)(2,1)S(1)} %get-tuple-element.49), channel_id=1, source_target_pairs={{0,2},{1,3},{2,0},{3,1},{4,6},{5,7},{6,4},{7,5},{8,10},{9,11},{10,... | collective-permute-start | bytes 442376 | tf_op jit(solution)/shard_map/ppermute | solution.py:31
  76.7 1.9 %collective-permute-start.25 = (bf16[2,256,256]{2,1,0:T(8,128)(2,1)S(1)}, bf16[2,256,256]{2,1,0:T(8,128)(2,1)S(1)}, u32[]{:S(2)}, u32[]{:S(2)}) collective-permute-start(bf16[2,256,256]{2,1,0:T(8,128)(2,1)S(1)} %get-tuple-element.57), channel_id=1, source_target_pairs={{0,24},{4,28},{8,16},{12,20},{16,8},{20,12},{24,0},{28,4},{1,25},{... | collective-permute-start | bytes 786440 | tf_op jit(solution)/shard_map/ppermute | solution.py:275
  80.0 4.0 %collective-permute-done.14.refs_2_ = bf16[2,32,1152]{2,1,0:T(8,128)(2,1)S(1)} collective-permute-done((bf16[2,32,1152]{2,1,0:T(8,128)(2,1)S(1)}, bf16[2,32,1152]{2,1,0:T(8,128)(2,1)S(1)}, u32[]{:S(2)}, u32[]{:S(2)}) %collective-permute-start.14) | collective-permute-done | bytes 147488 | tf_op jit(solution)/shard_map/ppermute | solution.py:31
  85.5 2.0 %shard_map.118 = (bf16[256,2048]{1,0:T(8,128)(2,1)}, bf16[8,256]{1,0:T(8,128)(2,1)}) custom-call(s32[2]{0:T(128)S(1)} %pad_add_fusion.pos, s32[8,256]{1,0:T(8,128)S(1)} %bitcast.12, bf16[8,256]{1,0:T(8,128)(2,1)S(1)} %bitcast.14, bf16[128,256]{1,0:T(8,128)(2,1)S(1)} %get-tuple-element.34.select, bf16[2,32,1152]{2,1,0:T(8,128)(2,1)S(1)} %get-tuple-element.47.refs_0_, ...), custom_call_target="tpu_custom_call" | custom-call | tf_op jit(solution)/shard_map/pallas_call | solution.py:257
  87.9 2.0 %collective-permute-done.27.refs_3_ = bf16[128,2304]{1,0:T(8,128)(2,1)S(1)} collective-permute-done((bf16[128,2304]{1,0:T(8,128)(2,1)S(1)}, bf16[128,2304]{1,0:T(8,128)(2,1)S(1)}, u32[]{:S(2)}, u32[]{:S(2)}) %collective-permute-start.27) | collective-permute-done | bytes 589856 | tf_op jit(solution)/shard_map/ppermute | solution.py:31
  (47 shorter events, 15.3 us)
Async XLA Ops:
  1.9 29.3 %collective-permute-start.8 = (bf16[768,768]{1,0:T(8,128)(2,1)S(1)}, bf16[768,768]{1,0:T(8,128)(2,1)S(1)}, u32[]{:S(2)}, u32[]{:S(2)}) collective-permute-start(bf16[768,768]{1,0:T(8,128)(2,1)S(1)} %shard_map.111.refs_8_.refs_0_), channel_id=1, source_target_pairs={{0,8},{4,20},{8,0},{12,28},{16,24},{20,4},{24,16},{28,12},{1,9},{5... | collective-permute-start | bytes 3538952 | tf_op jit(solution)/shard_map/ppermute | solution.py:275
  4.9 28.4 %collective-permute-start.3 = (bf16[768,768]{1,0:T(8,128)(2,1)S(1)}, bf16[768,768]{1,0:T(8,128)(2,1)S(1)}, u32[]{:S(2)}, u32[]{:S(2)}) collective-permute-start(bf16[768,768]{1,0:T(8,128)(2,1)S(1)} %shard_map.111.refs_8_.refs_0_), channel_id=1, source_target_pairs={{0,16},{4,12},{8,24},{12,4},{16,0},{20,28},{24,8},{28,20},{1,17},{... | collective-permute-start | bytes 3538952 | tf_op jit(solution)/shard_map/ppermute | solution.py:275
  9.1 12.1 %collective-permute-start = (bf16[2,64,1024]{2,1,0:T(8,128)(2,1)S(1)}, bf16[2,64,1024]{2,1,0:T(8,128)(2,1)S(1)}, u32[]{:S(2)}, u32[]{:S(2)}) collective-permute-start(bf16[2,64,1024]{2,1,0:T(8,128)(2,1)S(1)} %get-tuple-element.36), channel_id=1, source_target_pairs={{0,1},{1,0},{2,3},{3,2},{4,5},{5,4},{6,7},{7,6},{8,9},{9,8},{10,11... | collective-permute-start | bytes 786440 | tf_op jit(solution)/shard_map/ppermute | solution.py:31
  10.8 22.0 %collective-permute-start.1 = (bf16[2,64,1024]{2,1,0:T(8,128)(2,1)S(1)}, bf16[2,64,1024]{2,1,0:T(8,128)(2,1)S(1)}, u32[]{:S(2)}, u32[]{:S(2)}) collective-permute-start(bf16[2,64,1024]{2,1,0:T(8,128)(2,1)S(1)} %get-tuple-element.37), channel_id=1, source_target_pairs={{0,2},{1,3},{2,0},{3,1},{4,6},{5,7},{6,4},{7,5},{8,10},{9,11},{10,... | collective-permute-start | bytes 786440 | tf_op jit(solution)/shard_map/ppermute | solution.py:31
  13.3 19.9 %collective-permute-start.2 = (bf16[2,64,1024]{2,1,0:T(8,128)(2,1)S(1)}, bf16[2,64,1024]{2,1,0:T(8,128)(2,1)S(1)}, u32[]{:S(2)}, u32[]{:S(2)}) collective-permute-start(bf16[2,64,1024]{2,1,0:T(8,128)(2,1)S(1)} %get-tuple-element.38), channel_id=1, source_target_pairs={{0,3},{1,2},{2,1},{3,0},{4,7},{5,6},{6,5},{7,4},{8,11},{9,10},{10,... | collective-permute-start | bytes 786440 | tf_op jit(solution)/shard_map/ppermute | solution.py:31
  31.2 19.0 %collective-permute-start.10 = (bf16[768,768]{1,0:T(8,128)(2,1)S(1)}, bf16[768,768]{1,0:T(8,128)(2,1)S(1)}, u32[]{:S(2)}, u32[]{:S(2)}) collective-permute-start(bf16[768,768]{1,0:T(8,128)(2,1)S(1)} %collective-permute-done.8.refs_9_.refs_1_), channel_id=1, source_target_pairs={{0,16},{4,12},{8,24},{12,4},{16,0},{20,28},{24,8},{28,20},{1,17},{... | collective-permute-start | bytes 3538952 | tf_op jit(solution)/shard_map/ppermute | solution.py:275
  32.8 1.9 %collective-permute-start.6 = (bf16[2,64,1024]{2,1,0:T(8,128)(2,1)S(1)}, bf16[2,64,1024]{2,1,0:T(8,128)(2,1)S(1)}, u32[]{:S(2)}, u32[]{:S(2)}) collective-permute-start(bf16[2,64,1024]{2,1,0:T(8,128)(2,1)S(1)} %collective-permute-done.1.refs_2_), channel_id=1, source_target_pairs={{0,4},{4,0},{8,12},{12,8},{16,20},{20,16},{24,28},{28,24},{1,5},{5... | collective-permute-start | bytes 786440 | tf_op jit(solution)/shard_map/ppermute | solution.py:31
  33.3 2.1 %collective-permute-start.4 = (bf16[2,64,1024]{2,1,0:T(8,128)(2,1)S(1)}, bf16[2,64,1024]{2,1,0:T(8,128)(2,1)S(1)}, u32[]{:S(2)}, u32[]{:S(2)}) collective-permute-start(bf16[2,64,1024]{2,1,0:T(8,128)(2,1)S(1)} %get-tuple-element.39.refs_0_), channel_id=1, source_target_pairs={{0,4},{4,0},{8,12},{12,8},{16,20},{20,16},{24,28},{28,24},{1,5},{5... | collective-permute-start | bytes 786440 | tf_op jit(solution)/shard_map/ppermute | solution.py:31
  35.5 9.3 %collective-permute-start.9 = (bf16[2,256,256]{2,1,0:T(8,128)(2,1)S(1)}, bf16[2,256,256]{2,1,0:T(8,128)(2,1)S(1)}, u32[]{:S(2)}, u32[]{:S(2)}) collective-permute-start(bf16[2,256,256]{2,1,0:T(8,128)(2,1)S(1)} %get-tuple-element.40), channel_id=1, source_target_pairs={{0,8},{4,20},{8,0},{12,28},{16,24},{20,4},{24,16},{28,12},{1,9},{5... | collective-permute-start | bytes 786440 | tf_op jit(solution)/shard_map/ppermute | solution.py:275
  50.7 2.1 %collective-permute-start.11 = (bf16[128,2304]{1,0:T(8,128)(2,1)S(1)}, bf16[128,2304]{1,0:T(8,128)(2,1)S(1)}, u32[]{:S(2)}, u32[]{:S(2)}) collective-permute-start(bf16[128,2304]{1,0:T(8,128)(2,1)S(1)} %get-tuple-element.44), channel_id=1, source_target_pairs={{0,4},{4,0},{8,12},{12,8},{16,20},{20,16},{24,28},{28,24},{1,5},{5... | collective-permute-start | bytes 1769480 | tf_op jit(solution)/shard_map/ppermute | solution.py:31
  53.2 3.4 %collective-permute-start.12 = (bf16[128,2304]{1,0:T(8,128)(2,1)S(1)}, bf16[128,2304]{1,0:T(8,128)(2,1)S(1)}, u32[]{:S(2)}, u32[]{:S(2)}) collective-permute-start(bf16[128,2304]{1,0:T(8,128)(2,1)S(1)} %get-tuple-element.45.deltas.refs_10_), channel_id=1, source_target_pairs={{0,4},{4,0},{8,12},{12,8},{16,20},{20,16},{24,28},{28,24},{1,5},{5... | collective-permute-start | bytes 1769480 | tf_op jit(solution)/shard_map/ppermute | solution.py:31
  53.4 14.6 %collective-permute-start.20 = (bf16[128,2304]{1,0:T(8,128)(2,1)S(1)}, bf16[128,2304]{1,0:T(8,128)(2,1)S(1)}, u32[]{:S(2)}, u32[]{:S(2)}) collective-permute-start(bf16[128,2304]{1,0:T(8,128)(2,1)S(1)} %get-tuple-element.45.deltas.refs_10_), channel_id=1, source_target_pairs={{0,16},{4,12},{8,24},{12,4},{16,0},{20,28},{24,8},{28,20},{1,17},{... | collective-permute-start | bytes 1769480 | tf_op jit(solution)/shard_map/ppermute | solution.py:275
  55.0 16.3 %collective-permute-start.19 = (bf16[128,2304]{1,0:T(8,128)(2,1)S(1)}, bf16[128,2304]{1,0:T(8,128)(2,1)S(1)}, u32[]{:S(2)}, u32[]{:S(2)}) collective-permute-start(bf16[128,2304]{1,0:T(8,128)(2,1)S(1)} %get-tuple-element.45.deltas.refs_10_), channel_id=1, source_target_pairs={{0,8},{4,20},{8,0},{12,28},{16,24},{20,4},{24,16},{28,12},{1,9},{5... | collective-permute-start | bytes 1769480 | tf_op jit(solution)/shard_map/ppermute | solution.py:275
  57.6 10.3 %collective-permute-start.13 = (bf16[2,32,1152]{2,1,0:T(8,128)(2,1)S(1)}, bf16[2,32,1152]{2,1,0:T(8,128)(2,1)S(1)}, u32[]{:S(2)}, u32[]{:S(2)}) collective-permute-start(bf16[2,32,1152]{2,1,0:T(8,128)(2,1)S(1)} %get-tuple-element.48), channel_id=1, source_target_pairs={{0,1},{1,0},{2,3},{3,2},{4,5},{5,4},{6,7},{7,6},{8,9},{9,8},{10,11... | collective-permute-start | bytes 442376 | tf_op jit(solution)/shard_map/ppermute | solution.py:31
  59.3 9.3 %collective-permute-start.15 = (bf16[2,32,1152]{2,1,0:T(8,128)(2,1)S(1)}, bf16[2,32,1152]{2,1,0:T(8,128)(2,1)S(1)}, u32[]{:S(2)}, u32[]{:S(2)}) collective-permute-start(bf16[2,32,1152]{2,1,0:T(8,128)(2,1)S(1)} %get-tuple-element.50), channel_id=1, source_target_pairs={{0,3},{1,2},{2,1},{3,0},{4,7},{5,6},{6,5},{7,4},{8,11},{9,10},{10,... | collective-permute-start | bytes 442376 | tf_op jit(solution)/shard_map/ppermute | solution.py:31
  61.7 10.7 %collective-permute-start.18 = (bf16[2,256,256]{2,1,0:T(8,128)(2,1)S(1)}, bf16[2,256,256]{2,1,0:T(8,128)(2,1)S(1)}, u32[]{:S(2)}, u32[]{:S(2)}) collective-permute-start(bf16[2,256,256]{2,1,0:T(8,128)(2,1)S(1)} %get-tuple-element.51), channel_id=1, source_target_pairs={{0,16},{4,12},{8,24},{12,4},{16,0},{20,28},{24,8},{28,20},{1,17},{... | collective-permute-start | bytes 786440 | tf_op jit(solution)/shard_map/ppermute | solution.py:275
  68.6 8.2 %collective-permute-start.21 = (bf16[128,2304]{1,0:T(8,128)(2,1)S(1)}, bf16[128,2304]{1,0:T(8,128)(2,1)S(1)}, u32[]{:S(2)}, u32[]{:S(2)}) collective-permute-start(bf16[128,2304]{1,0:T(8,128)(2,1)S(1)} %collective-permute-done.20.refs_14_), channel_id=1, source_target_pairs={{0,4},{4,0},{8,12},{12,8},{16,20},{20,16},{24,28},{28,24},{1,5},{5... | collective-permute-start | bytes 1769480 | tf_op jit(solution)/shard_map/ppermute | solution.py:31
  71.2 7.4 %collective-permute-start.22 = (bf16[128,2304]{1,0:T(8,128)(2,1)S(1)}, bf16[128,2304]{1,0:T(8,128)(2,1)S(1)}, u32[]{:S(2)}, u32[]{:S(2)}) collective-permute-start(bf16[128,2304]{1,0:T(8,128)(2,1)S(1)} %collective-permute-done.19.refs_12_), channel_id=1, source_target_pairs={{0,4},{4,0},{8,12},{12,8},{16,20},{20,16},{24,28},{28,24},{1,5},{5... | collective-permute-start | bytes 1769480 | tf_op jit(solution)/shard_map/ppermute | solution.py:31
  72.4 15.5 %collective-permute-start.26 = (bf16[128,2304]{1,0:T(8,128)(2,1)S(1)}, bf16[128,2304]{1,0:T(8,128)(2,1)S(1)}, u32[]{:S(2)}, u32[]{:S(2)}) collective-permute-start(bf16[128,2304]{1,0:T(8,128)(2,1)S(1)} %collective-permute-done.19.refs_12_), channel_id=1, source_target_pairs={{0,16},{4,12},{8,24},{12,4},{16,0},{20,28},{24,8},{28,20},{1,17},{... | collective-permute-start | bytes 1769480 | tf_op jit(solution)/shard_map/ppermute | solution.py:275
  74.0 10.0 %collective-permute-start.14 = (bf16[2,32,1152]{2,1,0:T(8,128)(2,1)S(1)}, bf16[2,32,1152]{2,1,0:T(8,128)(2,1)S(1)}, u32[]{:S(2)}, u32[]{:S(2)}) collective-permute-start(bf16[2,32,1152]{2,1,0:T(8,128)(2,1)S(1)} %get-tuple-element.49), channel_id=1, source_target_pairs={{0,2},{1,3},{2,0},{3,1},{4,6},{5,7},{6,4},{7,5},{8,10},{9,11},{10,... | collective-permute-start | bytes 442376 | tf_op jit(solution)/shard_map/ppermute | solution.py:31
  76.7 7.2 %collective-permute-start.16 = (bf16[2,32,1152]{2,1,0:T(8,128)(2,1)S(1)}, bf16[2,32,1152]{2,1,0:T(8,128)(2,1)S(1)}, u32[]{:S(2)}, u32[]{:S(2)}) collective-permute-start(bf16[2,32,1152]{2,1,0:T(8,128)(2,1)S(1)} %get-tuple-element.47.refs_0_), channel_id=1, source_target_pairs={{0,4},{4,0},{8,12},{12,8},{16,20},{20,16},{24,28},{28,24},{1,5},{5... | collective-permute-start | bytes 442376 | tf_op jit(solution)/shard_map/ppermute | solution.py:31
  76.7 10.8 %collective-permute-start.25 = (bf16[2,256,256]{2,1,0:T(8,128)(2,1)S(1)}, bf16[2,256,256]{2,1,0:T(8,128)(2,1)S(1)}, u32[]{:S(2)}, u32[]{:S(2)}) collective-permute-start(bf16[2,256,256]{2,1,0:T(8,128)(2,1)S(1)} %get-tuple-element.57), channel_id=1, source_target_pairs={{0,24},{4,28},{8,16},{12,20},{16,8},{20,12},{24,0},{28,4},{1,25},{... | collective-permute-start | bytes 786440 | tf_op jit(solution)/shard_map/ppermute | solution.py:275
  78.6 5.8 %collective-permute-start.17 = (bf16[2,32,1152]{2,1,0:T(8,128)(2,1)S(1)}, bf16[2,32,1152]{2,1,0:T(8,128)(2,1)S(1)}, u32[]{:S(2)}, u32[]{:S(2)}) collective-permute-start(bf16[2,32,1152]{2,1,0:T(8,128)(2,1)S(1)} %collective-permute-done.13.refs_1_), channel_id=1, source_target_pairs={{0,4},{4,0},{8,12},{12,8},{16,20},{20,16},{24,28},{28,24},{1,5},{5... | collective-permute-start | bytes 442376 | tf_op jit(solution)/shard_map/ppermute | solution.py:31
  87.9 2.0 %collective-permute-start.27 = (bf16[128,2304]{1,0:T(8,128)(2,1)S(1)}, bf16[128,2304]{1,0:T(8,128)(2,1)S(1)}, u32[]{:S(2)}, u32[]{:S(2)}) collective-permute-start(bf16[128,2304]{1,0:T(8,128)(2,1)S(1)} %collective-permute-done.26.refs_2_), channel_id=1, source_target_pairs={{0,4},{4,0},{8,12},{12,8},{16,20},{20,16},{24,28},{28,24},{1,5},{5... | collective-permute-start | bytes 1769480 | tf_op jit(solution)/shard_map/ppermute | solution.py:31
  (6 other events, 18.0 us)
